TPU v7x, 32 devices: a whole 2x2x4 slice. The times are simulated.
32 devices in a mesh: gy: 4 (over x, core), gx: 8 (over z, y).
Axes of the slice: x: 2, y: 2, z: 4, core: 2. Of those that a mesh axis runs over, the one named last changes fastest.
Arguments:
- sky: bfloat16 [48, 256, 1024], P(None, 'gy', 'gx'), may hold values from -6 to 6
- lens_phi: bfloat16 [256, 1024], P('gy', 'gx'), may hold values from -6 to 6
- cotangent: bfloat16 [48, 256, 1024], P(None, 'gy', 'gx'), may hold values from -6 to 6
- tile_mask: int32 [32, 128], P('gy', 'gx'), may hold values 0 or 1
- weight_one: bfloat16 [3, 3, 48, 48], replicated, may hold values from -0.3125 to 0.3125
- weight_two: bfloat16 [3, 3, 48, 48], replicated, may hold values from -0.3125 to 0.3125
- cond_one: float32 [48], replicated, may hold values from -3 to 3
- bias_one: float32 [48], replicated, may hold values from -3 to 3
- cond_two: float32 [48], replicated, may hold values from -3 to 3
Outputs:
- delensed: bfloat16 [48, 256, 1024], P(None, 'gy', 'gx')
- grad_input: bfloat16 [48, 256, 1024], P(None, 'gy', 'gx')
- grad_w1: float32 [3, 3, 48, 48], replicated
- grad_w2: float32 [3, 3, 48, 48], replicated
- grad_cond: float32 [3, 48], replicated
All inputs are finite; a program needn't handle non-finite values. No bound on the sum of `tile_mask` on one device may be relied on, other than what follows from the above.
Results may differ from a plain program's by a relative error of at most 0.0035.
Values may be sent and summed in bfloat16 or wider, within the bound.
No kernel may reach another device: no remote copies, remote signals or barrier semaphores. Data moves between devices by JAX's collectives and lax.ppermute only.
A program may use at most 64 MiB of HBM per device.

v0:
```python
import jax
import jax.numpy as jnp
from jax import lax
from jax.sharding import PartitionSpec as P

TILE = 8


def padded_2(x, sides, width):
    for axis, dim in sides:
        size, length = (lax.axis_size(axis), x.shape[dim])
        up = [(i, (i + 1) % size) for i in range(size - 1)]
        down = [(j, i) for i, j in up]
        last = lax.slice_in_dim(x, length - width, length, axis=dim)
        first = lax.slice_in_dim(x, 0, width, axis=dim)
        before = lax.ppermute(last, axis, up)
        after = lax.ppermute(first, axis, down)
        x = jnp.concatenate([before, x, after], axis=dim)
    return x


def tap_forward(weight_tap, piece):
    chans, rows, cols = piece.shape
    flat = piece.reshape(chans, rows * cols)
    return jnp.dot(weight_tap, flat, preferred_element_type=jnp.float32).reshape(
        weight_tap.shape[0], rows, cols
    )


def forward_conv(weight, padded):
    rows = padded.shape[1] - 2
    cols = padded.shape[2] - 2
    total = jnp.zeros((weight.shape[2], rows, cols), jnp.float32)
    for ky in range(3):
        for kx in range(3):
            total = total + tap_forward(weight[ky, kx], padded[:, ky : ky + rows, kx : kx + cols])
    return total


def back_conv(weight, padded):
    rows = padded.shape[1] - 2
    cols = padded.shape[2] - 2
    total = jnp.zeros((weight.shape[3], rows, cols), jnp.float32)
    for ky in range(3):
        for kx in range(3):
            total = total + tap_forward(
                weight[ky, kx].T, padded[:, 2 - ky : 2 - ky + rows, 2 - kx : 2 - kx + cols]
            )
    return total


def weight_grad(grad, padded):
    rows = grad.shape[1]
    cols = grad.shape[2]
    left = grad.reshape(grad.shape[0], rows * cols)
    taps = []
    for ky in range(3):
        for kx in range(3):
            right = padded[:, ky : ky + rows, kx : kx + cols].reshape(padded.shape[0], rows * cols)
            taps.append(
                lax.dot_general(
                    left, right, (((1,), (1,)), ((), ())), preferred_element_type=jnp.float32
                )
            )
    return jnp.stack(taps).reshape(3, 3, grad.shape[0], padded.shape[0])


def silu_slope(pre):
    sigma = jax.nn.sigmoid(pre)
    return sigma * (1.0 + pre * (1.0 - sigma))


def local(
    sky, lens_phi, cotangent, tile_mask, weight_one, weight_two, cond_one, bias_one, cond_two
):
    rows = sky.shape[1]
    cols = sky.shape[2]
    cell_mask = jnp.repeat(jnp.repeat(tile_mask, TILE, axis=0), TILE, axis=1)
    mask_low = cell_mask.astype(jnp.bfloat16)
    mask_full = cell_mask.astype(jnp.float32)
    phi_full = lens_phi.astype(jnp.float32)
    masked_in = sky * mask_low
    grad_out = cotangent * mask_low
    padded_in = padded_2(masked_in, (("gy", 1), ("gx", 2)), 1)
    pre_one = (
        forward_conv(weight_one, padded_in)
        + cond_one[:, None, None] * phi_full
        + bias_one[:, None, None]
    )
    hidden = (jax.nn.silu(pre_one) * mask_full).astype(jnp.bfloat16)
    padded_hidden = padded_2(hidden, (("gy", 1), ("gx", 2)), 1)
    padded_grad = padded_2(grad_out, (("gy", 1), ("gx", 2)), 1)
    grad_hidden = back_conv(weight_two, padded_grad) * mask_full
    grad_pre = (grad_hidden * silu_slope(pre_one)).astype(jnp.bfloat16)
    padded_pre = padded_2(grad_pre, (("gy", 1), ("gx", 2)), 1)
    delensed = (
        (
            masked_in.astype(jnp.float32)
            + forward_conv(weight_two, padded_hidden)
            + cond_two[:, None, None] * phi_full
        )
        * mask_full
    ).astype(jnp.bfloat16)
    grad_input = (
        (grad_out.astype(jnp.float32) + back_conv(weight_one, padded_pre)) * mask_full
    ).astype(jnp.bfloat16)
    total_cells = rows * lax.axis_size("gy") * cols * lax.axis_size("gx")
    factor = 1.0 / jnp.sqrt(jnp.float32(total_cells))
    local_w1 = weight_grad(grad_pre, padded_in)
    local_w2 = weight_grad(grad_out, padded_hidden)
    pre_full = grad_pre.astype(jnp.float32)
    out_full = grad_out.astype(jnp.float32)
    local_cond = jnp.stack(
        [
            jnp.sum(pre_full * phi_full, axis=(1, 2)),
            jnp.sum(pre_full, axis=(1, 2)),
            jnp.sum(out_full * phi_full, axis=(1, 2)),
        ]
    )
    summed_w1, summed_w2, summed_cond = lax.psum((local_w1, local_w2, local_cond), ("gy", "gx"))
    return (delensed, grad_input, summed_w1 * factor, summed_w2 * factor, summed_cond * factor)


def solution(mesh):
    return jax.shard_map(
        local,
        mesh=mesh,
        in_specs=(
            P(None, "gy", "gx"),
            P("gy", "gx"),
            P(None, "gy", "gx"),
            P("gy", "gx"),
            P(),
            P(),
            P(),
            P(),
            P(),
        ),
        out_specs=(P(None, "gy", "gx"), P(None, "gy", "gx"), P(), P(), P()),
        check_vma=False,
    )
```

profile of v0, /device:TPU:8, one launch (start us, length us, event | category | flops | bytes accessed | tf_op | source)
XLA Modules:
  0.0 325.6 jit_solution(16044822988737957527)
XLA Ops:
  9.8 1.7 collective-permute-start
  14.7 4.3 %collective-permute-start.8 = (bf16[48,1,128]{2,0,1:T(8,128)(2,1)S(1)}, bf16[48,1,128]{2,0,1:T(8,128)(2,1)S(1)}, u32[]{:S(2)}, u32[]{:S(2)}) collective-permute-start(bf16[48,1,128]{2,0,1:T(8,128)(2,1)S(1)} %get-tuple-element.80), channel_id=1, source_target_pairs={{0,8},{8,16},{16,24},{1,9},{9,17},{17,25},{2,10},{10,18},{18,26},{... | collective-permute-start | bytes 36872 | tf_op jit(solution)/shard_map/ppermute | solution.py:16
  22.2 3.4 %collective-permute-start.2 = (bf16[48,66,1]{1,0,2:T(8,128)(2,1)S(1)}, bf16[48,66,1]{1,0,2:T(8,128)(2,1)S(1)}, u32[]{:S(2)}, u32[]{:S(2)}) collective-permute-start(bf16[48,66,1]{1,0,2:T(8,128)(2,1)S(1)} %copy.117), channel_id=1, source_target_pairs={{0,1},{1,2},{2,3},{3,4},{4,5},{5,6},{6,7},{8,9},{9,10},{10,11},{11... | collective-permute-start | bytes 19016 | tf_op jit(solution)/shard_map/ppermute | solution.py:16
  26.3 3.3 %collective-permute-start.3 = (bf16[48,66,1]{1,0,2:T(8,128)(2,1)S(1)}, bf16[48,66,1]{1,0,2:T(8,128)(2,1)S(1)}, u32[]{:S(2)}, u32[]{:S(2)}) collective-permute-start(bf16[48,66,1]{1,0,2:T(8,128)(2,1)S(1)} %copy.121), channel_id=1, source_target_pairs={{1,0},{2,1},{3,2},{4,3},{5,4},{6,5},{7,6},{9,8},{10,9},{11,10},{12... | collective-permute-start | bytes 19016 | tf_op jit(solution)/shard_map/ppermute | solution.py:17
  30.9 2.4 collective-permute-start.10
  34.0 3.9 %collective-permute-start.11 = (bf16[48,66,1]{1,0,2:T(8,128)(2,1)S(1)}, bf16[48,66,1]{1,0,2:T(8,128)(2,1)S(1)}, u32[]{:S(2)}, u32[]{:S(2)}) collective-permute-start(bf16[48,66,1]{1,0,2:T(8,128)(2,1)S(1)} %copy.151), channel_id=1, source_target_pairs={{0,1},{1,2},{2,3},{3,4},{4,5},{5,6},{6,7},{8,9},{9,10},{10,11},{11... | collective-permute-start | bytes 19016 | tf_op jit(solution)/shard_map/ppermute | solution.py:16
  43.5 2.4 slice_bitcast_fusion.18
  49.6 1.6 copy.148
  52.9 3.1 maximum_maximum_fusion.2
  66.1 2.1 fusion.3
  71.8 3.1 collective-permute-start.4
  80.1 42.8 %psum.23 = f32[3,48]{1,0:T(4,128)S(1)} all-reduce(f32[3,48]{1,0:T(4,128)S(1)} %pad_maximum_fusion.20), channel_id=1, replica_groups=mesh['gy'=4,'gx'=8] {'gy','gx'}, use_global_device_ids=true, to_apply=%region_5.6 | all-reduce | flops 144 | bytes 1152 | tf_op jit(solution)/shard_map/psum | solution.py:120
  127.7 2.5 copy.133
  130.1 4.2 %collective-permute-start.6 = (bf16[48,66,1]{1,0,2:T(8,128)(2,1)}, bf16[48,66,1]{1,0,2:T(8,128)(2,1)}, u32[]{:S(2)}, u32[]{:S(2)}) collective-permute-start(bf16[48,66,1]{1,0,2:T(8,128)(2,1)} %copy.133), channel_id=1, source_target_pairs={{0,1},{1,2},{2,3},{3,4},{4,5},{5,6},{6,7},{8,9},{9,10},{10,11},{11... | collective-permute-start | bytes 19016 | tf_op jit(solution)/shard_map/ppermute | solution.py:16
  134.4 2.5 copy.137
  136.8 3.3 %collective-permute-start.7 = (bf16[48,66,1]{1,0,2:T(8,128)(2,1)}, bf16[48,66,1]{1,0,2:T(8,128)(2,1)}, u32[]{:S(2)}, u32[]{:S(2)}) collective-permute-start(bf16[48,66,1]{1,0,2:T(8,128)(2,1)} %copy.137), channel_id=1, source_target_pairs={{1,0},{2,1},{3,2},{4,3},{5,4},{6,5},{7,6},{9,8},{10,9},{11,10},{12... | collective-permute-start | bytes 19016 | tf_op jit(solution)/shard_map/ppermute | solution.py:17
  141.7 1.8 copy.161
  143.5 4.5 %collective-permute-start.14 = (bf16[48,66,1]{1,0,2:T(8,128)(2,1)S(1)}, bf16[48,66,1]{1,0,2:T(8,128)(2,1)S(1)}, u32[]{:S(2)}, u32[]{:S(2)}) collective-permute-start(bf16[48,66,1]{1,0,2:T(8,128)(2,1)S(1)} %copy.161), channel_id=1, source_target_pairs={{1,0},{2,1},{3,2},{4,3},{5,4},{6,5},{7,6},{9,8},{10,9},{11,10},{12... | collective-permute-start | bytes 19016 | tf_op jit(solution)/shard_map/ppermute | solution.py:17
  148.0 2.5 copy.165
  150.5 1.9 collective-permute-start.15
  154.7 2.3 copy.134
  157.0 2.3 copy.138
  159.2 2.9 pad_maximum_fusion.1
  163.7 1.8 slice_bitcast_fusion.12
  170.4 2.1 convolution_add_fusion.4
  174.8 2.3 copy.166
  177.1 3.0 maximum_maximum_fusion.3
  180.1 1.9 slice_bitcast_fusion.1
  184.0 1.8 convolution_add_fusion.3
  201.5 113.7 %all-reduce.3.cloned.1.call-done = (f32[3,3,48,48]{3,2,1,0:T(8,128)}, f32[3,3,48,48]{3,2,1,0:T(8,128)}) async-done(((f32[3,3,48,48]{3,2,1,0:T(8,128)}, f32[3,3,48,48]{3,2,1,0:T(8,128)}), (f32[3,3,48,48]{3,2,1,0:T(8,128)}, f32[3,3,48,48]{3,2,1,0:T(8,128)})) %all-reduce.3.cloned.1.call-update) | async-done | bytes 165904 | tf_op jit(solution)/shard_map/psum | solution.py:120
  315.3 1.6 broadcast_multiply_fusion
  316.9 1.6 broadcast_multiply_fusion.1
  (206 shorter events, 75.6 us)
Async XLA Ops:
  7.2 5.7 %copy-start.34 = (bf16[64,128]{1,0:T(8,128)(2,1)S(1)}, bf16[64,128]{1,0:T(8,128)(2,1)}, u32[]{:S(2)}) copy-start(bf16[64,128]{1,0:T(8,128)(2,1)} %param.10) | copy-start | bytes 49156
  7.2 6.3 %copy-start.26 = (bf16[48,64,128]{2,1,0:T(8,128)(2,1)S(1)}, bf16[48,64,128]{2,1,0:T(8,128)(2,1)}, u32[]{:S(2)}) copy-start(bf16[48,64,128]{2,1,0:T(8,128)(2,1)} %param.11) | copy-start | bytes 2359300
  7.2 308.1 %all-reduce.3.cloned.1.call-start = ((), (), s32[]{:S(2)}) async-start(), calls=%async_computation | async-start | bytes 884736 | tf_op jit(solution)/shard_map/psum | solution.py:120
  9.8 11.1 %collective-permute-start = (bf16[48,1,128]{2,0,1:T(8,128)(2,1)S(1)}, bf16[48,1,128]{2,0,1:T(8,128)(2,1)S(1)}, u32[]{:S(2)}, u32[]{:S(2)}) collective-permute-start(bf16[48,1,128]{2,0,1:T(8,128)(2,1)S(1)} %get-tuple-element.88), channel_id=1, source_target_pairs={{0,8},{8,16},{16,24},{1,9},{9,17},{17,25},{2,10},{10,18},{18,26},{... | collective-permute-start | bytes 36872 | tf_op jit(solution)/shard_map/ppermute | solution.py:16
  11.6 9.4 %collective-permute-start.1 = (bf16[48,1,128]{2,0,1:T(8,128)(2,1)S(1)}, bf16[48,1,128]{2,0,1:T(8,128)(2,1)S(1)}, u32[]{:S(2)}, u32[]{:S(2)}) collective-permute-start(bf16[48,1,128]{2,0,1:T(8,128)(2,1)S(1)} %get-tuple-element.89), channel_id=1, source_target_pairs={{8,0},{16,8},{24,16},{9,1},{17,9},{25,17},{10,2},{18,10},{26,18},{... | collective-permute-start | bytes 36872 | tf_op jit(solution)/shard_map/ppermute | solution.py:17
  14.7 14.9 %collective-permute-start.8 = (bf16[48,1,128]{2,0,1:T(8,128)(2,1)S(1)}, bf16[48,1,128]{2,0,1:T(8,128)(2,1)S(1)}, u32[]{:S(2)}, u32[]{:S(2)}) collective-permute-start(bf16[48,1,128]{2,0,1:T(8,128)(2,1)S(1)} %get-tuple-element.80), channel_id=1, source_target_pairs={{0,8},{8,16},{16,24},{1,9},{9,17},{17,25},{2,10},{10,18},{18,26},{... | collective-permute-start | bytes 36872 | tf_op jit(solution)/shard_map/ppermute | solution.py:16
  19.0 10.6 %collective-permute-start.9 = (bf16[48,1,128]{2,0,1:T(8,128)(2,1)S(1)}, bf16[48,1,128]{2,0,1:T(8,128)(2,1)S(1)}, u32[]{:S(2)}, u32[]{:S(2)}) collective-permute-start(bf16[48,1,128]{2,0,1:T(8,128)(2,1)S(1)} %get-tuple-element.81), channel_id=1, source_target_pairs={{8,0},{16,8},{24,16},{9,1},{17,9},{25,17},{10,2},{18,10},{26,18},{... | collective-permute-start | bytes 36872 | tf_op jit(solution)/shard_map/ppermute | solution.py:17
  22.2 18.4 %collective-permute-start.2 = (bf16[48,66,1]{1,0,2:T(8,128)(2,1)S(1)}, bf16[48,66,1]{1,0,2:T(8,128)(2,1)S(1)}, u32[]{:S(2)}, u32[]{:S(2)}) collective-permute-start(bf16[48,66,1]{1,0,2:T(8,128)(2,1)S(1)} %copy.117), channel_id=1, source_target_pairs={{0,1},{1,2},{2,3},{3,4},{4,5},{5,6},{6,7},{8,9},{9,10},{10,11},{11... | collective-permute-start | bytes 19016 | tf_op jit(solution)/shard_map/ppermute | solution.py:16
  26.3 14.9 %collective-permute-start.3 = (bf16[48,66,1]{1,0,2:T(8,128)(2,1)S(1)}, bf16[48,66,1]{1,0,2:T(8,128)(2,1)S(1)}, u32[]{:S(2)}, u32[]{:S(2)}) collective-permute-start(bf16[48,66,1]{1,0,2:T(8,128)(2,1)S(1)} %copy.121), channel_id=1, source_target_pairs={{1,0},{2,1},{3,2},{4,3},{5,4},{6,5},{7,6},{9,8},{10,9},{11,10},{12... | collective-permute-start | bytes 19016 | tf_op jit(solution)/shard_map/ppermute | solution.py:17
  30.9 18.8 %collective-permute-start.10 = (bf16[48,66,1]{1,0,2:T(8,128)(2,1)S(1)}, bf16[48,66,1]{1,0,2:T(8,128)(2,1)S(1)}, u32[]{:S(2)}, u32[]{:S(2)}) collective-permute-start(bf16[48,66,1]{1,0,2:T(8,128)(2,1)S(1)} %copy.147), channel_id=1, source_target_pairs={{1,0},{2,1},{3,2},{4,3},{5,4},{6,5},{7,6},{9,8},{10,9},{11,10},{12... | collective-permute-start | bytes 19016 | tf_op jit(solution)/shard_map/ppermute | solution.py:17
  34.0 17.2 %collective-permute-start.11 = (bf16[48,66,1]{1,0,2:T(8,128)(2,1)S(1)}, bf16[48,66,1]{1,0,2:T(8,128)(2,1)S(1)}, u32[]{:S(2)}, u32[]{:S(2)}) collective-permute-start(bf16[48,66,1]{1,0,2:T(8,128)(2,1)S(1)} %copy.151), channel_id=1, source_target_pairs={{0,1},{1,2},{2,3},{3,4},{4,5},{5,6},{6,7},{8,9},{9,10},{10,11},{11... | collective-permute-start | bytes 19016 | tf_op jit(solution)/shard_map/ppermute | solution.py:16
  43.5 2.4 copy-start
  43.5 2.4 copy-start.2
  43.5 2.4 copy-start.29
  68.2 2.0 copy-start.3
  70.2 6.4 %copy-start.1 = (bf16[48,66,129]{2,0,1:T(8,128)(2,1)S(1)}, bf16[48,66,129]{2,0,1:T(8,128)(2,1)}, u32[]{:S(2)}) copy-start(bf16[48,66,129]{2,0,1:T(8,128)(2,1)} %copy-done) | copy-start | bytes 2452036
  71.8 54.3 %collective-permute-start.4 = (bf16[48,1,128]{2,0,1:T(8,128)(2,1)}, bf16[48,1,128]{2,0,1:T(8,128)(2,1)S(1)}, u32[]{:S(2)}, u32[]{:S(2)}) collective-permute-start(bf16[48,1,128]{2,0,1:T(8,128)(2,1)} %get-tuple-element.84), channel_id=1, source_target_pairs={{0,8},{8,16},{16,24},{1,9},{9,17},{17,25},{2,10},{10,18},{18,26},{... | collective-permute-start | bytes 36872 | tf_op jit(solution)/shard_map/ppermute | solution.py:16
  74.9 51.2 %collective-permute-start.5 = (bf16[48,1,128]{2,0,1:T(8,128)(2,1)}, bf16[48,1,128]{2,0,1:T(8,128)(2,1)S(1)}, u32[]{:S(2)}, u32[]{:S(2)}) collective-permute-start(bf16[48,1,128]{2,0,1:T(8,128)(2,1)} %get-tuple-element.85), channel_id=1, source_target_pairs={{8,0},{16,8},{24,16},{9,1},{17,9},{25,17},{10,2},{18,10},{26,18},{... | collective-permute-start | bytes 36872 | tf_op jit(solution)/shard_map/ppermute | solution.py:17
  78.6 1.5 copy-start.36
  78.6 46.2 %copy-start.35 = (bf16[48,1,128]{2,0,1:T(8,128)(2,1)S(1)}, bf16[48,1,128]{2,0,1:T(8,128)(2,1)}, u32[]{:S(2)}) copy-start(bf16[48,1,128]{2,0,1:T(8,128)(2,1)} %get-tuple-element.77) | copy-start | bytes 36868
  123.5 16.6 %collective-permute-start.12 = (bf16[48,1,128]{2,0,1:T(8,128)(2,1)}, bf16[48,1,128]{2,0,1:T(8,128)(2,1)S(1)}, u32[]{:S(2)}, u32[]{:S(2)}) collective-permute-start(bf16[48,1,128]{2,0,1:T(8,128)(2,1)} %get-tuple-element.76), channel_id=1, source_target_pairs={{0,8},{8,16},{16,24},{1,9},{9,17},{17,25},{2,10},{10,18},{18,26},{... | collective-permute-start | bytes 36872 | tf_op jit(solution)/shard_map/ppermute | solution.py:16
  124.8 15.3 %collective-permute-start.13 = (bf16[48,1,128]{2,0,1:T(8,128)(2,1)S(1)}, bf16[48,1,128]{2,0,1:T(8,128)(2,1)S(1)}, u32[]{:S(2)}, u32[]{:S(2)}) collective-permute-start(bf16[48,1,128]{2,0,1:T(8,128)(2,1)S(1)} %copy-done.35), channel_id=1, source_target_pairs={{8,0},{16,8},{24,16},{9,1},{17,9},{25,17},{10,2},{18,10},{26,18},{... | collective-permute-start | bytes 36872 | tf_op jit(solution)/shard_map/ppermute | solution.py:17
  130.1 24.5 %collective-permute-start.6 = (bf16[48,66,1]{1,0,2:T(8,128)(2,1)}, bf16[48,66,1]{1,0,2:T(8,128)(2,1)}, u32[]{:S(2)}, u32[]{:S(2)}) collective-permute-start(bf16[48,66,1]{1,0,2:T(8,128)(2,1)} %copy.133), channel_id=1, source_target_pairs={{0,1},{1,2},{2,3},{3,4},{4,5},{5,6},{6,7},{8,9},{9,10},{10,11},{11... | collective-permute-start | bytes 19016 | tf_op jit(solution)/shard_map/ppermute | solution.py:16
  136.8 20.2 %collective-permute-start.7 = (bf16[48,66,1]{1,0,2:T(8,128)(2,1)}, bf16[48,66,1]{1,0,2:T(8,128)(2,1)}, u32[]{:S(2)}, u32[]{:S(2)}) collective-permute-start(bf16[48,66,1]{1,0,2:T(8,128)(2,1)} %copy.137), channel_id=1, source_target_pairs={{1,0},{2,1},{3,2},{4,3},{5,4},{6,5},{7,6},{9,8},{10,9},{11,10},{12... | collective-permute-start | bytes 19016 | tf_op jit(solution)/shard_map/ppermute | solution.py:17
  143.5 30.5 %collective-permute-start.14 = (bf16[48,66,1]{1,0,2:T(8,128)(2,1)S(1)}, bf16[48,66,1]{1,0,2:T(8,128)(2,1)S(1)}, u32[]{:S(2)}, u32[]{:S(2)}) collective-permute-start(bf16[48,66,1]{1,0,2:T(8,128)(2,1)S(1)} %copy.161), channel_id=1, source_target_pairs={{1,0},{2,1},{3,2},{4,3},{5,4},{6,5},{7,6},{9,8},{10,9},{11,10},{12... | collective-permute-start | bytes 19016 | tf_op jit(solution)/shard_map/ppermute | solution.py:17
  150.5 24.3 %collective-permute-start.15 = (bf16[48,66,1]{1,0,2:T(8,128)(2,1)}, bf16[48,66,1]{1,0,2:T(8,128)(2,1)}, u32[]{:S(2)}, u32[]{:S(2)}) collective-permute-start(bf16[48,66,1]{1,0,2:T(8,128)(2,1)} %copy.165), channel_id=1, source_target_pairs={{0,1},{1,2},{2,3},{3,4},{4,5},{5,6},{6,7},{8,9},{9,10},{10,11},{11... | collective-permute-start | bytes 19016 | tf_op jit(solution)/shard_map/ppermute | solution.py:16
  169.0 1.4 copy-start.24
  169.0 1.4 copy-start.33
  169.0 1.4 copy-start.39
  169.0 1.4 copy-start.41
  182.4 1.6 copy-start.8
  184.0 1.8 copy-start.7
  (27 other events, 29.6 us)
Sparse Core Ops, SparseCore 0:
  184.1 131.1 all-reduce.2
where the time goes:
time: 332 us; the launch traced here: 326 us
  waiting for transfers between devices  114 us (34%)
  local copies, waits for them, and re-layouts  59.5 us (18%)
  blocking collectives  42.8 us (13%)
  starting transfers between devices  42.6 us (13%)
  other arithmetic  25.8 us (8%)
  matrix products  25.8 us (8%)
  between operations  15.3 us (5%)
    psum x1, waiting for transfers between devices, local(): lax.psum((local_w1, local_w2, local_cond), ('gy', 'gx'))  114 us
    psum x1, blocking collectives, local(): lax.psum((local_w1, local_w2, local_cond), ('gy', 'gx'))  42.8 us
    unnamed x93, local copies, waits for them, and re-layouts  29.6 us
    ppermute x8, starting transfers between devices, padded_2(): before = lax.ppermute(last, axis, up)  23.9 us
    dot_general x36, matrix products, tap_forward(): jnp.dot(weight_tap, flat, preferred_element_type=jnp.float32)  18.9 us
    ppermute x8, starting transfers between devices, padded_2(): after = lax.ppermute(first, axis, down)  18.7 us
    concatenate x8, other arithmetic, padded_2(): x = jnp.concatenate([before, x, after], axis=dim)  10.9 us
    slice x10, local copies, waits for them, and re-layouts, padded_2(): last = lax.slice_in_dim(x, length - width, length, axis=dim)  9.4 us
  transfers between devices with their start and end apart: 17, of which 1 were waited for; matrix products, arithmetic and copies ran while one was open for 20% of the time, Pallas kernels for 0%

commit v1 on v0

v1 whole, which is shorter than its diff:
```python
import jax
import jax.numpy as jnp
from jax import lax
from jax.experimental import pallas as pl
from jax.experimental.pallas import tpu as pltpu
from jax.sharding import PartitionSpec as P

TILE = 8
BF = jnp.bfloat16
F32 = jnp.float32
NT = (((1,), (1,)), ((), ()))
NN = (((1,), (0,)), ((), ()))
R1 = 3
R2 = 4


def lane_iota(rows):
    return lax.broadcasted_iota(jnp.int32, (rows, 128), 1)


def tile_rows(mask_ref):
    tcols = mask_ref.shape[1]
    lane = lax.broadcasted_iota(jnp.int32, (tcols, 128), 1)
    row = lax.broadcasted_iota(jnp.int32, (tcols, 128), 0)
    spread = (lane // TILE == row).astype(F32).astype(BF)
    return lax.dot_general(
        mask_ref[...].astype(F32).astype(BF), spread, NN, preferred_element_type=F32
    )


def row_kernel(sky_top, sky_bot, cot_top, cot_bot, phi_ref, mask_ref, up_ref, down_ref):
    chans = sky_top.shape[0]
    cells = tile_rows(mask_ref)
    for out, sky, cot, first, mrow, prow in (
        (up_ref, sky_top, cot_top, 0, 0, 0),
        (down_ref, sky_bot, cot_bot, 14, mask_ref.shape[0] - 1, phi_ref.shape[0] - 1),
    ):
        keep = cells[mrow : mrow + 1]
        low = jnp.broadcast_to(keep, (chans, 128)).astype(BF)
        for base, src in ((0, sky), (2 * chans, cot)):
            block = jnp.transpose(src[...], (1, 0, 2))
            for k in range(2):
                out[base + k * chans : base + (k + 1) * chans] = block[first + k] * low
        row = lax.broadcasted_iota(jnp.int32, (16, 128), 0)
        prow_v = jnp.broadcast_to(phi_ref[prow : prow + 1].astype(F32), (16, 128))
        extra = jnp.where(row == 0, prow_v, jnp.where(row == 1, keep, 0.0))
        out[4 * chans : 4 * chans + 16] = extra.astype(BF)


def col_kernel(sky_ref, cot_ref, phi_ref, mask_ref, top_ref, bot_ref, left_ref, right_ref, strip):
    chans, rows, width = sky_ref.shape
    half = chans // 2
    lane8 = lane_iota(8)
    row8 = lax.broadcasted_iota(jnp.int32, (8, 128), 0)
    pick = ((row8 < 2) & (lane8 == row8)) | (
        (row8 >= 2) & (row8 < 4) & (lane8 == row8 + (width - 4))
    )
    pick = pick.astype(F32).astype(BF)
    trows, tcols = mask_ref.shape
    prow = lax.broadcasted_iota(jnp.int32, (8, tcols), 0)
    pcol = lax.broadcasted_iota(jnp.int32, (8, tcols), 1)
    pick_t = ((prow < 2) & (pcol == 0)) | ((prow >= 2) & (prow < 4) & (pcol == tcols - 1))
    edge = lax.dot_general(
        pick_t.astype(F32).astype(BF),
        mask_ref[...].astype(F32).astype(BF),
        NT,
        preferred_element_type=F32,
    )
    lane_t = lax.broadcasted_iota(jnp.int32, (trows, 128), 1)
    row_t = lax.broadcasted_iota(jnp.int32, (trows, 128), 0)
    spread = (lane_t // TILE == row_t).astype(F32).astype(BF)
    keep = lax.dot_general(edge.astype(BF), spread, NN, preferred_element_type=F32)
    phis = lax.dot_general(pick, phi_ref[...], NT, preferred_element_type=F32)
    phis = jnp.concatenate([phis, jnp.zeros((8, 128 - rows), F32)], axis=1)
    lane = lane_iota(chans)
    for which, src in ((0, sky_ref), (1, cot_ref)):
        both = jnp.concatenate([src[:half], src[half:]], axis=1).reshape(half * 128, width)
        flat = lax.dot_general(pick, both, NT, preferred_element_type=F32)
        for j in range(half):
            strip[8 * j : 8 * j + 8] = flat[:, 128 * j : 128 * j + 128]
        for k in range(4):
            part = strip[pl.ds(k, half, stride=8), :]
            col = jnp.concatenate([part, pltpu.roll(part, 64, 1)], axis=0)
            col = (col * keep[k : k + 1]).astype(BF)
            at = (0, 1, width - 2, width - 1)[k]
            for ref, where in ((top_ref, (126, 127)), (bot_ref, (rows, rows + 1))):
                for n in range(2):
                    base = (2 * which + n) * chans
                    cell = ref[base : base + chans][:, at : at + 1]
                    col = jnp.where(lane == where[n], jnp.broadcast_to(cell, col.shape), col)
            out = (left_ref, right_ref)[k // 2]
            base = (2 * which + k % 2) * chans
            out[base : base + chans] = col
    row = lax.broadcasted_iota(jnp.int32, (16, 128), 0)
    lane16 = lane_iota(16)
    tops = top_ref[4 * chans : 4 * chans + 16].astype(F32)
    bots = bot_ref[4 * chans : 4 * chans + 16].astype(F32)
    for out, k, at in ((left_ref, 0, 0), (right_ref, 3, width - 1)):
        extra = jnp.where(
            row == 0,
            jnp.broadcast_to(phis[k : k + 1], (16, 128)),
            jnp.where(row == 1, jnp.broadcast_to(keep[k : k + 1], (16, 128)), 0.0),
        )
        extra = jnp.where(lane16 == 127, jnp.broadcast_to(tops[:, at : at + 1], (16, 128)), extra)
        extra = jnp.where(lane16 == rows, jnp.broadcast_to(bots[:, at : at + 1], (16, 128)), extra)
        out[4 * chans : 4 * chans + 16] = extra.astype(BF)


def silu_parts(pre):
    sigma = 1.0 / (1.0 + jnp.exp(-pre))
    return pre * sigma, sigma * (1.0 + pre * (1.0 - sigma))


def fill_sides(dst, y, base, step, chans, left_col, right_col, lane):
    at = y % 128
    centre = dst[base + chans : base + 2 * chans]
    left = jnp.where(
        lane == 0,
        jnp.broadcast_to(left_col[:, at : at + 1], centre.shape),
        pltpu.roll(centre, 1, 1),
    )
    right = jnp.where(
        lane == 127,
        jnp.broadcast_to(right_col[:, at : at + 1], centre.shape),
        pltpu.roll(centre, 127, 1),
    )
    dst[base : base + chans] = left
    dst[base + 2 * chans : base + 3 * chans] = right


def main_kernel(
    sky_ref, cot_ref, phi_ref, mask_ref, top_ref, bot_ref, lft_ref, rgt_ref, mylft_ref, myrgt_ref,
    w1c_ref, w2tc_ref, w1s_ref, w2ts_ref, w2s_ref, w1ts_ref, cond_ref,
    delens_ref, gin_ref, wire_ref,
    a3x, a3g, a3h, a3d, dz, gz, phix, maskx, outd, outg, acc1, acc2, cacc,
):
    chans, rows, width = sky_ref.shape
    step = 3 * chans
    lane = lane_iota(chans)
    trows = mask_ref.shape[0]
    zero = jnp.zeros((chans, 128), BF)

    cells = tile_rows(mask_ref)
    phix[0:1] = top_ref[4 * chans : 4 * chans + 16].astype(F32)[0:1]
    phix[rows + 1 : rows + 2] = bot_ref[4 * chans : 4 * chans + 16].astype(F32)[0:1]
    phix[1 : rows + 1] = phi_ref[...].astype(F32)
    maskx[0:1] = top_ref[4 * chans : 4 * chans + 16].astype(F32)[1:2]
    maskx[rows + 1 : rows + 2] = bot_ref[4 * chans : 4 * chans + 16].astype(F32)[1:2]
    for t in range(trows):
        maskx[1 + TILE * t : 1 + TILE * (t + 1)] = jnp.broadcast_to(cells[t : t + 1], (TILE, 128))

    gphi = jnp.zeros((chans, 128), F32)
    for which, src, dst in ((0, sky_ref, a3x), (1, cot_ref, a3g)):
        for j in range(rows // 16):
            block = jnp.transpose(src[:, 16 * j : 16 * j + 16, :], (1, 0, 2))
            for t in range(2):
                low = jnp.broadcast_to(cells[2 * j + t : 2 * j + t + 1], (chans, 128)).astype(BF)
                for n in range(TILE):
                    y = 16 * j + TILE * t + n
                    value = block[TILE * t + n] * low
                    dst[(y + 2) * step + chans : (y + 2) * step + 2 * chans] = value
                    if which:
                        gz[(y + 2) * chans : (y + 3) * chans] = value
                        gphi = gphi + value.astype(F32) * phix[y + 1 : y + 2]
        for ref, first in ((top_ref, -2), (bot_ref, rows)):
            for n in range(2):
                base = (first + n + 2) * step + chans
                dst[base : base + chans] = ref[(2 * which + n) * chans : (2 * which + n + 1) * chans]
        left_col = lft_ref[(2 * which + 1) * chans : (2 * which + 2) * chans]
        right_col = rgt_ref[2 * which * chans : (2 * which + 1) * chans]
        for y in range(-2, rows + 2):
            fill_sides(dst, y, (y + 2) * step, step, chans, left_col, right_col, lane)
    for z in (dz, gz):
        for y in (-2, -1, rows, rows + 1):
            z[(y + 2) * chans : (y + 3) * chans] = zero
    cacc[2] = gphi

    gain = cond_ref[:, 0:1]
    bias = cond_ref[:, 1:2]
    gain_two = cond_ref[:, 2:3]

    def ring(weights, which):
        base = 2 * which * chans
        pieces = []
        cols = (
            (lft_ref[base : base + chans], lft_ref[base + chans : base + 2 * chans],
             mylft_ref[base : base + chans]),
            (myrgt_ref[base + chans : base + 2 * chans], rgt_ref[base : base + chans],
             rgt_ref[base + chans : base + 2 * chans]),
        )
        for ky in range(3):
            for kx in range(3):
                pair = [
                    side[kx] if ky == 1 else pltpu.roll(side[kx], (1, 0, 127)[ky], 1)
                    for side in cols
                ]
                pieces.append(jnp.concatenate(pair, axis=1))
        return lax.dot_general(
            weights, jnp.concatenate(pieces, axis=0), NN, preferred_element_type=F32
        )

    extra_l = lft_ref[4 * chans : 4 * chans + 16].astype(F32)
    extra_r = rgt_ref[4 * chans : 4 * chans + 16].astype(F32)
    phi_c = jnp.concatenate([extra_l[0:1], extra_r[0:1]], axis=1)
    mask_c = jnp.concatenate([extra_l[1:2], extra_r[1:2]], axis=1)
    pre_c = ring(w1c_ref[...], 0) + gain * phi_c + bias
    act_c, slope_c = silu_parts(pre_c)
    hid_c = (act_c * mask_c).astype(BF)
    dpre_c = (ring(w2tc_ref[...], 1) * mask_c * slope_c).astype(BF)

    split = (rows + 2) // 2
    sums = (jnp.zeros((chans, 128), F32), jnp.zeros((chans, 128), F32))

    def first_pass(it, carry):
        y0 = R1 * it - 1
        win = (R1 + 2) * step

        def both(src):
            a = pl.multiple_of((y0 + 1) * step, 16)
            b = pl.multiple_of((y0 + split + 1) * step, 16)
            return jnp.concatenate([src[pl.ds(a, win), :], src[pl.ds(b, win), :]], axis=1)

        pre = lax.dot_general(w1s_ref[...], both(a3x), NN, preferred_element_type=F32)
        back = lax.dot_general(w2ts_ref[...], both(a3g), NN, preferred_element_type=F32)
        for h in range(2):
            for r in range(R1):
                row = y0 + h * split + r + 1
                here = (slice(r * chans, (r + 1) * chans), slice(h * 128, h * 128 + 128))
                keep = maskx[pl.ds(row, 1), :]
                act, slope = silu_parts(pre[here] + gain * phix[pl.ds(row, 1), :] + bias)
                base = pl.multiple_of(row * step + chans, 16)
                a3h[pl.ds(base, chans), :] = (act * keep).astype(BF)
                a3d[pl.ds(base, chans), :] = (back[here] * keep * slope).astype(BF)
        return carry

    lax.fori_loop(0, split // R1, first_pass, 0)

    for dst, col in ((a3h, hid_c), (a3d, dpre_c)):
        for y in range(-1, rows + 1):
            fill_sides(dst, y, (y + 1) * step, step, chans, col[:, :128], col[:, 128:], lane)
    dphi, dsum = sums
    for y in range(rows):
        value = a3d[(y + 1) * step + chans : (y + 1) * step + 2 * chans]
        dz[(y + 2) * chans : (y + 3) * chans] = value
        wide = value.astype(F32)
        dphi = dphi + wide * phix[y + 1 : y + 2]
        dsum = dsum + wide
    cacc[0] = dphi
    cacc[1] = dsum

    acc1[...] = jnp.zeros_like(acc1)
    acc2[...] = jnp.zeros_like(acc2)
    group = 6

    def grads(it, carry):
        for z, field, off, acc in ((dz, a3x, 2, acc1), (gz, a3h, 1, acc2)):
            lhs, rhs = [], []
            for n in range(group):
                r = group * it + n - 1
                lhs.append(z[pl.ds(pl.multiple_of((r + 1) * chans, 16), step), :])
                rhs.append(field[pl.ds(pl.multiple_of((r + off) * step, 16), step), :])
            acc[...] += lax.dot_general(
                jnp.concatenate(lhs, axis=1), jnp.concatenate(rhs, axis=1), NT,
                preferred_element_type=F32,
            )
        return carry

    lax.fori_loop(0, (rows + 2) // group, grads, 0)

    def second_pass(it, carry):
        y0 = R2 * it
        win = (R2 + 2) * step

        def both(src):
            a = pl.multiple_of(y0 * step, 16)
            b = pl.multiple_of((y0 + rows // 2) * step, 16)
            return jnp.concatenate([src[pl.ds(a, win), :], src[pl.ds(b, win), :]], axis=1)

        fwd = lax.dot_general(w2s_ref[...], both(a3h), NN, preferred_element_type=F32)
        bwd = lax.dot_general(w1ts_ref[...], both(a3d), NN, preferred_element_type=F32)
        for h in range(2):
            for r in range(R2):
                y = y0 + h * (rows // 2) + r
                here = (slice(r * chans, (r + 1) * chans), slice(h * 128, h * 128 + 128))
                keep = maskx[pl.ds(y + 1, 1), :]
                base = pl.multiple_of((y + 2) * step + chans, 16)
                x0 = a3x[pl.ds(base, chans), :].astype(F32)
                g0 = a3g[pl.ds(base, chans), :].astype(F32)
                out = (x0 + fwd[here] + gain_two * phix[pl.ds(y + 1, 1), :]) * keep
                outd[y] = out.astype(BF)
                outg[y] = ((g0 + bwd[here]) * keep).astype(BF)
        return carry

    lax.fori_loop(0, rows // (2 * R2), second_pass, 0)
    for j in range(rows // 16):
        delens_ref[:, 16 * j : 16 * j + 16, :] = jnp.transpose(outd[16 * j : 16 * j + 16], (1, 0, 2))
        gin_ref[:, 16 * j : 16 * j + 16, :] = jnp.transpose(outg[16 * j : 16 * j + 16], (1, 0, 2))

    wide = jnp.concatenate([acc1[...], acc2[...]], axis=1)
    wire_ref[0:step] = wide[:, :128]
    wire_ref[step : 2 * step] = wide[:, 128:256]
    rest = wide[:, 256 : 2 * step]
    cond = jnp.concatenate(
        [jnp.sum(cacc[k], axis=1, keepdims=True) for k in range(3)]
        + [jnp.zeros((chans, 128 - 3 * rest.shape[1] - 3), F32)],
        axis=1,
    )
    wire_ref[2 * step : 2 * step + chans] = jnp.concatenate(
        [rest[k * chans : (k + 1) * chans] for k in range(3)] + [cond], axis=1
    )


def unpack_kernel(factor, wire_ref, w1_ref, w2_ref, cond_ref):
    chans = w1_ref.shape[2]
    step = 3 * chans
    tail = wire_ref[2 * step : 2 * step + chans]
    rest_w = 2 * step - 256
    rest = jnp.concatenate([tail[:, k * rest_w : (k + 1) * rest_w] for k in range(3)], axis=0)
    wide = jnp.concatenate([wire_ref[0:step], wire_ref[step : 2 * step], rest], axis=1) * factor
    for ref, base in ((w1_ref, 0), (w2_ref, step)):
        for ky in range(3):
            for kx in range(3):
                ref[ky, kx] = wide[
                    (2 - ky) * chans : (3 - ky) * chans,
                    base + kx * chans : base + (kx + 1) * chans,
                ]
    cond_ref[...] = jnp.transpose(tail * factor)[3 * rest_w : 3 * rest_w + 3, :chans]


def stacked(block, count, chans):
    step = 3 * chans
    return jnp.concatenate(
        [jnp.pad(block, ((0, 0), (r * step, (count - 1 - r) * step))) for r in range(count)], axis=0
    )


def build(mesh):
    ny, nx = mesh.shape["gy"], mesh.shape["gx"]
    axes = ("gy", "gx")

    def links(move):
        pairs = []
        for a in range(ny):
            for b in range(nx):
                to = move(a, b)
                if 0 <= to[0] < ny and 0 <= to[1] < nx:
                    pairs.append((a * nx + b, to[0] * nx + to[1]))
        return pairs

    def send(value, move):
        return lax.ppermute(value, axes, links(move))

    def local(
        sky, lens_phi, cotangent, tile_mask, weight_one, weight_two, cond_one, bias_one, cond_two
    ):
        chans, rows, width = sky.shape
        step = 3 * chans
        edge = jax.ShapeDtypeStruct((4 * chans + 16, 128), BF)
        vmem = pl.BlockSpec(memory_space=pltpu.VMEM)
        first = pl.BlockSpec((chans, 16, width), lambda i: (0, 0, 0))
        last = pl.BlockSpec((chans, 16, width), lambda i: (0, rows // 16 - 1, 0))
        up, down = pl.pallas_call(
            row_kernel,
            grid=(1,),
            out_shape=(edge, edge),
            in_specs=[first, last, first, last, vmem, vmem],
            out_specs=(vmem, vmem),
            name="edge_rows",
        )(sky, sky, cotangent, cotangent, lens_phi, tile_mask)
        bot = send(up, lambda a, b: (a - 1, b))
        top = send(down, lambda a, b: (a + 1, b))

        def taps(weight, back):
            if back:
                return weight[::-1, ::-1].transpose(3, 0, 1, 2).reshape(chans, 3 * step)
            return weight.transpose(2, 0, 1, 3).reshape(chans, 3 * step)

        w1f, w1b = taps(weight_one, False), taps(weight_one, True)
        w2f, w2b = taps(weight_two, False), taps(weight_two, True)
        conds = jnp.stack([cond_one, bias_one, cond_two], axis=1)
        conds = jnp.pad(conds, ((0, 0), (0, 125)))

        to_left, to_right = pl.pallas_call(
            col_kernel,
            out_shape=(edge, edge),
            scratch_shapes=[pltpu.VMEM((8 * chans // 2, 128), F32)],
            name="edge_cols",
        )(sky, cotangent, lens_phi, tile_mask, top, bot)
        rgt = send(to_left, lambda a, b: (a, b - 1))
        lft = send(to_right, lambda a, b: (a, b + 1))

        field = pltpu.VMEM(((rows + 4) * step, 128), BF)
        inner = pltpu.VMEM(((rows + 2) * step, 128), BF)
        centre = pltpu.VMEM(((rows + 4) * chans, 128), BF)
        rowwise = pltpu.VMEM((rows + 8, 128), F32)
        outrow = pltpu.VMEM((rows, chans, 128), BF)
        acc = pltpu.VMEM((step, step), F32)
        maps = jax.ShapeDtypeStruct(sky.shape, BF)
        delensed, grad_input, wire = pl.pallas_call(
            main_kernel,
            out_shape=(maps, maps, jax.ShapeDtypeStruct((2 * step + chans, 128), F32)),
            scratch_shapes=[
                field, field, inner, inner, centre, centre, rowwise, rowwise, outrow, outrow,
                acc, acc, pltpu.VMEM((3, chans, 128), F32),
            ],
            compiler_params=pltpu.CompilerParams(vmem_limit_bytes=40 << 20),
            name="convolutions",
        )(
            sky, cotangent, lens_phi, tile_mask, top, bot, lft, rgt, to_left, to_right,
            w1f, w2b, stacked(w1f, R1, chans), stacked(w2b, R1, chans),
            stacked(w2f, R2, chans), stacked(w1b, R2, chans), conds,
        )

        bit = 1
        while bit < ny:
            wire = wire + send(wire, lambda a, b: (a ^ bit, b))
            bit *= 2
        bit = 1
        while bit < nx:
            wire = wire + send(wire, lambda a, b: (a, b ^ bit))
            bit *= 2

        factor = float(1.0 / (rows * ny * width * nx) ** 0.5)
        grads = jax.ShapeDtypeStruct((3, 3, chans, chans), F32)
        grad_w1, grad_w2, grad_cond = pl.pallas_call(
            lambda *refs: unpack_kernel(factor, *refs),
            out_shape=(grads, grads, jax.ShapeDtypeStruct((3, chans), F32)),
            name="unpack",
        )(wire)
        return delensed, grad_input, grad_w1, grad_w2, grad_cond

    return local


def solution(mesh):
    return jax.shard_map(
        build(mesh),
        mesh=mesh,
        in_specs=(
            P(None, "gy", "gx"),
            P("gy", "gx"),
            P(None, "gy", "gx"),
            P("gy", "gx"),
            P(),
            P(),
            P(),
            P(),
            P(),
        ),
        out_specs=(P(None, "gy", "gx"), P(None, "gy", "gx"), P(), P(), P()),
        check_vma=False,
    )
```

time: 332 us -> 76.9 us (0.23)
  the two profiles are of different devices: /device:TPU:8 before, /device:TPU:0 now
where the time goes in v1:
time: 76.9 us; the launch traced here: 76.4 us
  waiting for transfers between devices  27 us (35%)
  Pallas kernels  24.1 us (31%)
  starting transfers between devices  18.8 us (24%)
  local copies, waits for them, and re-layouts  4.56 us (6%)
  other arithmetic  1.09 us (1%)
  between operations  0.87 us (1%)
    ppermute x9, waiting for transfers between devices, send(): return lax.ppermute(value, axes, links(move))  27 us
    ppermute x9, starting transfers between devices, send(): return lax.ppermute(value, axes, links(move))  18.8 us
    pallas_call x1, Pallas kernels, local(): pl.pallas_call(main_kernel, out_shape=(maps, maps, jax.ShapeDtypeStruct((...  17.4 us
    unnamed x30, local copies, waits for them, and re-layouts  3.88 us
    pallas_call x1, Pallas kernels, local(): pl.pallas_call(col_kernel, out_shape=(edge, edge), scratch_shapes=[pltpu....  2.81 us
    pallas_call x1, Pallas kernels, local(): pl.pallas_call(row_kernel, grid=(1,), out_shape=(edge, edge), in_specs=[f...  2.05 us
    pallas_call x1, Pallas kernels, local(): pl.pallas_call(lambda *refs: unpack_kernel(factor, *refs), out_shape=(gra...  1.81 us
  transfers between devices with their start and end apart: 9, of which 8 were waited for; matrix products, arithmetic and copies ran while one was open for 1% of the time, Pallas kernels for 0%

profile of v1, /device:TPU:0, one launch (start us, length us, event | category | flops | bytes accessed | tf_op | source)
XLA Modules:
  0.0 76.4 jit_solution(4017052439061946888)
XLA Ops:
  0.6 2.0 %edge_rows.1 = (bf16[208,128]{1,0:T(8,128)(2,1)}, bf16[208,128]{1,0:T(8,128)(2,1)}) custom-call(bf16[48,64,128]{2,1,0:T(8,128)(2,1)} %sky_ref.3, bf16[48,64,128]{2,1,0:T(8,128)(2,1)} %sky_ref.3, bf16[48,64,128]{2,1,0:T(8,128)(2,1)} %cot_ref.3, bf16[48,64,128]{2,1,0:T(8,128)(2,1)} %cot_ref.3, bf16[64,128]{1,0:T(8,128)(2,1)} %phi_ref.5, s32[8,16]{1,0:T(8,128)} %mask_ref.5), custom_call_target="tpu_custom_call" | custom-call | tf_op jit(solution)/shard_map/edge_rows/pallas_call | solution.py:362
  2.7 2.3 %collective-permute-start = (bf16[208,128]{1,0:T(8,128)(2,1)}, bf16[208,128]{1,0:T(8,128)(2,1)S(1)}, u32[]{:S(2)}, u32[]{:S(2)}) collective-permute-start(bf16[208,128]{1,0:T(8,128)(2,1)} %get-tuple-element.15), channel_id=1, source_target_pairs={{0,8},{1,9},{2,10},{3,11},{4,12},{5,13},{6,14},{7,15},{8,16},{9,17... | collective-permute-start | bytes 159752 | tf_op jit(solution)/shard_map/ppermute | solution.py:351
  5.0 1.3 %collective-permute-start.1 = (bf16[208,128]{1,0:T(8,128)(2,1)}, bf16[208,128]{1,0:T(8,128)(2,1)S(1)}, u32[]{:S(2)}, u32[]{:S(2)}) collective-permute-start(bf16[208,128]{1,0:T(8,128)(2,1)} %get-tuple-element.16), channel_id=1, source_target_pairs={{8,0},{9,1},{10,2},{11,3},{12,4},{13,5},{14,6},{15,7},{16,8},{17,9... | collective-permute-start | bytes 159752 | tf_op jit(solution)/shard_map/ppermute | solution.py:351
  6.4 0.1 copy.34
  6.5 0.8 %copy-done.10 = bf16[3,3,48,48]{3,2,1,0:T(8,128)(2,1)S(1)} copy-done((bf16[3,3,48,48]{3,2,1,0:T(8,128)(2,1)S(1)}, bf16[3,3,48,48]{3,2,1,0:T(8,128)(2,1)}, u32[]{:S(2)}) %copy-start.10) | copy-done | bytes 41496
  7.5 0.1 reshape.24
  7.6 0.1 reshape.22.w1c_ref
  7.8 0.2 fusion.19
  8.0 0.1 fusion.24
  8.2 2.3 %collective-permute-done.1.bot_ref = bf16[208,128]{1,0:T(8,128)(2,1)S(1)} collective-permute-done((bf16[208,128]{1,0:T(8,128)(2,1)}, bf16[208,128]{1,0:T(8,128)(2,1)S(1)}, u32[]{:S(2)}, u32[]{:S(2)}) %collective-permute-start.1) | collective-permute-done | bytes 53280 | tf_op jit(solution)/shard_map/ppermute | solution.py:351
  10.5 0.6 copy-done.4
  11.1 2.8 %edge_cols.1 = (bf16[208,128]{1,0:T(8,128)(2,1)}, bf16[208,128]{1,0:T(8,128)(2,1)}) custom-call(bf16[48,64,128]{2,1,0:T(8,128)(2,1)} %sky_ref.3, bf16[48,64,128]{2,1,0:T(8,128)(2,1)} %cot_ref.3, bf16[64,128]{1,0:T(8,128)(2,1)} %phi_ref.5, s32[8,16]{1,0:T(8,128)} %mask_ref.5, bf16[208,128]{1,0:T(8,128)(2,1)} %copy-done.2, bf16[208,128]{1,0:T(8,128)(2,1)} %copy-done.4), custom_call_target="tpu_custom_call" | custom-call | tf_op jit(solution)/shard_map/edge_cols/pallas_call | solution.py:383
  13.9 3.5 %collective-permute-start.2 = (bf16[208,128]{1,0:T(8,128)(2,1)}, bf16[208,128]{1,0:T(8,128)(2,1)S(1)}, u32[]{:S(2)}, u32[]{:S(2)}) collective-permute-start(bf16[208,128]{1,0:T(8,128)(2,1)} %get-tuple-element.17.myrgt_ref), channel_id=1, source_target_pairs={{0,1},{1,2},{2,3},{3,4},{4,5},{5,6},{6,7},{8,9},{9,10},{10,11},{11... | collective-permute-start | bytes 159752 | tf_op jit(solution)/shard_map/ppermute | solution.py:351
  17.5 1.3 %collective-permute-start.3 = (bf16[208,128]{1,0:T(8,128)(2,1)}, bf16[208,128]{1,0:T(8,128)(2,1)S(1)}, u32[]{:S(2)}, u32[]{:S(2)}) collective-permute-start(bf16[208,128]{1,0:T(8,128)(2,1)} %get-tuple-element.18.mylft_ref), channel_id=1, source_target_pairs={{1,0},{2,1},{3,2},{4,3},{5,4},{6,5},{7,6},{9,8},{10,9},{11,10},{12... | collective-permute-start | bytes 159752 | tf_op jit(solution)/shard_map/ppermute | solution.py:351
  18.9 0.6 collective-permute-done.2.lft_ref
  19.6 4.2 %collective-permute-done.3.rgt_ref = bf16[208,128]{1,0:T(8,128)(2,1)S(1)} collective-permute-done((bf16[208,128]{1,0:T(8,128)(2,1)}, bf16[208,128]{1,0:T(8,128)(2,1)S(1)}, u32[]{:S(2)}, u32[]{:S(2)}) %collective-permute-start.3) | collective-permute-done | bytes 53280 | tf_op jit(solution)/shard_map/ppermute | solution.py:351
  23.8 0.8 %copy-done.5 = bf16[208,128]{1,0:T(8,128)(2,1)S(1)} copy-done((bf16[208,128]{1,0:T(8,128)(2,1)S(1)}, bf16[208,128]{1,0:T(8,128)(2,1)}, u32[]{:S(2)}) %copy-start.5) | copy-done | bytes 53272
  24.6 0.8 %copy-done.7 = bf16[208,128]{1,0:T(8,128)(2,1)S(1)} copy-done((bf16[208,128]{1,0:T(8,128)(2,1)S(1)}, bf16[208,128]{1,0:T(8,128)(2,1)}, u32[]{:S(2)}) %copy-start.7) | copy-done | bytes 53272
  25.4 0.8 %copy-done.8 = bf16[208,128]{1,0:T(8,128)(2,1)S(1)} copy-done((bf16[208,128]{1,0:T(8,128)(2,1)S(1)}, bf16[208,128]{1,0:T(8,128)(2,1)}, u32[]{:S(2)}) %copy-start.8) | copy-done | bytes 53272
  26.2 17.4 %convolutions.1 = (bf16[48,64,128]{2,1,0:T(8,128)(2,1)}, bf16[48,64,128]{2,1,0:T(8,128)(2,1)}, f32[336,128]{1,0:T(8,128)S(1)}) custom-call(bf16[48,64,128]{2,1,0:T(8,128)(2,1)S(1)} %copy-done, bf16[48,64,128]{2,1,0:T(8,128)(2,1)S(1)} %copy-done.1, bf16[64,128]{1,0:T(8,128)(2,1)S(1)} %copy-done.6, s32[8,16]{1,0:T(8,128)S(1)} %copy-done.9, ...), custom_call_target="tpu_custom_call" | custom-call | tf_op jit(solution)/shard_map/convolutions/pallas_call | solution.py:399
  43.6 1.4 %collective-permute-start.4 = (f32[336,128]{1,0:T(8,128)S(1)}, f32[336,128]{1,0:T(8,128)S(1)}, u32[]{:S(2)}, u32[]{:S(2)}) collective-permute-start(f32[336,128]{1,0:T(8,128)S(1)} %get-tuple-element.21), channel_id=1, source_target_pairs={{0,8},{1,9},{2,10},{3,11},{4,12},{5,13},{6,14},{7,15},{8,0},{9,1},... | collective-permute-start | bytes 516104 | tf_op jit(solution)/shard_map/ppermute | solution.py:351
  45.0 1.0 %collective-permute-done.4 = f32[336,128]{1,0:T(8,128)S(1)} collective-permute-done((f32[336,128]{1,0:T(8,128)S(1)}, f32[336,128]{1,0:T(8,128)S(1)}, u32[]{:S(2)}, u32[]{:S(2)}) %collective-permute-start.4) | collective-permute-done | bytes 172064 | tf_op jit(solution)/shard_map/ppermute | solution.py:351
  46.0 2.2 %collective-permute-start.5 = (f32[336,128]{1,0:T(8,128)S(1)}, f32[336,128]{1,0:T(8,128)S(1)}, u32[]{:S(2)}, u32[]{:S(2)}) collective-permute-start(f32[336,128]{1,0:T(8,128)S(1)} %add.45), channel_id=1, source_target_pairs={{0,16},{1,17},{2,18},{3,19},{4,20},{5,21},{6,22},{7,23},{8,24},{9,... | collective-permute-start | bytes 516104 | tf_op jit(solution)/shard_map/ppermute | solution.py:351
  48.2 4.7 %collective-permute-done.5 = f32[336,128]{1,0:T(8,128)S(1)} collective-permute-done((f32[336,128]{1,0:T(8,128)S(1)}, f32[336,128]{1,0:T(8,128)S(1)}, u32[]{:S(2)}, u32[]{:S(2)}) %collective-permute-start.5) | collective-permute-done | bytes 172064 | tf_op jit(solution)/shard_map/ppermute | solution.py:351
  52.9 2.5 %collective-permute-start.6 = (f32[336,128]{1,0:T(8,128)S(1)}, f32[336,128]{1,0:T(8,128)S(1)}, u32[]{:S(2)}, u32[]{:S(2)}) collective-permute-start(f32[336,128]{1,0:T(8,128)S(1)} %add.46), channel_id=1, source_target_pairs={{0,1},{1,0},{2,3},{3,2},{4,5},{5,4},{6,7},{7,6},{8,9},{9,8},{10,11... | collective-permute-start | bytes 516104 | tf_op jit(solution)/shard_map/ppermute | solution.py:351
  55.4 4.2 %collective-permute-done.6 = f32[336,128]{1,0:T(8,128)S(1)} collective-permute-done((f32[336,128]{1,0:T(8,128)S(1)}, f32[336,128]{1,0:T(8,128)S(1)}, u32[]{:S(2)}, u32[]{:S(2)}) %collective-permute-start.6) | collective-permute-done | bytes 172064 | tf_op jit(solution)/shard_map/ppermute | solution.py:351
  59.6 1.6 %collective-permute-start.7 = (f32[336,128]{1,0:T(8,128)S(1)}, f32[336,128]{1,0:T(8,128)S(1)}, u32[]{:S(2)}, u32[]{:S(2)}) collective-permute-start(f32[336,128]{1,0:T(8,128)S(1)} %add.47), channel_id=1, source_target_pairs={{0,2},{1,3},{2,0},{3,1},{4,6},{5,7},{6,4},{7,5},{8,10},{9,11},{10,... | collective-permute-start | bytes 516104 | tf_op jit(solution)/shard_map/ppermute | solution.py:351
  61.2 3.8 %collective-permute-done.7 = f32[336,128]{1,0:T(8,128)S(1)} collective-permute-done((f32[336,128]{1,0:T(8,128)S(1)}, f32[336,128]{1,0:T(8,128)S(1)}, u32[]{:S(2)}, u32[]{:S(2)}) %collective-permute-start.7) | collective-permute-done | bytes 172064 | tf_op jit(solution)/shard_map/ppermute | solution.py:351
  65.1 2.7 %collective-permute-start.8 = (f32[336,128]{1,0:T(8,128)S(1)}, f32[336,128]{1,0:T(8,128)S(1)}, u32[]{:S(2)}, u32[]{:S(2)}) collective-permute-start(f32[336,128]{1,0:T(8,128)S(1)} %add.48), channel_id=1, source_target_pairs={{0,4},{1,5},{2,6},{3,7},{4,0},{5,1},{6,2},{7,3},{8,12},{9,13},{10,... | collective-permute-start | bytes 516104 | tf_op jit(solution)/shard_map/ppermute | solution.py:351
  67.8 6.2 %collective-permute-done.8 = f32[336,128]{1,0:T(8,128)S(1)} collective-permute-done((f32[336,128]{1,0:T(8,128)S(1)}, f32[336,128]{1,0:T(8,128)S(1)}, u32[]{:S(2)}, u32[]{:S(2)}) %collective-permute-start.8) | collective-permute-done | bytes 172064 | tf_op jit(solution)/shard_map/ppermute | solution.py:351
  73.9 0.7 add.49.refs_0_
  74.6 1.8 %unpack.1 = (f32[3,3,48,48]{3,2,1,0:T(8,128)}, f32[3,3,48,48]{3,2,1,0:T(8,128)}, f32[3,48]{1,0:T(4,128)}) custom-call(f32[336,128]{1,0:T(8,128)} %add.49.refs_0_), custom_call_target="tpu_custom_call" | custom-call | tf_op jit(solution)/shard_map/unpack/pallas_call | solution.py:425
  (38 shorter events, 0.5 us)
Async XLA Ops:
  0.6 5.7 %copy-start.11 = (bf16[3,3,48,48]{3,2,1,0:T(8,128)(2,1)S(1)}, bf16[3,3,48,48]{3,2,1,0:T(8,128)(2,1)}, u32[]{:S(2)}) copy-start(bf16[3,3,48,48]{3,2,1,0:T(8,128)(2,1)} %param.13) | copy-start | bytes 124420
  2.7 5.4 %collective-permute-start = (bf16[208,128]{1,0:T(8,128)(2,1)}, bf16[208,128]{1,0:T(8,128)(2,1)S(1)}, u32[]{:S(2)}, u32[]{:S(2)}) collective-permute-start(bf16[208,128]{1,0:T(8,128)(2,1)} %get-tuple-element.15), channel_id=1, source_target_pairs={{0,8},{1,9},{2,10},{3,11},{4,12},{5,13},{6,14},{7,15},{8,16},{9,17... | collective-permute-start | bytes 159752 | tf_op jit(solution)/shard_map/ppermute | solution.py:351
  5.0 5.4 %collective-permute-start.1 = (bf16[208,128]{1,0:T(8,128)(2,1)}, bf16[208,128]{1,0:T(8,128)(2,1)S(1)}, u32[]{:S(2)}, u32[]{:S(2)}) collective-permute-start(bf16[208,128]{1,0:T(8,128)(2,1)} %get-tuple-element.16), channel_id=1, source_target_pairs={{8,0},{9,1},{10,2},{11,3},{12,4},{13,5},{14,6},{15,7},{16,8},{17,9... | collective-permute-start | bytes 159752 | tf_op jit(solution)/shard_map/ppermute | solution.py:351
  6.4 0.9 %copy-start.10 = (bf16[3,3,48,48]{3,2,1,0:T(8,128)(2,1)S(1)}, bf16[3,3,48,48]{3,2,1,0:T(8,128)(2,1)}, u32[]{:S(2)}) copy-start(bf16[3,3,48,48]{3,2,1,0:T(8,128)(2,1)} %param.14) | copy-start | bytes 124420
  8.1 15.6 %copy-start = (bf16[48,64,128]{2,1,0:T(8,128)(2,1)S(1)}, bf16[48,64,128]{2,1,0:T(8,128)(2,1)}, u32[]{:S(2)}) copy-start(bf16[48,64,128]{2,1,0:T(8,128)(2,1)} %sky_ref.3) | copy-start | bytes 2359300
  8.1 15.6 %copy-start.1 = (bf16[48,64,128]{2,1,0:T(8,128)(2,1)S(1)}, bf16[48,64,128]{2,1,0:T(8,128)(2,1)}, u32[]{:S(2)}) copy-start(bf16[48,64,128]{2,1,0:T(8,128)(2,1)} %cot_ref.3) | copy-start | bytes 2359300
  8.1 2.4 %copy-start.2 = (bf16[208,128]{1,0:T(8,128)(2,1)}, bf16[208,128]{1,0:T(8,128)(2,1)S(1)}, u32[]{:S(2)}) copy-start(bf16[208,128]{1,0:T(8,128)(2,1)S(1)} %collective-permute-done.top_ref) | copy-start | bytes 159748
  10.5 0.6 copy-start.4
  11.1 7.7 %copy-start.12 = (f32[48]{0:T(128)S(1)}, f32[48]{0:T(128)}, u32[]{:S(2)}) copy-start(f32[48]{0:T(128)} %param.17) | copy-start | bytes 580
  11.1 7.7 %copy-start.13 = (f32[48]{0:T(128)S(1)}, f32[48]{0:T(128)}, u32[]{:S(2)}) copy-start(f32[48]{0:T(128)} %param.16) | copy-start | bytes 580
  11.1 7.7 %copy-start.14 = (f32[48]{0:T(128)S(1)}, f32[48]{0:T(128)}, u32[]{:S(2)}) copy-start(f32[48]{0:T(128)} %param.15) | copy-start | bytes 580
  13.9 9.8 %copy-start.3 = (bf16[208,128]{1,0:T(8,128)(2,1)S(1)}, bf16[208,128]{1,0:T(8,128)(2,1)}, u32[]{:S(2)}) copy-start(bf16[208,128]{1,0:T(8,128)(2,1)} %copy-done.2) | copy-start | bytes 159748
  13.9 5.6 %collective-permute-start.2 = (bf16[208,128]{1,0:T(8,128)(2,1)}, bf16[208,128]{1,0:T(8,128)(2,1)S(1)}, u32[]{:S(2)}, u32[]{:S(2)}) collective-permute-start(bf16[208,128]{1,0:T(8,128)(2,1)} %get-tuple-element.17.myrgt_ref), channel_id=1, source_target_pairs={{0,1},{1,2},{2,3},{3,4},{4,5},{5,6},{6,7},{8,9},{9,10},{10,11},{11... | collective-permute-start | bytes 159752 | tf_op jit(solution)/shard_map/ppermute | solution.py:351
  17.5 6.2 %collective-permute-start.3 = (bf16[208,128]{1,0:T(8,128)(2,1)}, bf16[208,128]{1,0:T(8,128)(2,1)S(1)}, u32[]{:S(2)}, u32[]{:S(2)}) collective-permute-start(bf16[208,128]{1,0:T(8,128)(2,1)} %get-tuple-element.18.mylft_ref), channel_id=1, source_target_pairs={{1,0},{2,1},{3,2},{4,3},{5,4},{6,5},{7,6},{9,8},{10,9},{11,10},{12... | collective-permute-start | bytes 159752 | tf_op jit(solution)/shard_map/ppermute | solution.py:351
  18.9 4.8 %copy-start.6 = (bf16[64,128]{1,0:T(8,128)(2,1)S(1)}, bf16[64,128]{1,0:T(8,128)(2,1)}, u32[]{:S(2)}) copy-start(bf16[64,128]{1,0:T(8,128)(2,1)} %phi_ref.5) | copy-start | bytes 49156
  18.9 4.8 %copy-start.9 = (s32[8,16]{1,0:T(8,128)S(1)}, s32[8,16]{1,0:T(8,128)}, u32[]{:S(2)}) copy-start(s32[8,16]{1,0:T(8,128)} %mask_ref.5) | copy-start | bytes 1540
  23.8 0.8 %copy-start.5 = (bf16[208,128]{1,0:T(8,128)(2,1)S(1)}, bf16[208,128]{1,0:T(8,128)(2,1)}, u32[]{:S(2)}) copy-start(bf16[208,128]{1,0:T(8,128)(2,1)} %copy-done.4) | copy-start | bytes 159748
  24.6 0.8 %copy-start.7 = (bf16[208,128]{1,0:T(8,128)(2,1)S(1)}, bf16[208,128]{1,0:T(8,128)(2,1)}, u32[]{:S(2)}) copy-start(bf16[208,128]{1,0:T(8,128)(2,1)} %get-tuple-element.18.mylft_ref) | copy-start | bytes 159748
  25.4 0.8 %copy-start.8 = (bf16[208,128]{1,0:T(8,128)(2,1)S(1)}, bf16[208,128]{1,0:T(8,128)(2,1)}, u32[]{:S(2)}) copy-start(bf16[208,128]{1,0:T(8,128)(2,1)} %get-tuple-element.17.myrgt_ref) | copy-start | bytes 159748
  43.6 2.4 %collective-permute-start.4 = (f32[336,128]{1,0:T(8,128)S(1)}, f32[336,128]{1,0:T(8,128)S(1)}, u32[]{:S(2)}, u32[]{:S(2)}) collective-permute-start(f32[336,128]{1,0:T(8,128)S(1)} %get-tuple-element.21), channel_id=1, source_target_pairs={{0,8},{1,9},{2,10},{3,11},{4,12},{5,13},{6,14},{7,15},{8,0},{9,1},... | collective-permute-start | bytes 516104 | tf_op jit(solution)/shard_map/ppermute | solution.py:351
  46.0 6.8 %collective-permute-start.5 = (f32[336,128]{1,0:T(8,128)S(1)}, f32[336,128]{1,0:T(8,128)S(1)}, u32[]{:S(2)}, u32[]{:S(2)}) collective-permute-start(f32[336,128]{1,0:T(8,128)S(1)} %add.45), channel_id=1, source_target_pairs={{0,16},{1,17},{2,18},{3,19},{4,20},{5,21},{6,22},{7,23},{8,24},{9,... | collective-permute-start | bytes 516104 | tf_op jit(solution)/shard_map/ppermute | solution.py:351
  52.9 6.7 %collective-permute-start.6 = (f32[336,128]{1,0:T(8,128)S(1)}, f32[336,128]{1,0:T(8,128)S(1)}, u32[]{:S(2)}, u32[]{:S(2)}) collective-permute-start(f32[336,128]{1,0:T(8,128)S(1)} %add.46), channel_id=1, source_target_pairs={{0,1},{1,0},{2,3},{3,2},{4,5},{5,4},{6,7},{7,6},{8,9},{9,8},{10,11... | collective-permute-start | bytes 516104 | tf_op jit(solution)/shard_map/ppermute | solution.py:351
  59.6 5.5 %collective-permute-start.7 = (f32[336,128]{1,0:T(8,128)S(1)}, f32[336,128]{1,0:T(8,128)S(1)}, u32[]{:S(2)}, u32[]{:S(2)}) collective-permute-start(f32[336,128]{1,0:T(8,128)S(1)} %add.47), channel_id=1, source_target_pairs={{0,2},{1,3},{2,0},{3,1},{4,6},{5,7},{6,4},{7,5},{8,10},{9,11},{10,... | collective-permute-start | bytes 516104 | tf_op jit(solution)/shard_map/ppermute | solution.py:351
  65.1 8.8 %collective-permute-start.8 = (f32[336,128]{1,0:T(8,128)S(1)}, f32[336,128]{1,0:T(8,128)S(1)}, u32[]{:S(2)}, u32[]{:S(2)}) collective-permute-start(f32[336,128]{1,0:T(8,128)S(1)} %add.48), channel_id=1, source_target_pairs={{0,4},{1,5},{2,6},{3,7},{4,0},{5,1},{6,2},{7,3},{8,12},{9,13},{10,... | collective-permute-start | bytes 516104 | tf_op jit(solution)/shard_map/ppermute | solution.py:351

commit v2 on v1

v2 whole, which is shorter than its diff:
```python
import jax
import jax.numpy as jnp
from jax import lax
from jax.experimental import pallas as pl
from jax.experimental.pallas import tpu as pltpu
from jax.sharding import PartitionSpec as P

TILE = 8
BF = jnp.bfloat16
F32 = jnp.float32
NT = (((1,), (1,)), ((), ()))
NN = (((1,), (0,)), ((), ()))
R1 = 3
R2 = 4
GROUP1 = 6
GROUP2 = 8


def lane_iota(rows):
    return lax.broadcasted_iota(jnp.int32, (rows, 128), 1)


def tile_rows(mask_ref):
    tcols = mask_ref.shape[1]
    lane = lax.broadcasted_iota(jnp.int32, (tcols, 128), 1)
    row = lax.broadcasted_iota(jnp.int32, (tcols, 128), 0)
    spread = (lane // TILE == row).astype(F32).astype(BF)
    return lax.dot_general(
        mask_ref[...].astype(F32).astype(BF), spread, NN, preferred_element_type=F32
    )


def is_odd(axis):
    return lax.rem(lax.axis_index(axis), 2) == 1


def row_kernel(sky_top, sky_bot, cot_top, cot_bot, phi_ref, mask_ref, a_ref, b_ref):
    chans = sky_top.shape[0]
    cells = tile_rows(mask_ref)
    odd = is_odd("gy")
    parts = []
    for sky, cot, first, mrow, prow in (
        (sky_top, cot_top, 0, 0, 0),
        (sky_bot, cot_bot, 14, mask_ref.shape[0] - 1, phi_ref.shape[0] - 1),
    ):
        keep = cells[mrow : mrow + 1]
        low = jnp.broadcast_to(keep, (chans, 128)).astype(BF)
        part = []
        for src in (sky, cot):
            block = jnp.transpose(src[...], (1, 0, 2))
            part += [block[first] * low, block[first + 1] * low]
        row = lax.broadcasted_iota(jnp.int32, (16, 128), 0)
        prow_v = jnp.broadcast_to(phi_ref[prow : prow + 1].astype(F32), (16, 128))
        part.append(jnp.where(row == 0, prow_v, jnp.where(row == 1, keep, 0.0)).astype(BF))
        parts.append(jnp.concatenate(part, axis=0))
    up, down = parts
    a_ref[...] = jnp.where(odd, up, down)
    b_ref[...] = jnp.where(odd, down, up)


def col_kernel(
    sky_ref, cot_ref, phi_ref, mask_ref, a_ref, b_ref,
    sa_ref, sb_ref, own_ref, halo_ref, strip,
):
    chans, rows, width = sky_ref.shape
    size = a_ref.shape[0]
    odd = is_odd("gy")
    ra, rb = a_ref[...], b_ref[...]
    tops_all = jnp.where(odd, ra, rb)
    bots_all = jnp.where(odd, rb, ra)
    halo_ref[0] = tops_all
    halo_ref[1] = bots_all
    half = chans // 2
    lane8 = lane_iota(8)
    row8 = lax.broadcasted_iota(jnp.int32, (8, 128), 0)
    pick = ((row8 < 2) & (lane8 == row8)) | (
        (row8 >= 2) & (row8 < 4) & (lane8 == row8 + (width - 4))
    )
    pick = pick.astype(F32).astype(BF)
    trows, tcols = mask_ref.shape
    prow = lax.broadcasted_iota(jnp.int32, (8, tcols), 0)
    pcol = lax.broadcasted_iota(jnp.int32, (8, tcols), 1)
    pick_t = ((prow < 2) & (pcol == 0)) | ((prow >= 2) & (prow < 4) & (pcol == tcols - 1))
    edge = lax.dot_general(
        pick_t.astype(F32).astype(BF),
        mask_ref[...].astype(F32).astype(BF),
        NT,
        preferred_element_type=F32,
    )
    lane_t = lax.broadcasted_iota(jnp.int32, (trows, 128), 1)
    row_t = lax.broadcasted_iota(jnp.int32, (trows, 128), 0)
    spread = (lane_t // TILE == row_t).astype(F32).astype(BF)
    keep = lax.dot_general(edge.astype(BF), spread, NN, preferred_element_type=F32)
    phis = lax.dot_general(pick, phi_ref[...], NT, preferred_element_type=F32)
    phis = jnp.concatenate([phis, jnp.zeros((8, 128 - rows), F32)], axis=1)
    lane = lane_iota(chans)
    for which, src in ((0, sky_ref), (1, cot_ref)):
        both = jnp.concatenate([src[:half], src[half:]], axis=1).reshape(half * 128, width)
        flat = lax.dot_general(pick, both, NT, preferred_element_type=F32)
        for j in range(half):
            strip[8 * j : 8 * j + 8] = flat[:, 128 * j : 128 * j + 128]
        for k in range(4):
            part = strip[pl.ds(k, half, stride=8), :]
            col = jnp.concatenate([part, pltpu.roll(part, 64, 1)], axis=0)
            col = (col * keep[k : k + 1]).astype(BF)
            at = (0, 1, width - 2, width - 1)[k]
            for value, where in ((tops_all, (126, 127)), (bots_all, (rows, rows + 1))):
                for n in range(2):
                    base = (2 * which + n) * chans
                    cell = value[base : base + chans, at : at + 1]
                    col = jnp.where(lane == where[n], jnp.broadcast_to(cell, col.shape), col)
            base = (2 * which + k % 2) * chans
            own_ref[k // 2, base : base + chans] = col
    row = lax.broadcasted_iota(jnp.int32, (16, 128), 0)
    lane16 = lane_iota(16)
    tops = tops_all[4 * chans : size].astype(F32)
    bots = bots_all[4 * chans : size].astype(F32)
    for side, k, at in ((0, 0, 0), (1, 3, width - 1)):
        extra = jnp.where(
            row == 0,
            jnp.broadcast_to(phis[k : k + 1], (16, 128)),
            jnp.where(row == 1, jnp.broadcast_to(keep[k : k + 1], (16, 128)), 0.0),
        )
        extra = jnp.where(lane16 == 127, jnp.broadcast_to(tops[:, at : at + 1], (16, 128)), extra)
        extra = jnp.where(lane16 == rows, jnp.broadcast_to(bots[:, at : at + 1], (16, 128)), extra)
        own_ref[side, 4 * chans : size] = extra.astype(BF)
    odd_x = is_odd("gx")
    sa_ref[...] = jnp.where(odd_x, own_ref[0], own_ref[1])
    sb_ref[...] = jnp.where(odd_x, own_ref[1], own_ref[0])


def silu_parts(pre):
    sigma = 1.0 / (1.0 + jnp.exp(-pre))
    return pre * sigma, sigma * (1.0 + pre * (1.0 - sigma))


def two_windows(src, first, second, size):
    a = pl.multiple_of(first, 16)
    b = pl.multiple_of(second, 16)
    return jnp.concatenate([src[pl.ds(a, size), :], src[pl.ds(b, size), :]], axis=1)


def hidden_kernel(
    sky_ref, cot_ref, phi_ref, mask_ref, halo_ref, w1s_ref, w2ts_ref, cond_ref,
    hid_ref, dpre_ref, acc1, acc2, cacc,
    a3x, a3g, dz, phix, maskx,
):
    chans, rows, width = sky_ref.shape
    size = halo_ref.shape[1]
    step = 3 * chans
    trows = mask_ref.shape[0]
    cells = tile_rows(mask_ref)
    lane1 = lane_iota(1)
    inside = jnp.where((lane1 == 0) | (lane1 == 127), 0.0, 1.0)
    for k, at in ((0, 0), (1, rows + 1)):
        extra = halo_ref[k, 4 * chans : size].astype(F32)
        phix[at : at + 1] = extra[0:1]
        maskx[at : at + 1] = extra[1:2] * inside
    phix[1 : rows + 1] = phi_ref[...].astype(F32)
    for t in range(trows):
        maskx[1 + TILE * t : 1 + TILE * (t + 1)] = jnp.broadcast_to(
            cells[t : t + 1] * inside, (TILE, 128)
        )

    gphi = jnp.zeros((chans, 128), F32)

    def put(dst, y, value):
        base = (y + 2) * step
        dst[base : base + chans] = pltpu.roll(value, 1, 1)
        dst[base + chans : base + 2 * chans] = value
        dst[base + 2 * chans : base + 3 * chans] = pltpu.roll(value, 127, 1)

    for which, src, dst in ((0, sky_ref, a3x), (1, cot_ref, a3g)):
        for j in range(rows // 16):
            block = jnp.transpose(src[:, 16 * j : 16 * j + 16, :], (1, 0, 2))
            for t in range(2):
                low = jnp.broadcast_to(cells[2 * j + t : 2 * j + t + 1], (chans, 128)).astype(BF)
                for n in range(TILE):
                    y = 16 * j + TILE * t + n
                    value = block[TILE * t + n] * low
                    put(dst, y, value)
                    if which:
                        gphi = gphi + value.astype(F32) * phix[y + 1 : y + 2]
        for k, first in ((0, -2), (1, rows)):
            for n in range(2):
                base = (2 * which + n) * chans
                put(dst, first + n, halo_ref[k, base : base + chans])
    cacc[2] = gphi

    gain = cond_ref[:, 0:1]
    bias = cond_ref[:, 1:2]
    split = (rows + 2) // 2
    zero = jnp.zeros((chans, 128), BF)
    for y in (-2, -1, rows, rows + 1):
        dz[(y + 2) * chans : (y + 3) * chans] = zero

    def first_pass(it, carry):
        y0 = R1 * it - 1
        win = (R1 + 2) * step
        at = ((y0 + 1) * step, (y0 + split + 1) * step)
        pre = lax.dot_general(
            w1s_ref[...], two_windows(a3x, *at, win), NN, preferred_element_type=F32
        )
        back = lax.dot_general(
            w2ts_ref[...], two_windows(a3g, *at, win), NN, preferred_element_type=F32
        )
        for h in range(2):
            for r in range(R1):
                row = y0 + h * split + r + 1
                here = (slice(r * chans, (r + 1) * chans), slice(h * 128, h * 128 + 128))
                keep = maskx[pl.ds(row, 1), :]
                act, slope = silu_parts(pre[here] + gain * phix[pl.ds(row, 1), :] + bias)
                base = pl.multiple_of(row * chans, 16)
                hid_ref[pl.ds(base, chans), :] = (act * keep).astype(BF)
                dpre_ref[pl.ds(base, chans), :] = (back[here] * keep * slope).astype(BF)
        return carry

    lax.fori_loop(0, split // R1, first_pass, 0)

    dphi = jnp.zeros((chans, 128), F32)
    dsum = jnp.zeros((chans, 128), F32)
    for y in range(rows):
        value = dpre_ref[(y + 1) * chans : (y + 2) * chans]
        dz[(y + 2) * chans : (y + 3) * chans] = value
        wide = value.astype(F32)
        dphi = dphi + wide * phix[y + 1 : y + 2]
        dsum = dsum + wide
    cacc[0] = dphi
    cacc[1] = dsum

    acc1[...] = jnp.zeros_like(acc1)
    acc2[...] = jnp.zeros_like(acc2)

    def rows_of(src, start, size):
        return src[pl.ds(pl.multiple_of(start, 16), size), :]

    def grads_one(it, carry):
        ys = [GROUP1 * it + n - 1 for n in range(GROUP1)]
        acc1[...] += lax.dot_general(
            jnp.concatenate([rows_of(dz, (y + 1) * chans, step) for y in ys], axis=1),
            jnp.concatenate([rows_of(a3x, (y + 2) * step, step) for y in ys], axis=1),
            NT, preferred_element_type=F32,
        )
        return carry

    def grads_two(it, carry):
        ys = [GROUP2 * it + n for n in range(GROUP2)]
        acc2[...] += lax.dot_general(
            jnp.concatenate([rows_of(a3g, (y + 2) * step, step) for y in ys], axis=1),
            jnp.concatenate([rows_of(hid_ref, y * chans, step) for y in ys], axis=1),
            NT, preferred_element_type=F32,
        )
        return carry

    lax.fori_loop(0, (rows + 2) // GROUP1, grads_one, 0)
    lax.fori_loop(0, rows // GROUP2, grads_two, 0)


def edge_kernel(
    rows, a_ref, b_ref, own_ref, w1c_ref, w2tc_ref, cond_ref, acc1, acc2, cacc,
    hcol_ref, dcol_ref, keep_ref, give_ref, wire,
):
    size = a_ref.shape[0]
    chans = (size - 16) // 4
    step = 3 * chans
    odd = is_odd("gx")
    ra, rb = a_ref[...], b_ref[...]
    lft = jnp.where(odd, ra, rb)
    rgt = jnp.where(odd, rb, ra)
    own_l, own_r = own_ref[0], own_ref[1]

    def at(value, which, n):
        base = (2 * which + n) * chans
        return value[base : base + chans]

    def columns(which):
        return [at(v, which, n) for v in (lft, own_l, own_r, rgt) for n in range(2)]

    centres = (1, 2, 5, 6)

    def taps_of(cols):
        pieces = []
        for ky in range(3):
            moved = [c if ky == 1 else pltpu.roll(c, (1, 0, 127)[ky], 1) for c in cols]
            for kx in range(3):
                pieces.append(jnp.concatenate([moved[c + kx - 1] for c in centres], axis=1))
        return jnp.concatenate(pieces, axis=0)

    x_taps = taps_of(columns(0))
    g_cols = columns(1)
    extra = [v[4 * chans : size].astype(F32) for v in (lft, own_l, own_r, rgt)]
    phi_c = jnp.concatenate([e[0:1] for e in extra], axis=1)
    mask_c = jnp.concatenate([e[1:2] for e in extra], axis=1)
    pre = lax.dot_general(w1c_ref[...], x_taps, NN, preferred_element_type=F32)
    back = lax.dot_general(w2tc_ref[...], taps_of(g_cols), NN, preferred_element_type=F32)
    act, slope = silu_parts(pre + cond_ref[:, 0:1] * phi_c + cond_ref[:, 1:2])
    hcol = (act * mask_c).astype(BF)
    dcol = (back * mask_c * slope).astype(BF)
    hcol_ref[...] = hcol
    dcol_ref[...] = dcol

    mine = jnp.broadcast_to((lane_iota(1) < rows).astype(F32), (chans, 128)).astype(BF)
    d_own = [dcol[:, 128:256] * mine, dcol[:, 256:384] * mine]
    part1 = lax.dot_general(
        jnp.concatenate(d_own, axis=1), x_taps[:, 128:384], NT, preferred_element_type=F32
    )
    h_cols = [hcol[:, 128 * k : 128 * k + 128] for k in range(4)]
    g_own = {k: g_cols[n] * mine for k, n in ((0, 2), (1, 3), (2, 4), (3, 5))}
    for kx, pairs in (
        (0, ((0, 0), (1, 1))),
        (1, ((0, 1), (3, 2))),
        (2, ((2, 2), (3, 3))),
    ):
        lhs = jnp.concatenate([g_own[g] for g, _ in pairs], axis=1)
        rhs = []
        for ky in range(3):
            moved = [
                h_cols[h] if ky == 1 else pltpu.roll(h_cols[h], (1, 0, 127)[ky], 1)
                for _, h in pairs
            ]
            rhs.append(jnp.concatenate(moved, axis=1))
        part2 = lax.dot_general(
            lhs, jnp.concatenate(rhs, axis=0), NT, preferred_element_type=F32
        )
        low = (2 - kx) * chans
        wide = jnp.concatenate(
            [
                acc1[low : low + chans] + part1[:, kx * step : (kx + 1) * step],
                acc2[low : low + chans] + part2,
            ],
            axis=1,
        )
        wire[low : low + chans] = wide[:, :128]
        wire[step + low : step + low + chans] = wide[:, 128:256]
        if kx == 0:
            tails = []
        tails.insert(0, wide[:, 256 : 2 * step])
    dphi, dsum = cacc[0], cacc[1]
    for d, k in ((d_own[0], 1), (d_own[1], 2)):
        dphi = dphi + d.astype(F32) * extra[k][0:1]
        dsum = dsum + d.astype(F32)
    sums = [jnp.sum(v, axis=1, keepdims=True) for v in (dphi, dsum, cacc[2])]
    fill = jnp.zeros((chans, 128 - 3 * tails[0].shape[1] - 3), F32)
    wire[2 * step : 2 * step + chans] = jnp.concatenate(tails + sums + [fill], axis=1)
    count = wire.shape[0] // 2
    core = lax.rem(lax.axis_index("gy"), 2)
    keep_ref[...] = wire[pl.ds(pl.multiple_of(core * count, 8), count), :]
    give_ref[...] = wire[pl.ds(pl.multiple_of((1 - core) * count, 8), count), :]


def output_kernel(
    with_phi, src_ref, phi_ref, mask_ref, mid_ref, col_ref, weights_ref, cond_ref,
    out_ref, a3, rowbuf, phix,
):
    chans, rows, width = src_ref.shape
    step = 3 * chans
    lane = lane_iota(chans)
    cells = tile_rows(mask_ref)
    cols = [col_ref[:, 128 * k : 128 * k + 128] for k in range(4)]
    if with_phi:
        phix[...] = phi_ref[...].astype(F32)
        gain = cond_ref[:, 2:3]

    def cell(col, y):
        at = y % 128
        return jnp.broadcast_to(col[:, at : at + 1], (chans, 128))

    for y in range(-1, rows + 1):
        centre = mid_ref[(y + 1) * chans : (y + 2) * chans]
        centre = jnp.where(lane == 0, cell(cols[1], y), centre)
        centre = jnp.where(lane == 127, cell(cols[2], y), centre)
        base = (y + 1) * step
        a3[base : base + chans] = jnp.where(
            lane == 0, cell(cols[0], y), pltpu.roll(centre, 1, 1)
        )
        a3[base + chans : base + 2 * chans] = centre
        a3[base + 2 * chans : base + 3 * chans] = jnp.where(
            lane == 127, cell(cols[3], y), pltpu.roll(centre, 127, 1)
        )

    def second_pass(it, carry):
        y0 = R2 * it
        got = lax.dot_general(
            weights_ref[...],
            two_windows(a3, y0 * step, (y0 + rows // 2) * step, (R2 + 2) * step),
            NN, preferred_element_type=F32,
        )
        for h in range(2):
            for r in range(R2):
                y = y0 + h * (rows // 2) + r
                part = got[r * chans : (r + 1) * chans, h * 128 : h * 128 + 128]
                if with_phi:
                    part = part + gain * phix[pl.ds(y, 1), :]
                rowbuf[y] = part
        return carry

    lax.fori_loop(0, rows // (2 * R2), second_pass, 0)
    for j in range(rows // 16):
        block = jnp.transpose(src_ref[:, 16 * j : 16 * j + 16, :], (1, 0, 2))
        done = []
        for n in range(16):
            keep = cells[(16 * j + n) // TILE : (16 * j + n) // TILE + 1]
            done.append(((rowbuf[16 * j + n] + block[n].astype(F32)) * keep).astype(BF))
        out_ref[:, 16 * j : 16 * j + 16, :] = jnp.transpose(jnp.stack(done), (1, 0, 2))


def unpack_kernel(factor, keep_ref, other_ref, w1_ref, w2_ref, cond_ref, wire):
    chans = w1_ref.shape[2]
    step = 3 * chans
    count = keep_ref.shape[0]
    core = lax.rem(lax.axis_index("gy"), 2)
    wire[pl.ds(pl.multiple_of(core * count, 8), count), :] = keep_ref[...]
    wire[pl.ds(pl.multiple_of((1 - core) * count, 8), count), :] = other_ref[...]
    tail = wire[2 * step : 2 * step + chans] * factor
    rest_w = 2 * step - 256
    for n in range(3):
        low = n * chans
        wide = jnp.concatenate(
            [
                wire[low : low + chans] * factor,
                wire[step + low : step + low + chans] * factor,
                tail[:, n * rest_w : (n + 1) * rest_w],
            ],
            axis=1,
        )
        for k in range(3):
            w1_ref[2 - n, k] = wide[:, k * chans : (k + 1) * chans]
            w2_ref[k, 2 - n] = wide[:, step + k * chans : step + (k + 1) * chans]
    cond_ref[...] = jnp.transpose(tail)[3 * rest_w : 3 * rest_w + 3, :chans]


def stacked(block, count, chans):
    step = 3 * chans
    return jnp.concatenate(
        [jnp.pad(block, ((0, 0), (r * step, (count - 1 - r) * step))) for r in range(count)], axis=0
    )


def build(mesh):
    ny, nx = mesh.shape["gy"], mesh.shape["gx"]
    axes = ("gy", "gx")

    def send(value, move):
        pairs = []
        for a in range(ny):
            for b in range(nx):
                to = move(a, b)
                if 0 <= to[0] < ny and 0 <= to[1] < nx:
                    pairs.append((a * nx + b, to[0] * nx + to[1]))
        return lax.ppermute(value, axes, pairs)

    def swap(first, second, axis):
        def partner(offset):
            def move(a, b):
                v = [a, b]
                v[axis] += 1 if (v[axis] + offset) % 2 == 0 else -1
                return v

            return move

        return send(first, partner(0)), send(second, partner(1))

    def local(
        sky, lens_phi, cotangent, tile_mask, weight_one, weight_two, cond_one, bias_one, cond_two
    ):
        chans, rows, width = sky.shape
        step = 3 * chans
        size = 4 * chans + 16
        edge = jax.ShapeDtypeStruct((size, 128), BF)
        edges = jax.ShapeDtypeStruct((2, size, 128), BF)
        vmem = pl.BlockSpec(memory_space=pltpu.VMEM)
        first = pl.BlockSpec((chans, 16, width), lambda i: (0, 0, 0))
        last = pl.BlockSpec((chans, 16, width), lambda i: (0, rows // 16 - 1, 0))
        ra, rb = pl.pallas_call(
            row_kernel,
            grid=(1,),
            out_shape=(edge, edge),
            in_specs=[first, last, first, last, vmem, vmem],
            out_specs=(vmem, vmem),
            name="edge_rows",
        )(sky, sky, cotangent, cotangent, lens_phi, tile_mask)
        ra, rb = swap(ra, rb, 0)

        def taps(weight, back):
            if back:
                return weight[::-1, ::-1].transpose(3, 0, 1, 2).reshape(chans, 3 * step)
            return weight.transpose(2, 0, 1, 3).reshape(chans, 3 * step)

        w1f, w1b = taps(weight_one, False), taps(weight_one, True)
        w2f, w2b = taps(weight_two, False), taps(weight_two, True)
        conds = jnp.stack([cond_one, bias_one, cond_two], axis=1)
        conds = jnp.pad(conds, ((0, 0), (0, 125)))

        ca, cb, own, halo = pl.pallas_call(
            col_kernel,
            out_shape=(edge, edge, edges, edges),
            scratch_shapes=[pltpu.VMEM((8 * chans // 2, 128), F32)],
            name="edge_cols",
        )(sky, cotangent, lens_phi, tile_mask, ra, rb)
        ca, cb = swap(ca, cb, 1)

        flops = 2 * 9 * chans * chans * rows * width
        field = pltpu.VMEM(((rows + 4) * step, 128), BF)
        rowwise = pltpu.VMEM((rows + 8, 128), F32)
        inner = jax.ShapeDtypeStruct(((rows + 2) * chans, 128), BF)
        acc = jax.ShapeDtypeStruct((step, step), F32)
        hid, dpre, acc1, acc2, cacc = pl.pallas_call(
            hidden_kernel,
            out_shape=(inner, inner, acc, acc, jax.ShapeDtypeStruct((3, chans, 128), F32)),
            scratch_shapes=[
                field, field, pltpu.VMEM(((rows + 4) * chans, 128), BF), rowwise, rowwise,
            ],
            compiler_params=pltpu.CompilerParams(vmem_limit_bytes=32 << 20),
            cost_estimate=pl.CostEstimate(
                flops=8 * flops, bytes_accessed=8 << 20, transcendentals=0
            ),
            name="hidden",
        )(
            sky, cotangent, lens_phi, tile_mask, halo,
            stacked(w1f, R1, chans), stacked(w2b, R1, chans), conds,
        )

        cols = jax.ShapeDtypeStruct((chans, 512), BF)
        count = (2 * step + chans) // 2
        wires = jax.ShapeDtypeStruct((count, 128), F32)
        hcol, dcol, keep, give = pl.pallas_call(
            lambda *refs: edge_kernel(rows, *refs),
            out_shape=(cols, cols, wires, wires),
            scratch_shapes=[pltpu.VMEM((2 * count, 128), F32)],
            name="edge_parts",
        )(ca, cb, own, w1f, w2b, conds, acc1, acc2, cacc)

        def output(with_phi, src, mid, col, weights, name):
            return pl.pallas_call(
                lambda *refs: output_kernel(with_phi, *refs),
                out_shape=jax.ShapeDtypeStruct(src.shape, BF),
                scratch_shapes=[
                    pltpu.VMEM(((rows + 2) * step, 128), BF),
                    pltpu.VMEM((rows, chans, 128), F32),
                    pltpu.VMEM((rows, 128), F32),
                ],
                compiler_params=pltpu.CompilerParams(vmem_limit_bytes=16 << 20),
                cost_estimate=pl.CostEstimate(
                    flops=2 * flops, bytes_accessed=4 << 20, transcendentals=0
                ),
                name=name,
            )(src, lens_phi, tile_mask, mid, col, weights, conds)

        delensed = output(True, sky, hid, hcol, stacked(w2f, R2, chans), "delensed")
        grad_input = output(False, cotangent, dpre, dcol, stacked(w1b, R2, chans), "grad_input")

        keep = keep + send(give, lambda a, b: (a ^ 1, b))
        for bit in [1 << k for k in range(1, ny.bit_length() - 1)]:
            keep = keep + send(keep, lambda a, b: (a ^ bit, b))
        for bit in [1 << k for k in range(nx.bit_length() - 1)]:
            keep = keep + send(keep, lambda a, b: (a, b ^ bit))
        other = send(keep, lambda a, b: (a ^ 1, b))

        factor = float(1.0 / (rows * ny * width * nx) ** 0.5)
        grads = jax.ShapeDtypeStruct((3, 3, chans, chans), F32)
        grad_w1, grad_w2, grad_cond = pl.pallas_call(
            lambda *refs: unpack_kernel(factor, *refs),
            out_shape=(grads, grads, jax.ShapeDtypeStruct((3, chans), F32)),
            scratch_shapes=[pltpu.VMEM((2 * count, 128), F32)],
            name="unpack",
        )(keep, other)
        return delensed, grad_input, grad_w1, grad_w2, grad_cond

    return local


def solution(mesh):
    return jax.shard_map(
        build(mesh),
        mesh=mesh,
        in_specs=(
            P(None, "gy", "gx"),
            P("gy", "gx"),
            P(None, "gy", "gx"),
            P("gy", "gx"),
            P(),
            P(),
            P(),
            P(),
            P(),
        ),
        out_specs=(P(None, "gy", "gx"), P(None, "gy", "gx"), P(), P(), P()),
        check_vma=False,
    )
```

time: 76.9 us -> 82.7 us (1.075)
  waiting for transfers between devices: 27 us -> 11.8 us
  Pallas kernels: 24.1 us -> 39.1 us
  local copies, waits for them, and re-layouts: 4.56 us -> 9.83 us
  other arithmetic: 1.09 us -> 3.55 us
  starting transfers between devices: 18.8 us -> 16.5 us
    ppermute x9 -> x10, waiting for transfers between devices: 27 us -> 11.8 us  [send(): return lax.ppermute(value, axes, pairs)]
    pallas_call x2 -> x5, Pallas kernels: 20.2 us -> 35.1 us  [the longest x2 19.6 us: output(): pl.pallas_call(lambda *refs: output_kernel(with_phi, *refs), out_shape=ja...]
    unnamed x30 -> x52, local copies, waits for them, and re-layouts: 3.88 us -> 8.25 us
    ppermute x9 -> x10, starting transfers between devices: 18.8 us -> 16.5 us  [send(): return lax.ppermute(value, axes, pairs)]
    add x5, other arithmetic: 0.77 us -> 2.51 us  [the longest x3 0.96 us: local(): keep = keep + send(keep, lambda a, b: (a, b ^ bit))]
    transpose x2, local copies, waits for them, and re-layouts: 0.12 us -> 1.02 us  [taps(): return weight.transpose(2, 0, 1, 3).reshape(chans, 3 * step)]
  transfers between devices with their start and end apart: 9 -> 10, of which waited for: 8 -> 5; matrix products, arithmetic and copies ran while one was open for 1% -> 3% of each run, Pallas kernels for 0% -> 36%
where the time goes in v2:
time: 82.7 us; the launch traced here: 81.7 us
  Pallas kernels  39.1 us (47%)
  starting transfers between devices  16.5 us (20%)
  waiting for transfers between devices  11.8 us (14%)
  local copies, waits for them, and re-layouts  9.83 us (12%)
  other arithmetic  3.55 us (4%)
  between operations  0.91 us (1%)
    pallas_call x2, Pallas kernels, output(): pl.pallas_call(lambda *refs: output_kernel(with_phi, *refs), out_shape=ja...  19.6 us
    ppermute x10, starting transfers between devices, send(): return lax.ppermute(value, axes, pairs)  16.5 us
    ppermute x10, waiting for transfers between devices, send(): return lax.ppermute(value, axes, pairs)  11.8 us
    pallas_call x1, Pallas kernels, local(): pl.pallas_call(hidden_kernel, out_shape=(inner, inner, acc, acc, jax.Shap...  9.99 us
    unnamed x52, local copies, waits for them, and re-layouts  8.25 us
    pallas_call x1, Pallas kernels, local(): pl.pallas_call(col_kernel, out_shape=(edge, edge, edges, edges), scratch_...  2.83 us
    pallas_call x1, Pallas kernels, local(): pl.pallas_call(lambda *refs: edge_kernel(rows, *refs), out_shape=(cols, c...  2.66 us
    pallas_call x1, Pallas kernels, local(): pl.pallas_call(row_kernel, grid=(1,), out_shape=(edge, edge), in_specs=[f...  2.05 us
  transfers between devices with their start and end apart: 10, of which 5 were waited for; matrix products, arithmetic and copies ran while one was open for 3% of the time, Pallas kernels for 36%

profile of v2, /device:TPU:0, one launch (start us, length us, event | category | flops | bytes accessed | tf_op | source)
XLA Modules:
  0.0 81.7 jit_solution(3167145895997301544)
XLA Ops:
  0.6 2.1 %edge_rows.1 = (bf16[208,128]{1,0:T(8,128)(2,1)}, bf16[208,128]{1,0:T(8,128)(2,1)}) custom-call(bf16[48,64,128]{2,1,0:T(8,128)(2,1)} %refs_0_.2, bf16[48,64,128]{2,1,0:T(8,128)(2,1)} %refs_0_.2, bf16[48,64,128]{2,1,0:T(8,128)(2,1)} %refs_0_.3, bf16[48,64,128]{2,1,0:T(8,128)(2,1)} %refs_0_.3, bf16[64,128]{1,0:T(8,128)(2,1)} %refs_1_.3, s32[8,16]{1,0:T(8,128)} %refs_2_.3), custom_call_target="tpu_custom_call" | custom-call | tf_op jit(solution)/shard_map/edge_rows/pallas_call | solution.py:474
  3.1 0.7 collective-permute-start.1
  4.0 0.8 copy-done.15
  5.4 0.8 fusion.24
  6.2 0.6 copy-done.23
  8.3 2.8 %edge_cols.1 = (bf16[208,128]{1,0:T(8,128)(2,1)}, bf16[208,128]{1,0:T(8,128)(2,1)}, bf16[2,208,128]{2,1,0:T(8,128)(2,1)}, bf16[2,208,128]{2,1,0:T(8,128)(2,1)}) custom-call(bf16[48,64,128]{2,1,0:T(8,128)(2,1)} %refs_0_.2, bf16[48,64,128]{2,1,0:T(8,128)(2,1)} %refs_0_.3, bf16[64,128]{1,0:T(8,128)(2,1)} %refs_1_.3, s32[8,16]{1,0:T(8,128)} %refs_2_.3, ...), custom_call_target="tpu_custom_call" | custom-call | tf_op jit(solution)/shard_map/edge_cols/pallas_call | solution.py:494
  11.1 2.5 %collective-permute-start.2 = (bf16[208,128]{1,0:T(8,128)(2,1)}, bf16[208,128]{1,0:T(8,128)(2,1)S(1)}, u32[]{:S(2)}, u32[]{:S(2)}) collective-permute-start(bf16[208,128]{1,0:T(8,128)(2,1)} %get-tuple-element.27), channel_id=1, source_target_pairs={{0,1},{1,0},{2,3},{3,2},{4,5},{5,4},{6,7},{7,6},{8,9},{9,8},{10,11... | collective-permute-start | bytes 159752 | tf_op jit(solution)/shard_map/ppermute | solution.py:450
  13.7 1.3 %collective-permute-start.3 = (bf16[208,128]{1,0:T(8,128)(2,1)}, bf16[208,128]{1,0:T(8,128)(2,1)}, u32[]{:S(2)}, u32[]{:S(2)}) collective-permute-start(bf16[208,128]{1,0:T(8,128)(2,1)} %get-tuple-element.28), channel_id=1, source_target_pairs={{1,2},{2,1},{3,4},{4,3},{5,6},{6,5},{9,10},{10,9},{11,12},{12,11},... | collective-permute-start | bytes 159752 | tf_op jit(solution)/shard_map/ppermute | solution.py:450
  15.0 0.9 %copy-done.5 = bf16[144,720]{1,0:T(8,128)(2,1)S(1)} copy-done((bf16[144,720]{1,0:T(8,128)(2,1)S(1)}, bf16[144,720]{1,0:T(8,128)(2,1)}, u32[]{:S(2)}) %copy-start.5) | copy-done | bytes 207384
  15.9 0.9 %copy-done.12 = bf16[2,208,128]{2,1,0:T(8,128)(2,1)S(1)} copy-done((bf16[2,208,128]{2,1,0:T(8,128)(2,1)S(1)}, bf16[2,208,128]{2,1,0:T(8,128)(2,1)}, u32[]{:S(2)}) %copy-start.12) | copy-done | bytes 106520
  16.8 10.0 %hidden.1 = (bf16[3168,128]{1,0:T(8,128)(2,1)S(1)}, bf16[3168,128]{1,0:T(8,128)(2,1)S(1)}, f32[144,144]{1,0:T(8,128)S(1)}, f32[144,144]{1,0:T(8,128)S(1)}, f32[3,48,128]{2,1,0:T(8,128)S(1)}) custom-call(bf16[48,64,128]{2,1,0:T(8,128)(2,1)S(1)} %copy-done, bf16[48,64,128]{2,1,0:T(8,128)(2,1)S(1)} %copy-done.1, bf16[64,128]{1,0:T(8,128)(2,1)S(1)} %copy-done.4, ...), custom_call_target="tpu_custom_call" | custom-call | flops 2717908992 | bytes 8388608 | tf_op jit(solution)/shard_map/hidden/pallas_call | solution.py:507
  26.8 0.7 copy-done.6
  27.5 0.7 copy-done.7
  29.4 2.7 %edge_parts.1 = (bf16[48,512]{1,0:T(8,128)(2,1)}, bf16[48,512]{1,0:T(8,128)(2,1)}, f32[168,128]{1,0:T(8,128)}, f32[168,128]{1,0:T(8,128)}) custom-call(bf16[208,128]{1,0:T(8,128)(2,1)} %copy-done.21, bf16[208,128]{1,0:T(8,128)(2,1)} %collective-permute-done.3.refs_1_, bf16[2,208,128]{2,1,0:T(8,128)(2,1)} %get-tuple-element.29.refs_2_, ...), custom_call_target="tpu_custom_call" | custom-call | tf_op jit(solution)/shard_map/edge_parts/pallas_call | solution.py:526
  32.0 2.6 %collective-permute-start.4 = (f32[168,128]{1,0:T(8,128)}, f32[168,128]{1,0:T(8,128)S(1)}, u32[]{:S(2)}, u32[]{:S(2)}) collective-permute-start(f32[168,128]{1,0:T(8,128)} %get-tuple-element.37), channel_id=1, source_target_pairs={{0,8},{1,9},{2,10},{3,11},{4,12},{5,13},{6,14},{7,15},{8,0},{9,1},... | collective-permute-start | bytes 258056 | tf_op jit(solution)/shard_map/ppermute | solution.py:450
  34.7 1.1 %collective-permute-done.4 = f32[168,128]{1,0:T(8,128)S(1)} collective-permute-done((f32[168,128]{1,0:T(8,128)}, f32[168,128]{1,0:T(8,128)S(1)}, u32[]{:S(2)}, u32[]{:S(2)}) %collective-permute-start.4) | collective-permute-done | bytes 86048 | tf_op jit(solution)/shard_map/ppermute | solution.py:450
  35.8 0.9 %add.45 = f32[168,128]{1,0:T(8,128)S(1)} add(f32[168,128]{1,0:T(8,128)} %get-tuple-element.36, f32[168,128]{1,0:T(8,128)S(1)} %collective-permute-done.4) | non-fusion elementwise | flops 21504 | bytes 258048 | tf_op jit(solution)/shard_map/add | solution.py:552
  36.7 1.2 %collective-permute-start.5 = (f32[168,128]{1,0:T(8,128)S(1)}, f32[168,128]{1,0:T(8,128)S(1)}, u32[]{:S(2)}, u32[]{:S(2)}) collective-permute-start(f32[168,128]{1,0:T(8,128)S(1)} %add.45), channel_id=1, source_target_pairs={{0,16},{1,17},{2,18},{3,19},{4,20},{5,21},{6,22},{7,23},{8,24},{9,... | collective-permute-start | bytes 258056 | tf_op jit(solution)/shard_map/ppermute | solution.py:450
  37.9 3.6 %collective-permute-done.5 = f32[168,128]{1,0:T(8,128)S(1)} collective-permute-done((f32[168,128]{1,0:T(8,128)S(1)}, f32[168,128]{1,0:T(8,128)S(1)}, u32[]{:S(2)}, u32[]{:S(2)}) %collective-permute-start.5) | collective-permute-done | bytes 86048 | tf_op jit(solution)/shard_map/ppermute | solution.py:450
  41.6 0.6 add.46
  42.2 3.4 %collective-permute-start.6 = (f32[168,128]{1,0:T(8,128)}, f32[168,128]{1,0:T(8,128)}, u32[]{:S(2)}, u32[]{:S(2)}) collective-permute-start(f32[168,128]{1,0:T(8,128)} %add.46), channel_id=1, source_target_pairs={{0,1},{1,0},{2,3},{3,2},{4,5},{5,4},{6,7},{7,6},{8,9},{9,8},{10,11... | collective-permute-start | bytes 258056 | tf_op jit(solution)/shard_map/ppermute | solution.py:450
  45.6 1.0 %copy.31 = bf16[48,3,3,48]{3,2,1,0:T(4,128)(2,1)S(1)} copy(bf16[48,3,3,48]{3,0,2,1:T(8,128)(2,1)} %bitcast.14) | data formatting | bytes 82944 | tf_op jit(solution)/shard_map/transpose | solution.py:487
  46.8 1.6 %collective-permute-done.6 = f32[168,128]{1,0:T(8,128)} collective-permute-done((f32[168,128]{1,0:T(8,128)}, f32[168,128]{1,0:T(8,128)}, u32[]{:S(2)}, u32[]{:S(2)}) %collective-permute-start.6) | collective-permute-done | bytes 86048 | tf_op jit(solution)/shard_map/ppermute | solution.py:450
  48.4 0.9 %add.47 = f32[168,128]{1,0:T(8,128)S(1)} add(f32[168,128]{1,0:T(8,128)} %add.46, f32[168,128]{1,0:T(8,128)} %collective-permute-done.6) | non-fusion elementwise | flops 21504 | bytes 258048 | tf_op jit(solution)/shard_map/add | solution.py:556
  49.3 1.6 %collective-permute-start.7 = (f32[168,128]{1,0:T(8,128)S(1)}, f32[168,128]{1,0:T(8,128)S(1)}, u32[]{:S(2)}, u32[]{:S(2)}) collective-permute-start(f32[168,128]{1,0:T(8,128)S(1)} %add.47), channel_id=1, source_target_pairs={{0,2},{1,3},{2,0},{3,1},{4,6},{5,7},{6,4},{7,5},{8,10},{9,11},{10,... | collective-permute-start | bytes 258056 | tf_op jit(solution)/shard_map/ppermute | solution.py:450
  51.1 2.8 %collective-permute-done.7 = f32[168,128]{1,0:T(8,128)S(1)} collective-permute-done((f32[168,128]{1,0:T(8,128)S(1)}, f32[168,128]{1,0:T(8,128)S(1)}, u32[]{:S(2)}, u32[]{:S(2)}) %collective-permute-start.7) | collective-permute-done | bytes 86048 | tf_op jit(solution)/shard_map/ppermute | solution.py:450
  53.9 2.7 %collective-permute-start.8 = (f32[168,128]{1,0:T(8,128)S(1)}, f32[168,128]{1,0:T(8,128)S(1)}, u32[]{:S(2)}, u32[]{:S(2)}) collective-permute-start(f32[168,128]{1,0:T(8,128)S(1)} %add.48), channel_id=1, source_target_pairs={{0,4},{1,5},{2,6},{3,7},{4,0},{5,1},{6,2},{7,3},{8,12},{9,13},{10,... | collective-permute-start | bytes 258056 | tf_op jit(solution)/shard_map/ppermute | solution.py:450
  56.7 2.7 %collective-permute-done.8 = f32[168,128]{1,0:T(8,128)S(1)} collective-permute-done((f32[168,128]{1,0:T(8,128)S(1)}, f32[168,128]{1,0:T(8,128)S(1)}, u32[]{:S(2)}, u32[]{:S(2)}) %collective-permute-start.8) | collective-permute-done | bytes 86048 | tf_op jit(solution)/shard_map/ppermute | solution.py:450
  59.5 9.8 %delensed.1 = bf16[48,64,128]{2,1,0:T(8,128)(2,1)} custom-call(bf16[48,64,128]{2,1,0:T(8,128)(2,1)S(1)} %copy-done, bf16[64,128]{1,0:T(8,128)(2,1)S(1)} %copy-done.4, s32[8,16]{1,0:T(8,128)S(1)} %copy-done.9, bf16[3168,128]{1,0:T(8,128)(2,1)S(1)} %get-tuple-element.26.refs_3_, bf16[48,512]{1,0:T(8,128)(2,1)S(1)} %copy-done.11, ...), custom_call_target="tpu_custom_call" | custom-call | flops 679477248 | bytes 4194304 | tf_op jit(solution)/shard_map/delensed/pallas_call | solution.py:534
  69.3 9.8 %grad_input.1 = bf16[48,64,128]{2,1,0:T(8,128)(2,1)} custom-call(bf16[48,64,128]{2,1,0:T(8,128)(2,1)S(1)} %copy-done.1, bf16[64,128]{1,0:T(8,128)(2,1)S(1)} %copy-done.4, s32[8,16]{1,0:T(8,128)S(1)} %copy-done.9, bf16[3168,128]{1,0:T(8,128)(2,1)S(1)} %get-tuple-element.34.refs_3_, bf16[48,512]{1,0:T(8,128)(2,1)S(1)} %copy-done.10, ...), custom_call_target="tpu_custom_call" | custom-call | flops 679477248 | bytes 4194304 | tf_op jit(solution)/shard_map/grad_input/pallas_call | solution.py:534
  79.1 0.6 copy-done.19
  79.8 2.0 %unpack.1 = (f32[3,3,48,48]{3,2,1,0:T(8,128)}, f32[3,3,48,48]{3,2,1,0:T(8,128)}, f32[3,48]{1,0:T(4,128)}) custom-call(f32[168,128]{1,0:T(8,128)} %copy-done.18, f32[168,128]{1,0:T(8,128)} %copy-done.19), custom_call_target="tpu_custom_call" | custom-call | tf_op jit(solution)/shard_map/unpack/pallas_call | solution.py:561
  (66 shorter events, 4.5 us)
Async XLA Ops:
  0.6 3.2 %copy-start.13 = (bf16[3,3,48,48]{3,2,1,0:T(8,128)(2,1)S(1)}, bf16[3,3,48,48]{3,2,1,0:T(8,128)(2,1)}, u32[]{:S(2)}) copy-start(bf16[3,3,48,48]{3,2,1,0:T(8,128)(2,1)} %param.13) | copy-start | bytes 124420
  2.7 4.4 %collective-permute-start = (bf16[208,128]{1,0:T(8,128)(2,1)}, bf16[208,128]{1,0:T(8,128)(2,1)S(1)}, u32[]{:S(2)}, u32[]{:S(2)}) collective-permute-start(bf16[208,128]{1,0:T(8,128)(2,1)} %get-tuple-element.23), channel_id=1, source_target_pairs={{0,8},{1,9},{2,10},{3,11},{4,12},{5,13},{6,14},{7,15},{8,0},{9,1},... | collective-permute-start | bytes 159752 | tf_op jit(solution)/shard_map/ppermute | solution.py:450
  3.1 3.9 %collective-permute-start.1 = (bf16[208,128]{1,0:T(8,128)(2,1)}, bf16[208,128]{1,0:T(8,128)(2,1)S(1)}, u32[]{:S(2)}, u32[]{:S(2)}) collective-permute-start(bf16[208,128]{1,0:T(8,128)(2,1)} %get-tuple-element.24), channel_id=1, source_target_pairs={{8,16},{9,17},{10,18},{11,19},{12,20},{13,21},{14,22},{15,23},{16,... | collective-permute-start | bytes 159752 | tf_op jit(solution)/shard_map/ppermute | solution.py:450
  3.9 0.9 %copy-start.15 = (bf16[3,3,48,48]{3,2,1,0:T(8,128)(2,1)S(1)}, bf16[3,3,48,48]{3,2,1,0:T(8,128)(2,1)}, u32[]{:S(2)}) copy-start(bf16[3,3,48,48]{3,2,1,0:T(8,128)(2,1)} %param.14) | copy-start | bytes 124420
  5.4 0.8 copy-start.17
  6.2 0.7 copy-start.23
  6.2 0.7 copy-start.24
  6.2 0.7 copy-start.25
  7.0 7.9 %copy-start.2 = (f32[48,128]{1,0:T(8,128)}, f32[48,128]{1,0:T(8,128)S(1)}, u32[]{:S(2)}) copy-start(f32[48,128]{1,0:T(8,128)S(1)} %pad.59.cond_ref.refs_5_.refs_6_) | copy-start | bytes 73732
  7.0 7.9 %copy-start = (bf16[48,64,128]{2,1,0:T(8,128)(2,1)S(1)}, bf16[48,64,128]{2,1,0:T(8,128)(2,1)}, u32[]{:S(2)}) copy-start(bf16[48,64,128]{2,1,0:T(8,128)(2,1)} %refs_0_.2) | copy-start | bytes 2359300
  7.0 7.9 %copy-start.1 = (bf16[48,64,128]{2,1,0:T(8,128)(2,1)S(1)}, bf16[48,64,128]{2,1,0:T(8,128)(2,1)}, u32[]{:S(2)}) copy-start(bf16[48,64,128]{2,1,0:T(8,128)(2,1)} %refs_0_.3) | copy-start | bytes 2359300
  7.0 7.9 %copy-start.4 = (bf16[64,128]{1,0:T(8,128)(2,1)S(1)}, bf16[64,128]{1,0:T(8,128)(2,1)}, u32[]{:S(2)}) copy-start(bf16[64,128]{1,0:T(8,128)(2,1)} %refs_1_.3) | copy-start | bytes 49156
  11.1 3.8 %copy-start.9 = (s32[8,16]{1,0:T(8,128)S(1)}, s32[8,16]{1,0:T(8,128)}, u32[]{:S(2)}) copy-start(s32[8,16]{1,0:T(8,128)} %refs_2_.3) | copy-start | bytes 1540
  11.1 17.6 %collective-permute-start.2 = (bf16[208,128]{1,0:T(8,128)(2,1)}, bf16[208,128]{1,0:T(8,128)(2,1)S(1)}, u32[]{:S(2)}, u32[]{:S(2)}) collective-permute-start(bf16[208,128]{1,0:T(8,128)(2,1)} %get-tuple-element.27), channel_id=1, source_target_pairs={{0,1},{1,0},{2,3},{3,2},{4,5},{5,4},{6,7},{7,6},{8,9},{9,8},{10,11... | collective-permute-start | bytes 159752 | tf_op jit(solution)/shard_map/ppermute | solution.py:450
  13.7 15.1 %collective-permute-start.3 = (bf16[208,128]{1,0:T(8,128)(2,1)}, bf16[208,128]{1,0:T(8,128)(2,1)}, u32[]{:S(2)}, u32[]{:S(2)}) collective-permute-start(bf16[208,128]{1,0:T(8,128)(2,1)} %get-tuple-element.28), channel_id=1, source_target_pairs={{1,2},{2,1},{3,4},{4,3},{5,6},{6,5},{9,10},{10,9},{11,12},{12,11},... | collective-permute-start | bytes 159752 | tf_op jit(solution)/shard_map/ppermute | solution.py:450
  15.0 0.9 %copy-start.5 = (bf16[144,720]{1,0:T(8,128)(2,1)S(1)}, bf16[144,720]{1,0:T(8,128)(2,1)}, u32[]{:S(2)}) copy-start(bf16[144,720]{1,0:T(8,128)(2,1)} %get-tuple-element.42.w2ts_ref) | copy-start | bytes 622084
  15.9 0.9 %copy-start.12 = (bf16[2,208,128]{2,1,0:T(8,128)(2,1)S(1)}, bf16[2,208,128]{2,1,0:T(8,128)(2,1)}, u32[]{:S(2)}) copy-start(bf16[2,208,128]{2,1,0:T(8,128)(2,1)} %get-tuple-element.25.halo_ref) | copy-start | bytes 319492
  26.8 0.7 copy-start.6
  27.5 0.7 copy-start.7
  28.1 0.6 copy-start.8
  32.0 3.7 %collective-permute-start.4 = (f32[168,128]{1,0:T(8,128)}, f32[168,128]{1,0:T(8,128)S(1)}, u32[]{:S(2)}, u32[]{:S(2)}) collective-permute-start(f32[168,128]{1,0:T(8,128)} %get-tuple-element.37), channel_id=1, source_target_pairs={{0,8},{1,9},{2,10},{3,11},{4,12},{5,13},{6,14},{7,15},{8,0},{9,1},... | collective-permute-start | bytes 258056 | tf_op jit(solution)/shard_map/ppermute | solution.py:450
  36.7 8.9 %copy-start.14 = (bf16[3,3,48,48]{3,2,1,0:T(8,128)(2,1)S(1)}, bf16[3,3,48,48]{3,2,1,0:T(8,128)(2,1)}, u32[]{:S(2)}) copy-start(bf16[3,3,48,48]{3,2,1,0:T(8,128)(2,1)} %param.13) | copy-start | bytes 124420
  36.7 4.9 %collective-permute-start.5 = (f32[168,128]{1,0:T(8,128)S(1)}, f32[168,128]{1,0:T(8,128)S(1)}, u32[]{:S(2)}, u32[]{:S(2)}) collective-permute-start(f32[168,128]{1,0:T(8,128)S(1)} %add.45), channel_id=1, source_target_pairs={{0,16},{1,17},{2,18},{3,19},{4,20},{5,21},{6,22},{7,23},{8,24},{9,... | collective-permute-start | bytes 258056 | tf_op jit(solution)/shard_map/ppermute | solution.py:450
  42.2 6.2 %collective-permute-start.6 = (f32[168,128]{1,0:T(8,128)}, f32[168,128]{1,0:T(8,128)}, u32[]{:S(2)}, u32[]{:S(2)}) collective-permute-start(f32[168,128]{1,0:T(8,128)} %add.46), channel_id=1, source_target_pairs={{0,1},{1,0},{2,3},{3,2},{4,5},{5,4},{6,7},{7,6},{8,9},{9,8},{10,11... | collective-permute-start | bytes 258056 | tf_op jit(solution)/shard_map/ppermute | solution.py:450
  49.3 4.6 %collective-permute-start.7 = (f32[168,128]{1,0:T(8,128)S(1)}, f32[168,128]{1,0:T(8,128)S(1)}, u32[]{:S(2)}, u32[]{:S(2)}) collective-permute-start(f32[168,128]{1,0:T(8,128)S(1)} %add.47), channel_id=1, source_target_pairs={{0,2},{1,3},{2,0},{3,1},{4,6},{5,7},{6,4},{7,5},{8,10},{9,11},{10,... | collective-permute-start | bytes 258056 | tf_op jit(solution)/shard_map/ppermute | solution.py:450
  53.9 5.4 %collective-permute-start.8 = (f32[168,128]{1,0:T(8,128)S(1)}, f32[168,128]{1,0:T(8,128)S(1)}, u32[]{:S(2)}, u32[]{:S(2)}) collective-permute-start(f32[168,128]{1,0:T(8,128)S(1)} %add.48), channel_id=1, source_target_pairs={{0,4},{1,5},{2,6},{3,7},{4,0},{5,1},{6,2},{7,3},{8,12},{9,13},{10,... | collective-permute-start | bytes 258056 | tf_op jit(solution)/shard_map/ppermute | solution.py:450
  56.7 2.8 %copy-start.3 = (f32[48,128]{1,0:T(8,128)S(1)}, f32[48,128]{1,0:T(8,128)}, u32[]{:S(2)}) copy-start(f32[48,128]{1,0:T(8,128)} %copy-done.2) | copy-start | bytes 73732
  56.7 2.8 %copy-start.11 = (bf16[48,512]{1,0:T(8,128)(2,1)S(1)}, bf16[48,512]{1,0:T(8,128)(2,1)}, u32[]{:S(2)}) copy-start(bf16[48,512]{1,0:T(8,128)(2,1)} %get-tuple-element.33.refs_4_) | copy-start | bytes 147460
  59.4 9.9 %copy-start.18 = (f32[168,128]{1,0:T(8,128)}, f32[168,128]{1,0:T(8,128)S(1)}, u32[]{:S(2)}) copy-start(f32[168,128]{1,0:T(8,128)S(1)} %add.49.refs_0_) | copy-start | bytes 258052
  59.4 19.7 %collective-permute-start.9 = (f32[168,128]{1,0:T(8,128)S(1)}, f32[168,128]{1,0:T(8,128)S(1)}, u32[]{:S(2)}, u32[]{:S(2)}) collective-permute-start(f32[168,128]{1,0:T(8,128)S(1)} %add.49.refs_0_), channel_id=1, source_target_pairs={{0,8},{1,9},{2,10},{3,11},{4,12},{5,13},{6,14},{7,15},{8,0},{9,1},... | collective-permute-start | bytes 258056 | tf_op jit(solution)/shard_map/ppermute | solution.py:450
  59.5 9.8 %copy-start.10 = (bf16[48,512]{1,0:T(8,128)(2,1)S(1)}, bf16[48,512]{1,0:T(8,128)(2,1)}, u32[]{:S(2)}) copy-start(bf16[48,512]{1,0:T(8,128)(2,1)} %get-tuple-element.35.refs_4_) | copy-start | bytes 147460
  79.1 0.6 copy-start.19
  (4 other events, 2.5 us)

commit v3 on v2

--- a/solution.py
+++ b/solution.py
@@ -10,6 +10,7 @@
 F32 = jnp.float32
 NT = (((1,), (1,)), ((), ()))
 NN = (((1,), (0,)), ((), ()))
+TN = (((0,), (0,)), ((), ()))
 R1 = 3
 R2 = 4
 GROUP1 = 6
@@ -135,9 +136,7 @@
 
 
 def two_windows(src, first, second, size):
-    a = pl.multiple_of(first, 16)
-    b = pl.multiple_of(second, 16)
-    return jnp.concatenate([src[pl.ds(a, size), :], src[pl.ds(b, size), :]], axis=1)
+    return jnp.concatenate([src[first : first + size], src[second : second + size]], axis=1)
 
 
 def hidden_kernel(
@@ -194,7 +193,7 @@
     for y in (-2, -1, rows, rows + 1):
         dz[(y + 2) * chans : (y + 3) * chans] = zero
 
-    def first_pass(it, carry):
+    def first_pass(it, dphi, dsum):
         y0 = R1 * it - 1
         win = (R1 + 2) * step
         at = ((y0 + 1) * step, (y0 + split + 1) * step)
@@ -208,23 +207,23 @@
             for r in range(R1):
                 row = y0 + h * split + r + 1
                 here = (slice(r * chans, (r + 1) * chans), slice(h * 128, h * 128 + 128))
-                keep = maskx[pl.ds(row, 1), :]
-                act, slope = silu_parts(pre[here] + gain * phix[pl.ds(row, 1), :] + bias)
-                base = pl.multiple_of(row * chans, 16)
-                hid_ref[pl.ds(base, chans), :] = (act * keep).astype(BF)
-                dpre_ref[pl.ds(base, chans), :] = (back[here] * keep * slope).astype(BF)
-        return carry
-
-    lax.fori_loop(0, split // R1, first_pass, 0)
+                keep = maskx[row : row + 1]
+                act, slope = silu_parts(pre[here] + gain * phix[row : row + 1] + bias)
+                base = row * chans
+                hid_ref[base : base + chans] = (act * keep).astype(BF)
+                value = (back[here] * keep * slope).astype(BF)
+                dpre_ref[base : base + chans] = value
+                if 1 <= row <= rows:
+                    dz[base + chans : base + 2 * chans] = value
+                    wide = value.astype(F32)
+                    dphi = dphi + wide * phix[row : row + 1]
+                    dsum = dsum + wide
+        return dphi, dsum
 
     dphi = jnp.zeros((chans, 128), F32)
     dsum = jnp.zeros((chans, 128), F32)
-    for y in range(rows):
-        value = dpre_ref[(y + 1) * chans : (y + 2) * chans]
-        dz[(y + 2) * chans : (y + 3) * chans] = value
-        wide = value.astype(F32)
-        dphi = dphi + wide * phix[y + 1 : y + 2]
-        dsum = dsum + wide
+    for it in range(split // R1):
+        dphi, dsum = first_pass(it, dphi, dsum)
     cacc[0] = dphi
     cacc[1] = dsum
 
@@ -232,33 +231,34 @@
     acc2[...] = jnp.zeros_like(acc2)
 
     def rows_of(src, start, size):
-        return src[pl.ds(pl.multiple_of(start, 16), size), :]
-
-    def grads_one(it, carry):
+        return src[start : start + size]
+
+    def grads_one(it):
         ys = [GROUP1 * it + n - 1 for n in range(GROUP1)]
         acc1[...] += lax.dot_general(
             jnp.concatenate([rows_of(dz, (y + 1) * chans, step) for y in ys], axis=1),
             jnp.concatenate([rows_of(a3x, (y + 2) * step, step) for y in ys], axis=1),
             NT, preferred_element_type=F32,
         )
-        return carry
-
-    def grads_two(it, carry):
+
+    def grads_two(it):
         ys = [GROUP2 * it + n for n in range(GROUP2)]
         acc2[...] += lax.dot_general(
             jnp.concatenate([rows_of(a3g, (y + 2) * step, step) for y in ys], axis=1),
             jnp.concatenate([rows_of(hid_ref, y * chans, step) for y in ys], axis=1),
             NT, preferred_element_type=F32,
         )
-        return carry
-
-    lax.fori_loop(0, (rows + 2) // GROUP1, grads_one, 0)
-    lax.fori_loop(0, rows // GROUP2, grads_two, 0)
+
+    for it in range((rows + 2) // GROUP1):
+        grads_one(it)
+    for it in range(rows // GROUP2):
+        grads_two(it)
 
 
 def edge_kernel(
-    rows, a_ref, b_ref, own_ref, w1c_ref, w2tc_ref, cond_ref, acc1, acc2, cacc,
-    hcol_ref, dcol_ref, keep_ref, give_ref, wire,
+    rows, a_ref, b_ref, own_ref, w1c_ref, w2tc_ref, w2c_ref, w1tc_ref, cond_ref,
+    acc1, acc2, cacc,
+    hfix_ref, dfix_ref, keep_ref, give_ref, wire,
 ):
     size = a_ref.shape[0]
     chans = (size - 16) // 4
@@ -296,8 +296,6 @@
     act, slope = silu_parts(pre + cond_ref[:, 0:1] * phi_c + cond_ref[:, 1:2])
     hcol = (act * mask_c).astype(BF)
     dcol = (back * mask_c * slope).astype(BF)
-    hcol_ref[...] = hcol
-    dcol_ref[...] = dcol
 
     mine = jnp.broadcast_to((lane_iota(1) < rows).astype(F32), (chans, 128)).astype(BF)
     d_own = [dcol[:, 128:256] * mine, dcol[:, 256:384] * mine]
@@ -342,6 +340,27 @@
     sums = [jnp.sum(v, axis=1, keepdims=True) for v in (dphi, dsum, cacc[2])]
     fill = jnp.zeros((chans, 128 - 3 * tails[0].shape[1] - 3), F32)
     wire[2 * step : 2 * step + chans] = jnp.concatenate(tails + sums + [fill], axis=1)
+    none = jnp.zeros((chans, 128), BF)
+    half = chans // 2
+    lane = lane_iota(half)
+    for weights, field, fix in ((w2c_ref, hcol, hfix_ref), (w1tc_ref, dcol, dfix_ref)):
+        f = [field[:, 128 * k : 128 * k + 128] for k in range(4)]
+        pieces = []
+        for ky in range(3):
+            m = [c if ky == 1 else pltpu.roll(c, (1, 0, 127)[ky], 1) for c in f]
+            pieces.append(jnp.concatenate([m[0], m[1], none, none], axis=1))
+            pieces.append(jnp.concatenate([m[1], none, none, m[2]], axis=1))
+            pieces.append(jnp.concatenate([none, none, m[2], m[3]], axis=1))
+        fixes = lax.dot_general(
+            weights[...], jnp.concatenate(pieces, axis=0), NN, preferred_element_type=F32
+        )
+        for k in range(4):
+            col = fixes[:, 128 * k : 128 * k + 128]
+            part = jnp.where(lane < rows, col[:half], pltpu.roll(col[half:], rows, 1))
+            high = part.astype(BF).astype(F32)
+            fix[pl.ds(k, half, stride=8), :] = high
+            fix[pl.ds(4 + k, half, stride=8), :] = part - high
+
     count = wire.shape[0] // 2
     core = lax.rem(lax.axis_index("gy"), 2)
     keep_ref[...] = wire[pl.ds(pl.multiple_of(core * count, 8), count), :]
@@ -349,36 +368,34 @@
 
 
 def output_kernel(
-    with_phi, src_ref, phi_ref, mask_ref, mid_ref, col_ref, weights_ref, cond_ref,
-    out_ref, a3, rowbuf, phix,
+    with_phi, src_ref, phi_ref, mask_ref, mid_ref, fix_ref, weights_ref, cond_ref,
+    out_ref, a3, rowbuf, fixbuf,
 ):
     chans, rows, width = src_ref.shape
     step = 3 * chans
-    lane = lane_iota(chans)
+    half = chans // 2
     cells = tile_rows(mask_ref)
-    cols = [col_ref[:, 128 * k : 128 * k + 128] for k in range(4)]
     if with_phi:
-        phix[...] = phi_ref[...].astype(F32)
+        phi = phi_ref[...].astype(F32)
         gain = cond_ref[:, 2:3]
-
-    def cell(col, y):
-        at = y % 128
-        return jnp.broadcast_to(col[:, at : at + 1], (chans, 128))
-
-    for y in range(-1, rows + 1):
-        centre = mid_ref[(y + 1) * chans : (y + 2) * chans]
-        centre = jnp.where(lane == 0, cell(cols[1], y), centre)
-        centre = jnp.where(lane == 127, cell(cols[2], y), centre)
-        base = (y + 1) * step
-        a3[base : base + chans] = jnp.where(
-            lane == 0, cell(cols[0], y), pltpu.roll(centre, 1, 1)
-        )
+    lane8 = lane_iota(8)
+    row8 = lax.rem(lax.broadcasted_iota(jnp.int32, (8, 128), 0), 4)
+    place = (lane8 == jnp.where(row8 < 2, row8, row8 + (width - 4))).astype(F32).astype(BF)
+    for j in range(half):
+        got = lax.dot_general(
+            fix_ref[8 * j : 8 * j + 8].astype(BF), place, TN, preferred_element_type=F32
+        )
+        fixbuf[j] = got[:rows]
+        fixbuf[j + half] = got[rows:]
+
+    for y in range(rows + 2):
+        centre = mid_ref[y * chans : (y + 1) * chans]
+        base = y * step
+        a3[base : base + chans] = pltpu.roll(centre, 1, 1)
         a3[base + chans : base + 2 * chans] = centre
-        a3[base + 2 * chans : base + 3 * chans] = jnp.where(
-            lane == 127, cell(cols[3], y), pltpu.roll(centre, 127, 1)
-        )
-
-    def second_pass(it, carry):
+        a3[base + 2 * chans : base + 3 * chans] = pltpu.roll(centre, 127, 1)
+
+    for it in range(rows // (2 * R2)):
         y0 = R2 * it
         got = lax.dot_general(
             weights_ref[...],
@@ -390,18 +407,17 @@
                 y = y0 + h * (rows // 2) + r
                 part = got[r * chans : (r + 1) * chans, h * 128 : h * 128 + 128]
                 if with_phi:
-                    part = part + gain * phix[pl.ds(y, 1), :]
+                    part = part + gain * phi[y : y + 1]
                 rowbuf[y] = part
-        return carry
-
-    lax.fori_loop(0, rows // (2 * R2), second_pass, 0)
+
     for j in range(rows // 16):
-        block = jnp.transpose(src_ref[:, 16 * j : 16 * j + 16, :], (1, 0, 2))
-        done = []
-        for n in range(16):
-            keep = cells[(16 * j + n) // TILE : (16 * j + n) // TILE + 1]
-            done.append(((rowbuf[16 * j + n] + block[n].astype(F32)) * keep).astype(BF))
-        out_ref[:, 16 * j : 16 * j + 16, :] = jnp.transpose(jnp.stack(done), (1, 0, 2))
+        here = slice(16 * j, 16 * j + 16)
+        keep = jnp.concatenate(
+            [jnp.broadcast_to(cells[2 * j + t : 2 * j + t + 1], (TILE, 128)) for t in range(2)],
+            axis=0,
+        )
+        total = jnp.transpose(rowbuf[here], (1, 0, 2)) + fixbuf[:, here, :]
+        out_ref[:, here, :] = ((total + src_ref[:, here, :].astype(F32)) * keep[None]).astype(BF)
 
 
 def unpack_kernel(factor, keep_ref, other_ref, w1_ref, w2_ref, cond_ref, wire):
@@ -429,6 +445,10 @@
     cond_ref[...] = jnp.transpose(tail)[3 * rest_w : 3 * rest_w + 3, :chans]
 
 
+def limit(mib):
+    return pltpu.CompilerParams(vmem_limit_bytes=mib << 20)
+
+
 def stacked(block, count, chans):
     step = 3 * chans
     return jnp.concatenate(
@@ -466,6 +486,7 @@
         chans, rows, width = sky.shape
         step = 3 * chans
         size = 4 * chans + 16
+        assert 2 * rows == 128 and width == 128
         edge = jax.ShapeDtypeStruct((size, 128), BF)
         edges = jax.ShapeDtypeStruct((2, size, 128), BF)
         vmem = pl.BlockSpec(memory_space=pltpu.VMEM)
@@ -477,6 +498,7 @@
             out_shape=(edge, edge),
             in_specs=[first, last, first, last, vmem, vmem],
             out_specs=(vmem, vmem),
+            compiler_params=limit(8),
             name="edge_rows",
         )(sky, sky, cotangent, cotangent, lens_phi, tile_mask)
         ra, rb = swap(ra, rb, 0)
@@ -495,6 +517,7 @@
             col_kernel,
             out_shape=(edge, edge, edges, edges),
             scratch_shapes=[pltpu.VMEM((8 * chans // 2, 128), F32)],
+            compiler_params=limit(8),
             name="edge_cols",
         )(sky, cotangent, lens_phi, tile_mask, ra, rb)
         ca, cb = swap(ca, cb, 1)
@@ -510,7 +533,7 @@
             scratch_shapes=[
                 field, field, pltpu.VMEM(((rows + 4) * chans, 128), BF), rowwise, rowwise,
             ],
-            compiler_params=pltpu.CompilerParams(vmem_limit_bytes=32 << 20),
+            compiler_params=limit(16),
             cost_estimate=pl.CostEstimate(
                 flops=8 * flops, bytes_accessed=8 << 20, transcendentals=0
             ),
@@ -520,40 +543,49 @@
             stacked(w1f, R1, chans), stacked(w2b, R1, chans), conds,
         )
 
-        cols = jax.ShapeDtypeStruct((chans, 512), BF)
+        fix = jax.ShapeDtypeStruct((4 * chans, 128), F32)
         count = (2 * step + chans) // 2
         wires = jax.ShapeDtypeStruct((count, 128), F32)
-        hcol, dcol, keep, give = pl.pallas_call(
+        hfix, dfix, keep, give = pl.pallas_call(
             lambda *refs: edge_kernel(rows, *refs),
-            out_shape=(cols, cols, wires, wires),
+            out_shape=(fix, fix, wires, wires),
             scratch_shapes=[pltpu.VMEM((2 * count, 128), F32)],
+            compiler_params=limit(8),
             name="edge_parts",
-        )(ca, cb, own, w1f, w2b, conds, acc1, acc2, cacc)
-
-        def output(with_phi, src, mid, col, weights, name):
+        )(ca, cb, own, w1f, w2b, w2f, w1b, conds, acc1, acc2, cacc)
+
+        def output(with_phi, src, mid, fix, weights, name):
             return pl.pallas_call(
                 lambda *refs: output_kernel(with_phi, *refs),
                 out_shape=jax.ShapeDtypeStruct(src.shape, BF),
                 scratch_shapes=[
                     pltpu.VMEM(((rows + 2) * step, 128), BF),
                     pltpu.VMEM((rows, chans, 128), F32),
-                    pltpu.VMEM((rows, 128), F32),
+                    pltpu.VMEM((chans, rows, 128), F32),
                 ],
-                compiler_params=pltpu.CompilerParams(vmem_limit_bytes=16 << 20),
+                compiler_params=limit(16),
                 cost_estimate=pl.CostEstimate(
                     flops=2 * flops, bytes_accessed=4 << 20, transcendentals=0
                 ),
                 name=name,
-            )(src, lens_phi, tile_mask, mid, col, weights, conds)
-
-        delensed = output(True, sky, hid, hcol, stacked(w2f, R2, chans), "delensed")
-        grad_input = output(False, cotangent, dpre, dcol, stacked(w1b, R2, chans), "grad_input")
-
+            )(src, lens_phi, tile_mask, mid, fix, weights, conds)
+
+        w2s, w1s = stacked(w2f, R2, chans), stacked(w1b, R2, chans)
+        moves = [lambda a, b, bit=1 << k: (a ^ bit, b) for k in range(1, ny.bit_length() - 1)]
+        moves += [lambda a, b, bit=1 << k: (a, b ^ bit) for k in range(nx.bit_length() - 1)]
         keep = keep + send(give, lambda a, b: (a ^ 1, b))
-        for bit in [1 << k for k in range(1, ny.bit_length() - 1)]:
-            keep = keep + send(keep, lambda a, b: (a ^ bit, b))
-        for bit in [1 << k for k in range(nx.bit_length() - 1)]:
-            keep = keep + send(keep, lambda a, b: (a, b ^ bit))
+        outs = []
+        for n, move in enumerate(moves):
+            if n == 0:
+                keep, hfix = lax.optimization_barrier((keep, hfix))
+                outs.append(output(True, sky, hid, hfix, w2s, "delensed"))
+            if n == 1:
+                keep, dfix = lax.optimization_barrier((keep, dfix))
+                outs.append(output(False, cotangent, dpre, dfix, w1s, "grad_input"))
+            keep = keep + send(keep, move)
+            if n < 2:
+                keep, outs[n] = lax.optimization_barrier((keep, outs[n]))
+        delensed, grad_input = outs
         other = send(keep, lambda a, b: (a ^ 1, b))
 
         factor = float(1.0 / (rows * ny * width * nx) ** 0.5)
@@ -562,6 +594,7 @@
             lambda *refs: unpack_kernel(factor, *refs),
             out_shape=(grads, grads, jax.ShapeDtypeStruct((3, chans), F32)),
             scratch_shapes=[pltpu.VMEM((2 * count, 128), F32)],
+            compiler_params=limit(8),
             name="unpack",
         )(keep, other)
         return delensed, grad_input, grad_w1, grad_w2, grad_cond

time: 82.7 us -> 45.6 us (0.55)
  Pallas kernels: 39.1 us -> 12.1 us
  local copies, waits for them, and re-layouts: 9.83 us -> 6.28 us
  other arithmetic: 3.55 us -> 0.42 us
  waiting for transfers between devices: 11.8 us -> 8.83 us
    pallas_call x2, Pallas kernels: 19.6 us -> 5.21 us  [output(): pl.pallas_call(lambda *refs: output_kernel(with_phi, *refs), out_shape=ja...]
    pallas_call x1, Pallas kernels: 9.99 us -> 4.04 us  [local(): pl.pallas_call(hidden_kernel, out_shape=(inner, inner, acc, acc, jax.Shap...]
    ppermute x10, waiting for transfers between devices: 11.8 us -> 8.83 us  [send(): return lax.ppermute(value, axes, pairs)]
    unnamed x52 -> x26, local copies, waits for them, and re-layouts: 8.25 us -> 5.61 us
    pallas_call x1, Pallas kernels: 2.83 us -> 0.76 us  [local(): pl.pallas_call(col_kernel, out_shape=(edge, edge, edges, edges), scratch_...]
    pallas_call x1, Pallas kernels: 2.05 us -> 0.19 us  [local(): pl.pallas_call(row_kernel, grid=(1,), out_shape=(edge, edge), in_specs=[f...]
    pallas_call x1, Pallas kernels: 2.66 us -> 0.86 us  [local(): pl.pallas_call(lambda *refs: edge_kernel(rows, *refs), out_shape=(fix, fi...]
    add x4, other arithmetic: 1.61 us -> 0.05 us  [local(): keep = keep + send(keep, move)]
  transfers between devices with their start and end apart: 10 -> 10, of which waited for: 5 -> 5; matrix products, arithmetic and copies ran while one was open for 3% -> 2% of each run, Pallas kernels for 36% -> 20%
where the time goes in v3:
time: 45.6 us; the launch traced here: 45.2 us
  starting transfers between devices  16.8 us (37%)
  Pallas kernels  12.1 us (27%)
  waiting for transfers between devices  8.83 us (19%)
  local copies, waits for them, and re-layouts  6.28 us (14%)
  between operations  0.85 us (2%)
    ppermute x10, starting transfers between devices, send(): return lax.ppermute(value, axes, pairs)  16.8 us
    ppermute x10, waiting for transfers between devices, send(): return lax.ppermute(value, axes, pairs)  8.83 us
    unnamed x26, local copies, waits for them, and re-layouts  5.61 us
    pallas_call x2, Pallas kernels, output(): pl.pallas_call(lambda *refs: output_kernel(with_phi, *refs), out_shape=ja...  5.21 us
    pallas_call x1, Pallas kernels, local(): pl.pallas_call(hidden_kernel, out_shape=(inner, inner, acc, acc, jax.Shap...  4.04 us
    pallas_call x1, Pallas kernels, local(): pl.pallas_call(lambda *refs: unpack_kernel(factor, *refs), out_shape=(gra...  1.04 us
  transfers between devices with their start and end apart: 10, of which 5 were waited for; matrix products, arithmetic and copies ran while one was open for 2% of the time, Pallas kernels for 20%

profile of v3, /device:TPU:0, one launch (start us, length us, event | category | flops | bytes accessed | tf_op | source)
XLA Modules:
  0.0 45.2 jit_solution(3836903858293713859)
XLA Ops:
  0.6 1.1 %copy-done = bf16[48,64,128]{2,1,0:T(8,128)(2,1)S(1)} copy-done((bf16[48,64,128]{2,1,0:T(8,128)(2,1)S(1)}, bf16[48,64,128]{2,1,0:T(8,128)(2,1)}, u32[]{:S(2)}) %copy-start) | copy-done | bytes 786456
  1.8 1.1 %copy-done.2 = bf16[48,64,128]{2,1,0:T(8,128)(2,1)S(1)} copy-done((bf16[48,64,128]{2,1,0:T(8,128)(2,1)S(1)}, bf16[48,64,128]{2,1,0:T(8,128)(2,1)}, u32[]{:S(2)}) %copy-start.2) | copy-done | bytes 786456
  2.9 0.7 %copy-done.4 = bf16[64,128]{1,0:T(8,128)(2,1)S(1)} copy-done((bf16[64,128]{1,0:T(8,128)(2,1)S(1)}, bf16[64,128]{1,0:T(8,128)(2,1)}, u32[]{:S(2)}) %copy-start.4) | copy-done | bytes 16408
  3.6 0.7 %copy-done.6 = s32[8,16]{1,0:T(8,128)S(1)} copy-done((s32[8,16]{1,0:T(8,128)S(1)}, s32[8,16]{1,0:T(8,128)}, u32[]{:S(2)}) %copy-start.6) | copy-done | bytes 536
  4.3 0.2 edge_rows.1
  4.5 0.5 %collective-permute-start = (bf16[208,128]{1,0:T(8,128)(2,1)S(1)}, bf16[208,128]{1,0:T(8,128)(2,1)S(1)}, u32[]{:S(2)}, u32[]{:S(2)}) collective-permute-start(bf16[208,128]{1,0:T(8,128)(2,1)S(1)} %get-tuple-element.31), channel_id=1, source_target_pairs={{0,8},{1,9},{2,10},{3,11},{4,12},{5,13},{6,14},{7,15},{8,0},{9,1},... | collective-permute-start | bytes 159752 | tf_op jit(solution)/shard_map/ppermute | solution.py:470
  5.0 0.7 %collective-permute-start.1 = (bf16[208,128]{1,0:T(8,128)(2,1)S(1)}, bf16[208,128]{1,0:T(8,128)(2,1)S(1)}, u32[]{:S(2)}, u32[]{:S(2)}) collective-permute-start(bf16[208,128]{1,0:T(8,128)(2,1)S(1)} %get-tuple-element.32), channel_id=1, source_target_pairs={{8,16},{9,17},{10,18},{11,19},{12,20},{13,21},{14,22},{15,23},{16,... | collective-permute-start | bytes 159752 | tf_op jit(solution)/shard_map/ppermute | solution.py:470
  5.8 0.1 reshape.22.refs_3_
  5.9 0.8 %copy-done.9 = bf16[3,3,48,48]{3,2,1,0:T(8,128)(2,1)S(1)} copy-done((bf16[3,3,48,48]{3,2,1,0:T(8,128)(2,1)S(1)}, bf16[3,3,48,48]{3,2,1,0:T(8,128)(2,1)}, u32[]{:S(2)}) %copy-start.9) | copy-done | bytes 41496
  6.8 0.1 fusion.24
  6.9 0.4 copy-done.10
  7.4 0.1 reshape.24.refs_5_
  7.8 0.2 copy-done.3
  8.1 0.5 %copy-done.5 = bf16[64,128]{1,0:T(8,128)(2,1)S(1)} copy-done((bf16[64,128]{1,0:T(8,128)(2,1)S(1)}, bf16[64,128]{1,0:T(8,128)(2,1)}, u32[]{:S(2)}) %copy-start.5) | copy-done | bytes 16408
  8.6 0.8 %edge_cols.1 = (bf16[208,128]{1,0:T(8,128)(2,1)S(1)}, bf16[208,128]{1,0:T(8,128)(2,1)S(1)}, bf16[2,208,128]{2,1,0:T(8,128)(2,1)S(1)}, bf16[2,208,128]{2,1,0:T(8,128)(2,1)S(1)}) custom-call(bf16[48,64,128]{2,1,0:T(8,128)(2,1)S(1)} %copy-done.1, bf16[48,64,128]{2,1,0:T(8,128)(2,1)S(1)} %copy-done.3, bf16[64,128]{1,0:T(8,128)(2,1)S(1)} %copy-done.5, ...), custom_call_target="tpu_custom_call" | custom-call | tf_op jit(solution)/shard_map/edge_cols/pallas_call | solution.py:516
  9.3 2.6 %collective-permute-start.2 = (bf16[208,128]{1,0:T(8,128)(2,1)S(1)}, bf16[208,128]{1,0:T(8,128)(2,1)S(1)}, u32[]{:S(2)}, u32[]{:S(2)}) collective-permute-start(bf16[208,128]{1,0:T(8,128)(2,1)S(1)} %get-tuple-element.33), channel_id=1, source_target_pairs={{0,1},{1,0},{2,3},{3,2},{4,5},{5,4},{6,7},{7,6},{8,9},{9,8},{10,11... | collective-permute-start | bytes 159752 | tf_op jit(solution)/shard_map/ppermute | solution.py:470
  11.9 0.7 %collective-permute-start.3 = (bf16[208,128]{1,0:T(8,128)(2,1)S(1)}, bf16[208,128]{1,0:T(8,128)(2,1)S(1)}, u32[]{:S(2)}, u32[]{:S(2)}) collective-permute-start(bf16[208,128]{1,0:T(8,128)(2,1)S(1)} %get-tuple-element.34), channel_id=1, source_target_pairs={{1,2},{2,1},{3,4},{4,3},{5,6},{6,5},{9,10},{10,9},{11,12},{12,11},... | collective-permute-start | bytes 159752 | tf_op jit(solution)/shard_map/ppermute | solution.py:470
  12.6 4.0 %hidden.1 = (bf16[3168,128]{1,0:T(8,128)(2,1)S(1)}, bf16[3168,128]{1,0:T(8,128)(2,1)S(1)}, f32[144,144]{1,0:T(8,128)S(1)}, f32[144,144]{1,0:T(8,128)S(1)}, f32[3,48,128]{2,1,0:T(8,128)S(1)}) custom-call(bf16[48,64,128]{2,1,0:T(8,128)(2,1)S(1)} %copy-done.1, bf16[48,64,128]{2,1,0:T(8,128)(2,1)S(1)} %copy-done.3, bf16[64,128]{1,0:T(8,128)(2,1)S(1)} %copy-done.5, ...), custom_call_target="tpu_custom_call" | custom-call | flops 2717908992 | bytes 8388608 | tf_op jit(solution)/shard_map/hidden/pallas_call | solution.py:530
  16.7 0.9 %edge_parts.1 = (f32[192,128]{1,0:T(8,128)S(1)}, f32[192,128]{1,0:T(8,128)S(1)}, f32[168,128]{1,0:T(8,128)S(1)}, f32[168,128]{1,0:T(8,128)S(1)}) custom-call(bf16[208,128]{1,0:T(8,128)(2,1)S(1)} %collective-permute-done.2.refs_0_, bf16[208,128]{1,0:T(8,128)(2,1)S(1)} %collective-permute-done.3.refs_1_, bf16[2,208,128]{2,1,0:T(8,128)(2,1)S(1)} %get-tuple-element.35.refs_2_, ...), custom_call_target="tpu_custom_call" | custom-call | tf_op jit(solution)/shard_map/edge_parts/pallas_call | solution.py:549
  17.5 2.6 %collective-permute-start.4 = (f32[168,128]{1,0:T(8,128)S(1)}, f32[168,128]{1,0:T(8,128)S(1)}, u32[]{:S(2)}, u32[]{:S(2)}) collective-permute-start(f32[168,128]{1,0:T(8,128)S(1)} %get-tuple-element.41), channel_id=1, source_target_pairs={{0,8},{1,9},{2,10},{3,11},{4,12},{5,13},{6,14},{7,15},{8,0},{9,1},... | collective-permute-start | bytes 258056 | tf_op jit(solution)/shard_map/ppermute | solution.py:470
  20.2 0.9 %collective-permute-done.4 = f32[168,128]{1,0:T(8,128)S(1)} collective-permute-done((f32[168,128]{1,0:T(8,128)S(1)}, f32[168,128]{1,0:T(8,128)S(1)}, u32[]{:S(2)}, u32[]{:S(2)}) %collective-permute-start.4) | collective-permute-done | bytes 86048 | tf_op jit(solution)/shard_map/ppermute | solution.py:470
  21.1 1.3 %collective-permute-start.5 = (f32[168,128]{1,0:T(8,128)S(1)}, f32[168,128]{1,0:T(8,128)S(1)}, u32[]{:S(2)}, u32[]{:S(2)}) collective-permute-start(f32[168,128]{1,0:T(8,128)S(1)} %add.45), channel_id=1, source_target_pairs={{0,16},{1,17},{2,18},{3,19},{4,20},{5,21},{6,22},{7,23},{8,24},{9,... | collective-permute-start | bytes 258056 | tf_op jit(solution)/shard_map/ppermute | solution.py:470
  22.5 2.6 %delensed.1 = bf16[48,64,128]{2,1,0:T(8,128)(2,1)} custom-call(bf16[48,64,128]{2,1,0:T(8,128)(2,1)S(1)} %copy-done.1, bf16[64,128]{1,0:T(8,128)(2,1)S(1)} %copy-done.5, s32[8,16]{1,0:T(8,128)S(1)} %copy-done.7, bf16[3168,128]{1,0:T(8,128)(2,1)S(1)} %get-tuple-element.44.refs_3_, f32[192,128]{1,0:T(8,128)S(1)} %get-tuple-element.45.refs_4_, ...), custom_call_target="tpu_custom_call" | custom-call | flops 679477248 | bytes 4194304 | tf_op jit(solution)/shard_map/delensed/pallas_call | solution.py:558
  25.0 0.9 %collective-permute-done.5 = f32[168,128]{1,0:T(8,128)S(1)} collective-permute-done((f32[168,128]{1,0:T(8,128)S(1)}, f32[168,128]{1,0:T(8,128)S(1)}, u32[]{:S(2)}, u32[]{:S(2)}) %collective-permute-start.5) | collective-permute-done | bytes 86048 | tf_op jit(solution)/shard_map/ppermute | solution.py:470
  26.0 4.1 %collective-permute-start.6 = (f32[168,128]{1,0:T(8,128)S(1)}, f32[168,128]{1,0:T(8,128)S(1)}, u32[]{:S(2)}, u32[]{:S(2)}) collective-permute-start(f32[168,128]{1,0:T(8,128)S(1)} %add.46), channel_id=1, source_target_pairs={{0,1},{1,0},{2,3},{3,2},{4,5},{5,4},{6,7},{7,6},{8,9},{9,8},{10,11... | collective-permute-start | bytes 258056 | tf_op jit(solution)/shard_map/ppermute | solution.py:470
  30.2 2.6 %grad_input.1 = bf16[48,64,128]{2,1,0:T(8,128)(2,1)} custom-call(bf16[48,64,128]{2,1,0:T(8,128)(2,1)S(1)} %copy-done.3, bf16[64,128]{1,0:T(8,128)(2,1)S(1)} %copy-done.5, s32[8,16]{1,0:T(8,128)S(1)} %copy-done.7, bf16[3168,128]{1,0:T(8,128)(2,1)S(1)} %get-tuple-element.50.refs_3_, f32[192,128]{1,0:T(8,128)S(1)} %get-tuple-element.51.refs_4_, ...), custom_call_target="tpu_custom_call" | custom-call | flops 679477248 | bytes 4194304 | tf_op jit(solution)/shard_map/grad_input/pallas_call | solution.py:558
  32.8 1.6 %collective-permute-start.7 = (f32[168,128]{1,0:T(8,128)S(1)}, f32[168,128]{1,0:T(8,128)S(1)}, u32[]{:S(2)}, u32[]{:S(2)}) collective-permute-start(f32[168,128]{1,0:T(8,128)S(1)} %add.47), channel_id=1, source_target_pairs={{0,2},{1,3},{2,0},{3,1},{4,6},{5,7},{6,4},{7,5},{8,10},{9,11},{10,... | collective-permute-start | bytes 258056 | tf_op jit(solution)/shard_map/ppermute | solution.py:470
  34.5 2.9 %collective-permute-done.7 = f32[168,128]{1,0:T(8,128)S(1)} collective-permute-done((f32[168,128]{1,0:T(8,128)S(1)}, f32[168,128]{1,0:T(8,128)S(1)}, u32[]{:S(2)}, u32[]{:S(2)}) %collective-permute-start.7) | collective-permute-done | bytes 86048 | tf_op jit(solution)/shard_map/ppermute | solution.py:470
  37.4 2.6 %collective-permute-start.8 = (f32[168,128]{1,0:T(8,128)S(1)}, f32[168,128]{1,0:T(8,128)S(1)}, u32[]{:S(2)}, u32[]{:S(2)}) collective-permute-start(f32[168,128]{1,0:T(8,128)S(1)} %add.48), channel_id=1, source_target_pairs={{0,4},{1,5},{2,6},{3,7},{4,0},{5,1},{6,2},{7,3},{8,12},{9,13},{10,... | collective-permute-start | bytes 258056 | tf_op jit(solution)/shard_map/ppermute | solution.py:470
  40.0 2.8 %collective-permute-done.8 = f32[168,128]{1,0:T(8,128)S(1)} collective-permute-done((f32[168,128]{1,0:T(8,128)S(1)}, f32[168,128]{1,0:T(8,128)S(1)}, u32[]{:S(2)}, u32[]{:S(2)}) %collective-permute-start.8) | collective-permute-done | bytes 86048 | tf_op jit(solution)/shard_map/ppermute | solution.py:470
  42.9 1.3 %collective-permute-done.9.refs_1_ = f32[168,128]{1,0:T(8,128)S(1)} collective-permute-done((f32[168,128]{1,0:T(8,128)S(1)}, f32[168,128]{1,0:T(8,128)S(1)}, u32[]{:S(2)}, u32[]{:S(2)}) %collective-permute-start.9) | collective-permute-done | bytes 86048 | tf_op jit(solution)/shard_map/ppermute | solution.py:470
  44.2 1.0 %unpack.1 = (f32[3,3,48,48]{3,2,1,0:T(8,128)}, f32[3,3,48,48]{3,2,1,0:T(8,128)}, f32[3,48]{1,0:T(4,128)}) custom-call(f32[168,128]{1,0:T(8,128)S(1)} %add.49.refs_0_, f32[168,128]{1,0:T(8,128)S(1)} %collective-permute-done.9.refs_1_), custom_call_target="tpu_custom_call" | custom-call | tf_op jit(solution)/shard_map/unpack/pallas_call | solution.py:593
  (40 shorter events, 0.9 us)
Async XLA Ops:
  0.6 1.1 %copy-start = (bf16[48,64,128]{2,1,0:T(8,128)(2,1)S(1)}, bf16[48,64,128]{2,1,0:T(8,128)(2,1)}, u32[]{:S(2)}) copy-start(bf16[48,64,128]{2,1,0:T(8,128)(2,1)} %refs_0_.2) | copy-start | bytes 2359300
  1.8 1.1 %copy-start.2 = (bf16[48,64,128]{2,1,0:T(8,128)(2,1)S(1)}, bf16[48,64,128]{2,1,0:T(8,128)(2,1)}, u32[]{:S(2)}) copy-start(bf16[48,64,128]{2,1,0:T(8,128)(2,1)} %refs_0_.3) | copy-start | bytes 2359300
  2.9 0.7 %copy-start.4 = (bf16[64,128]{1,0:T(8,128)(2,1)S(1)}, bf16[64,128]{1,0:T(8,128)(2,1)}, u32[]{:S(2)}) copy-start(bf16[64,128]{1,0:T(8,128)(2,1)} %refs_1_.3) | copy-start | bytes 49156
  3.6 0.7 %copy-start.6 = (s32[8,16]{1,0:T(8,128)S(1)}, s32[8,16]{1,0:T(8,128)}, u32[]{:S(2)}) copy-start(s32[8,16]{1,0:T(8,128)} %refs_2_.3) | copy-start | bytes 1540
  4.3 1.4 %copy-start.8 = (bf16[3,3,48,48]{3,2,1,0:T(8,128)(2,1)S(1)}, bf16[3,3,48,48]{3,2,1,0:T(8,128)(2,1)}, u32[]{:S(2)}) copy-start(bf16[3,3,48,48]{3,2,1,0:T(8,128)(2,1)} %param.13) | copy-start | bytes 124420
  4.5 3.3 %collective-permute-start = (bf16[208,128]{1,0:T(8,128)(2,1)S(1)}, bf16[208,128]{1,0:T(8,128)(2,1)S(1)}, u32[]{:S(2)}, u32[]{:S(2)}) collective-permute-start(bf16[208,128]{1,0:T(8,128)(2,1)S(1)} %get-tuple-element.31), channel_id=1, source_target_pairs={{0,8},{1,9},{2,10},{3,11},{4,12},{5,13},{6,14},{7,15},{8,0},{9,1},... | collective-permute-start | bytes 159752 | tf_op jit(solution)/shard_map/ppermute | solution.py:470
  5.0 2.8 %collective-permute-start.1 = (bf16[208,128]{1,0:T(8,128)(2,1)S(1)}, bf16[208,128]{1,0:T(8,128)(2,1)S(1)}, u32[]{:S(2)}, u32[]{:S(2)}) collective-permute-start(bf16[208,128]{1,0:T(8,128)(2,1)S(1)} %get-tuple-element.32), channel_id=1, source_target_pairs={{8,16},{9,17},{10,18},{11,19},{12,20},{13,21},{14,22},{15,23},{16,... | collective-permute-start | bytes 159752 | tf_op jit(solution)/shard_map/ppermute | solution.py:470
  5.8 0.9 %copy-start.9 = (bf16[3,3,48,48]{3,2,1,0:T(8,128)(2,1)S(1)}, bf16[3,3,48,48]{3,2,1,0:T(8,128)(2,1)}, u32[]{:S(2)}) copy-start(bf16[3,3,48,48]{3,2,1,0:T(8,128)(2,1)} %param.14) | copy-start | bytes 124420
  6.7 0.7 %copy-start.10 = (f32[48]{0:T(128)S(1)}, f32[48]{0:T(128)}, u32[]{:S(2)}) copy-start(f32[48]{0:T(128)} %param.17) | copy-start | bytes 580
  6.7 0.7 %copy-start.11 = (f32[48]{0:T(128)S(1)}, f32[48]{0:T(128)}, u32[]{:S(2)}) copy-start(f32[48]{0:T(128)} %param.16) | copy-start | bytes 580
  6.7 0.7 %copy-start.12 = (f32[48]{0:T(128)S(1)}, f32[48]{0:T(128)}, u32[]{:S(2)}) copy-start(f32[48]{0:T(128)} %param.15) | copy-start | bytes 580
  6.7 1.2 %copy-start.1 = (bf16[48,64,128]{2,1,0:T(8,128)(2,1)S(1)}, bf16[48,64,128]{2,1,0:T(8,128)(2,1)}, u32[]{:S(2)}) copy-start(bf16[48,64,128]{2,1,0:T(8,128)(2,1)} %refs_0_.2) | copy-start | bytes 2359300
  6.7 1.4 %copy-start.3 = (bf16[48,64,128]{2,1,0:T(8,128)(2,1)S(1)}, bf16[48,64,128]{2,1,0:T(8,128)(2,1)}, u32[]{:S(2)}) copy-start(bf16[48,64,128]{2,1,0:T(8,128)(2,1)} %refs_0_.3) | copy-start | bytes 2359300
  7.8 0.8 %copy-start.5 = (bf16[64,128]{1,0:T(8,128)(2,1)S(1)}, bf16[64,128]{1,0:T(8,128)(2,1)}, u32[]{:S(2)}) copy-start(bf16[64,128]{1,0:T(8,128)(2,1)} %refs_1_.3) | copy-start | bytes 49156
  7.8 0.8 %copy-start.7 = (s32[8,16]{1,0:T(8,128)S(1)}, s32[8,16]{1,0:T(8,128)}, u32[]{:S(2)}) copy-start(s32[8,16]{1,0:T(8,128)} %refs_2_.3) | copy-start | bytes 1540
  9.3 7.3 %collective-permute-start.2 = (bf16[208,128]{1,0:T(8,128)(2,1)S(1)}, bf16[208,128]{1,0:T(8,128)(2,1)S(1)}, u32[]{:S(2)}, u32[]{:S(2)}) collective-permute-start(bf16[208,128]{1,0:T(8,128)(2,1)S(1)} %get-tuple-element.33), channel_id=1, source_target_pairs={{0,1},{1,0},{2,3},{3,2},{4,5},{5,4},{6,7},{7,6},{8,9},{9,8},{10,11... | collective-permute-start | bytes 159752 | tf_op jit(solution)/shard_map/ppermute | solution.py:470
  11.9 4.7 %collective-permute-start.3 = (bf16[208,128]{1,0:T(8,128)(2,1)S(1)}, bf16[208,128]{1,0:T(8,128)(2,1)S(1)}, u32[]{:S(2)}, u32[]{:S(2)}) collective-permute-start(bf16[208,128]{1,0:T(8,128)(2,1)S(1)} %get-tuple-element.34), channel_id=1, source_target_pairs={{1,2},{2,1},{3,4},{4,3},{5,6},{6,5},{9,10},{10,9},{11,12},{12,11},... | collective-permute-start | bytes 159752 | tf_op jit(solution)/shard_map/ppermute | solution.py:470
  17.5 3.6 %collective-permute-start.4 = (f32[168,128]{1,0:T(8,128)S(1)}, f32[168,128]{1,0:T(8,128)S(1)}, u32[]{:S(2)}, u32[]{:S(2)}) collective-permute-start(f32[168,128]{1,0:T(8,128)S(1)} %get-tuple-element.41), channel_id=1, source_target_pairs={{0,8},{1,9},{2,10},{3,11},{4,12},{5,13},{6,14},{7,15},{8,0},{9,1},... | collective-permute-start | bytes 258056 | tf_op jit(solution)/shard_map/ppermute | solution.py:470
  21.1 4.9 %collective-permute-start.5 = (f32[168,128]{1,0:T(8,128)S(1)}, f32[168,128]{1,0:T(8,128)S(1)}, u32[]{:S(2)}, u32[]{:S(2)}) collective-permute-start(f32[168,128]{1,0:T(8,128)S(1)} %add.45), channel_id=1, source_target_pairs={{0,16},{1,17},{2,18},{3,19},{4,20},{5,21},{6,22},{7,23},{8,24},{9,... | collective-permute-start | bytes 258056 | tf_op jit(solution)/shard_map/ppermute | solution.py:470
  26.0 6.8 %collective-permute-start.6 = (f32[168,128]{1,0:T(8,128)S(1)}, f32[168,128]{1,0:T(8,128)S(1)}, u32[]{:S(2)}, u32[]{:S(2)}) collective-permute-start(f32[168,128]{1,0:T(8,128)S(1)} %add.46), channel_id=1, source_target_pairs={{0,1},{1,0},{2,3},{3,2},{4,5},{5,4},{6,7},{7,6},{8,9},{9,8},{10,11... | collective-permute-start | bytes 258056 | tf_op jit(solution)/shard_map/ppermute | solution.py:470
  32.8 4.6 %collective-permute-start.7 = (f32[168,128]{1,0:T(8,128)S(1)}, f32[168,128]{1,0:T(8,128)S(1)}, u32[]{:S(2)}, u32[]{:S(2)}) collective-permute-start(f32[168,128]{1,0:T(8,128)S(1)} %add.47), channel_id=1, source_target_pairs={{0,2},{1,3},{2,0},{3,1},{4,6},{5,7},{6,4},{7,5},{8,10},{9,11},{10,... | collective-permute-start | bytes 258056 | tf_op jit(solution)/shard_map/ppermute | solution.py:470
  37.4 5.4 %collective-permute-start.8 = (f32[168,128]{1,0:T(8,128)S(1)}, f32[168,128]{1,0:T(8,128)S(1)}, u32[]{:S(2)}, u32[]{:S(2)}) collective-permute-start(f32[168,128]{1,0:T(8,128)S(1)} %add.48), channel_id=1, source_target_pairs={{0,4},{1,5},{2,6},{3,7},{4,0},{5,1},{6,2},{7,3},{8,12},{9,13},{10,... | collective-permute-start | bytes 258056 | tf_op jit(solution)/shard_map/ppermute | solution.py:470
  42.9 1.3 %collective-permute-start.9 = (f32[168,128]{1,0:T(8,128)S(1)}, f32[168,128]{1,0:T(8,128)S(1)}, u32[]{:S(2)}, u32[]{:S(2)}) collective-permute-start(f32[168,128]{1,0:T(8,128)S(1)} %add.49.refs_0_), channel_id=1, source_target_pairs={{0,8},{1,9},{2,10},{3,11},{4,12},{5,13},{6,14},{7,15},{8,0},{9,1},... | collective-permute-start | bytes 258056 | tf_op jit(solution)/shard_map/ppermute | solution.py:470

commit v4 on v3

--- a/solution.py
+++ b/solution.py
@@ -35,43 +35,66 @@
     return lax.rem(lax.axis_index(axis), 2) == 1
 
 
-def row_kernel(sky_top, sky_bot, cot_top, cot_bot, phi_ref, mask_ref, a_ref, b_ref):
-    chans = sky_top.shape[0]
-    cells = tile_rows(mask_ref)
+def row_kernel(sky_ref, cot_ref, phi_ref, mask_ref, a_ref, b_ref, blocks, phis, tiles, sems):
+    chans, rows, _ = sky_ref.shape
+    copies = []
+    for n, (src, dst) in enumerate(
+        [
+            (ref.at[:, pl.ds(first, 16), :], blocks.at[k])
+            for k, (ref, first) in enumerate(
+                ((sky_ref, 0), (cot_ref, 0), (sky_ref, rows - 16), (cot_ref, rows - 16))
+            )
+        ]
+        + [(phi_ref.at[pl.ds(0, 16), :], phis.at[0]), (phi_ref.at[pl.ds(rows - 16, 16), :], phis.at[1])]
+        + [(mask_ref, tiles)]
+    ):
+        copies.append(pltpu.make_async_copy(src, dst, sems.at[n]))
+        copies[-1].start()
+    for copy in copies:
+        copy.wait()
+    cells = tile_rows(tiles)
     odd = is_odd("gy")
     parts = []
-    for sky, cot, first, mrow, prow in (
-        (sky_top, cot_top, 0, 0, 0),
-        (sky_bot, cot_bot, 14, mask_ref.shape[0] - 1, phi_ref.shape[0] - 1),
-    ):
+    for side, (first, mrow) in enumerate(((0, 0), (14, tiles.shape[0] - 1))):
         keep = cells[mrow : mrow + 1]
         low = jnp.broadcast_to(keep, (chans, 128)).astype(BF)
         part = []
-        for src in (sky, cot):
-            block = jnp.transpose(src[...], (1, 0, 2))
+        for k in range(2):
+            block = jnp.transpose(blocks[2 * side + k], (1, 0, 2))
             part += [block[first] * low, block[first + 1] * low]
         row = lax.broadcasted_iota(jnp.int32, (16, 128), 0)
-        prow_v = jnp.broadcast_to(phi_ref[prow : prow + 1].astype(F32), (16, 128))
-        part.append(jnp.where(row == 0, prow_v, jnp.where(row == 1, keep, 0.0)).astype(BF))
+        prow = phis[side].astype(F32)[15 * side : 15 * side + 1]
+        prow = jnp.broadcast_to(prow, (16, 128))
+        part.append(jnp.where(row == 0, prow, jnp.where(row == 1, keep, 0.0)).astype(BF))
         parts.append(jnp.concatenate(part, axis=0))
     up, down = parts
     a_ref[...] = jnp.where(odd, up, down)
     b_ref[...] = jnp.where(odd, down, up)
 
 
-def col_kernel(
-    sky_ref, cot_ref, phi_ref, mask_ref, a_ref, b_ref,
-    sa_ref, sb_ref, own_ref, halo_ref, strip,
+def prep_kernel(
+    sky_hbm, cot_hbm, phi_hbm, mask_hbm, a3, own_ref, gphi_ref, phix, maskx,
+    strip, sky_ref, cot_ref, phi_ref, mask_ref, sems,
 ):
     chans, rows, width = sky_ref.shape
-    size = a_ref.shape[0]
-    odd = is_odd("gy")
-    ra, rb = a_ref[...], b_ref[...]
-    tops_all = jnp.where(odd, ra, rb)
-    bots_all = jnp.where(odd, rb, ra)
-    halo_ref[0] = tops_all
-    halo_ref[1] = bots_all
+    size = own_ref.shape[1]
+    step = 3 * chans
     half = chans // 2
+    copies = [
+        pltpu.make_async_copy(src, dst, sems.at[n])
+        for n, (src, dst) in enumerate(
+            ((mask_hbm, mask_ref), (phi_hbm, phi_ref), (sky_hbm, sky_ref), (cot_hbm, cot_ref))
+        )
+    ]
+    for copy in copies:
+        copy.start()
+    copies[0].wait()
+    copies[1].wait()
+    cells = tile_rows(mask_ref)
+    phi = phi_ref[...].astype(F32)
+    phix[...] = phi
+    for t in range(mask_ref.shape[0]):
+        maskx[TILE * t : TILE * (t + 1)] = jnp.broadcast_to(cells[t : t + 1], (TILE, 128))
     lane8 = lane_iota(8)
     row8 = lax.broadcasted_iota(jnp.int32, (8, 128), 0)
     pick = ((row8 < 2) & (lane8 == row8)) | (
@@ -94,82 +117,18 @@
     keep = lax.dot_general(edge.astype(BF), spread, NN, preferred_element_type=F32)
     phis = lax.dot_general(pick, phi_ref[...], NT, preferred_element_type=F32)
     phis = jnp.concatenate([phis, jnp.zeros((8, 128 - rows), F32)], axis=1)
-    lane = lane_iota(chans)
+    gphi = jnp.zeros((chans, 128), F32)
     for which, src in ((0, sky_ref), (1, cot_ref)):
+        copies[2 + which].wait()
         both = jnp.concatenate([src[:half], src[half:]], axis=1).reshape(half * 128, width)
         flat = lax.dot_general(pick, both, NT, preferred_element_type=F32)
         for j in range(half):
-            strip[8 * j : 8 * j + 8] = flat[:, 128 * j : 128 * j + 128]
+            strip[which, 8 * j : 8 * j + 8] = flat[:, 128 * j : 128 * j + 128]
         for k in range(4):
-            part = strip[pl.ds(k, half, stride=8), :]
+            part = strip[which, pl.ds(k, half, stride=8), :]
             col = jnp.concatenate([part, pltpu.roll(part, 64, 1)], axis=0)
-            col = (col * keep[k : k + 1]).astype(BF)
-            at = (0, 1, width - 2, width - 1)[k]
-            for value, where in ((tops_all, (126, 127)), (bots_all, (rows, rows + 1))):
-                for n in range(2):
-                    base = (2 * which + n) * chans
-                    cell = value[base : base + chans, at : at + 1]
-                    col = jnp.where(lane == where[n], jnp.broadcast_to(cell, col.shape), col)
             base = (2 * which + k % 2) * chans
-            own_ref[k // 2, base : base + chans] = col
-    row = lax.broadcasted_iota(jnp.int32, (16, 128), 0)
-    lane16 = lane_iota(16)
-    tops = tops_all[4 * chans : size].astype(F32)
-    bots = bots_all[4 * chans : size].astype(F32)
-    for side, k, at in ((0, 0, 0), (1, 3, width - 1)):
-        extra = jnp.where(
-            row == 0,
-            jnp.broadcast_to(phis[k : k + 1], (16, 128)),
-            jnp.where(row == 1, jnp.broadcast_to(keep[k : k + 1], (16, 128)), 0.0),
-        )
-        extra = jnp.where(lane16 == 127, jnp.broadcast_to(tops[:, at : at + 1], (16, 128)), extra)
-        extra = jnp.where(lane16 == rows, jnp.broadcast_to(bots[:, at : at + 1], (16, 128)), extra)
-        own_ref[side, 4 * chans : size] = extra.astype(BF)
-    odd_x = is_odd("gx")
-    sa_ref[...] = jnp.where(odd_x, own_ref[0], own_ref[1])
-    sb_ref[...] = jnp.where(odd_x, own_ref[1], own_ref[0])
-
-
-def silu_parts(pre):
-    sigma = 1.0 / (1.0 + jnp.exp(-pre))
-    return pre * sigma, sigma * (1.0 + pre * (1.0 - sigma))
-
-
-def two_windows(src, first, second, size):
-    return jnp.concatenate([src[first : first + size], src[second : second + size]], axis=1)
-
-
-def hidden_kernel(
-    sky_ref, cot_ref, phi_ref, mask_ref, halo_ref, w1s_ref, w2ts_ref, cond_ref,
-    hid_ref, dpre_ref, acc1, acc2, cacc,
-    a3x, a3g, dz, phix, maskx,
-):
-    chans, rows, width = sky_ref.shape
-    size = halo_ref.shape[1]
-    step = 3 * chans
-    trows = mask_ref.shape[0]
-    cells = tile_rows(mask_ref)
-    lane1 = lane_iota(1)
-    inside = jnp.where((lane1 == 0) | (lane1 == 127), 0.0, 1.0)
-    for k, at in ((0, 0), (1, rows + 1)):
-        extra = halo_ref[k, 4 * chans : size].astype(F32)
-        phix[at : at + 1] = extra[0:1]
-        maskx[at : at + 1] = extra[1:2] * inside
-    phix[1 : rows + 1] = phi_ref[...].astype(F32)
-    for t in range(trows):
-        maskx[1 + TILE * t : 1 + TILE * (t + 1)] = jnp.broadcast_to(
-            cells[t : t + 1] * inside, (TILE, 128)
-        )
-
-    gphi = jnp.zeros((chans, 128), F32)
-
-    def put(dst, y, value):
-        base = (y + 2) * step
-        dst[base : base + chans] = pltpu.roll(value, 1, 1)
-        dst[base + chans : base + 2 * chans] = value
-        dst[base + 2 * chans : base + 3 * chans] = pltpu.roll(value, 127, 1)
-
-    for which, src, dst in ((0, sky_ref, a3x), (1, cot_ref, a3g)):
+            own_ref[k // 2, base : base + chans] = (col * keep[k : k + 1]).astype(BF)
         for j in range(rows // 16):
             block = jnp.transpose(src[:, 16 * j : 16 * j + 16, :], (1, 0, 2))
             for t in range(2):
@@ -177,14 +136,103 @@
                 for n in range(TILE):
                     y = 16 * j + TILE * t + n
                     value = block[TILE * t + n] * low
-                    put(dst, y, value)
+                    a3[which, y * step : (y + 1) * step] = three_copies(value)
                     if which:
-                        gphi = gphi + value.astype(F32) * phix[y + 1 : y + 2]
-        for k, first in ((0, -2), (1, rows)):
+                        gphi = gphi + value.astype(F32) * phi[y : y + 1]
+    gphi_ref[...] = gphi
+    row = lax.broadcasted_iota(jnp.int32, (16, 128), 0)
+    for side, k in ((0, 0), (1, 3)):
+        extra = jnp.where(
+            row == 0,
+            jnp.broadcast_to(phis[k : k + 1], (16, 128)),
+            jnp.where(row == 1, jnp.broadcast_to(keep[k : k + 1], (16, 128)), 0.0),
+        )
+        own_ref[side, 4 * chans : size] = extra.astype(BF)
+
+
+def three_copies(value):
+    return jnp.concatenate([pltpu.roll(value, 1, 1), value, pltpu.roll(value, 127, 1)], axis=0)
+
+
+def col_kernel(rows, width, mine_ref, a_ref, b_ref, sa_ref, sb_ref, own_ref, halo_ref):
+    size = a_ref.shape[0]
+    odd = is_odd("gy")
+    ra, rb = a_ref[...], b_ref[...]
+    tops = jnp.where(odd, ra, rb)
+    bots = jnp.where(odd, rb, ra)
+    halo_ref[0] = tops
+    halo_ref[1] = bots
+    chans = (size - 16) // 4
+    lane = lane_iota(chans)
+    lane16 = lane_iota(16)
+    sides = []
+    for side in range(2):
+        parts = []
+        for m in range(4):
+            which, k = divmod(m, 2)
+            at = k + (width - 2) * side
+            col = mine_ref[side, m * chans : (m + 1) * chans]
+            for value, where in ((tops, (126, 127)), (bots, (rows, rows + 1))):
+                for n in range(2):
+                    base = (2 * which + n) * chans
+                    cell = value[base : base + chans, at : at + 1]
+                    col = jnp.where(lane == where[n], jnp.broadcast_to(cell, col.shape), col)
+            parts.append(col)
+        at = (width - 1) * side
+        extra = mine_ref[side, 4 * chans : size].astype(F32)
+        for value, where in ((tops, 127), (bots, rows)):
+            cell = value[4 * chans : size].astype(F32)[:, at : at + 1]
+            extra = jnp.where(lane16 == where, jnp.broadcast_to(cell, (16, 128)), extra)
+        parts.append(extra.astype(BF))
+        sides.append(jnp.concatenate(parts, axis=0))
+        own_ref[side] = sides[side]
+    odd_x = is_odd("gx")
+    sa_ref[...] = jnp.where(odd_x, sides[0], sides[1])
+    sb_ref[...] = jnp.where(odd_x, sides[1], sides[0])
+
+
+def silu_parts(pre):
+    sigma = 1.0 / (1.0 + jnp.exp(-pre))
+    return pre * sigma, sigma * (1.0 + pre * (1.0 - sigma))
+
+
+def hidden_kernel(
+    a3, phi_own, mask_own, halo_ref, w1s_ref, w2ts_ref, cond_ref,
+    hid_ref, dpre_ref, acc1, acc2, cacc,
+    dz, phix, maskx, ringx, ringg,
+):
+    rows, width = phi_own.shape
+    a3x, a3g = a3.at[0], a3.at[1]
+    size = halo_ref.shape[1]
+    chans = (size - 16) // 4
+    step = 3 * chans
+    lane1 = lane_iota(1)
+    inside = jnp.where((lane1 == 0) | (lane1 == 127), 0.0, 1.0)
+    for k, at in ((0, 0), (1, rows + 1)):
+        extra = halo_ref[k, 4 * chans : size].astype(F32)
+        phix[at : at + 1] = extra[0:1]
+        maskx[at : at + 1] = extra[1:2] * inside
+    phix[1 : rows + 1] = phi_own[...]
+    maskx[1 : rows + 1] = mask_own[...] * inside
+    for which, ring in ((0, ringx), (1, ringg)):
+        for k in range(2):
             for n in range(2):
                 base = (2 * which + n) * chans
-                put(dst, first + n, halo_ref[k, base : base + chans])
-    cacc[2] = gphi
+                ring[(2 * k + n) * step : (2 * k + n + 1) * step] = three_copies(
+                    halo_ref[k, base : base + chans]
+                )
+
+    def window(own, ring, y, count):
+        parts = []
+        if y < 0:
+            parts.append(ring[(y + 2) * step : min(2, y + 2 + count) * step])
+        low, high = max(y, 0), min(y + count, rows)
+        if low < high:
+            parts.append(own[low * step : high * step])
+        if y + count > rows:
+            low = max(y, rows) - rows
+            parts.append(ring[(2 + low) * step : (2 + y + count - rows) * step])
+        return parts[0] if len(parts) == 1 else jnp.concatenate(parts, axis=0)
 
     gain = cond_ref[:, 0:1]
     bias = cond_ref[:, 1:2]
@@ -195,14 +243,13 @@
 
     def first_pass(it, dphi, dsum):
         y0 = R1 * it - 1
-        win = (R1 + 2) * step
-        at = ((y0 + 1) * step, (y0 + split + 1) * step)
-        pre = lax.dot_general(
-            w1s_ref[...], two_windows(a3x, *at, win), NN, preferred_element_type=F32
-        )
-        back = lax.dot_general(
-            w2ts_ref[...], two_windows(a3g, *at, win), NN, preferred_element_type=F32
-        )
+
+        def both(own, ring):
+            pair = [window(own, ring, y0 - 1 + h * split, R1 + 2) for h in range(2)]
+            return jnp.concatenate(pair, axis=1)
+
+        pre = lax.dot_general(w1s_ref[...], both(a3x, ringx), NN, preferred_element_type=F32)
+        back = lax.dot_general(w2ts_ref[...], both(a3g, ringg), NN, preferred_element_type=F32)
         for h in range(2):
             for r in range(R1):
                 row = y0 + h * split + r + 1
@@ -237,14 +284,14 @@
         ys = [GROUP1 * it + n - 1 for n in range(GROUP1)]
         acc1[...] += lax.dot_general(
             jnp.concatenate([rows_of(dz, (y + 1) * chans, step) for y in ys], axis=1),
-            jnp.concatenate([rows_of(a3x, (y + 2) * step, step) for y in ys], axis=1),
+            jnp.concatenate([window(a3x, ringx, y, 1) for y in ys], axis=1),
             NT, preferred_element_type=F32,
         )
 
     def grads_two(it):
         ys = [GROUP2 * it + n for n in range(GROUP2)]
         acc2[...] += lax.dot_general(
-            jnp.concatenate([rows_of(a3g, (y + 2) * step, step) for y in ys], axis=1),
+            jnp.concatenate([window(a3g, ringg, y, 1) for y in ys], axis=1),
             jnp.concatenate([rows_of(hid_ref, y * chans, step) for y in ys], axis=1),
             NT, preferred_element_type=F32,
         )
@@ -257,7 +304,7 @@
 
 def edge_kernel(
     rows, a_ref, b_ref, own_ref, w1c_ref, w2tc_ref, w2c_ref, w1tc_ref, cond_ref,
-    acc1, acc2, cacc,
+    acc1, acc2, cacc, gphi_ref,
     hfix_ref, dfix_ref, keep_ref, give_ref, wire,
 ):
     size = a_ref.shape[0]
@@ -337,7 +384,7 @@
     for d, k in ((d_own[0], 1), (d_own[1], 2)):
         dphi = dphi + d.astype(F32) * extra[k][0:1]
         dsum = dsum + d.astype(F32)
-    sums = [jnp.sum(v, axis=1, keepdims=True) for v in (dphi, dsum, cacc[2])]
+    sums = [jnp.sum(v, axis=1, keepdims=True) for v in (dphi, dsum, gphi_ref[...])]
     fill = jnp.zeros((chans, 128 - 3 * tails[0].shape[1] - 3), F32)
     wire[2 * step : 2 * step + chans] = jnp.concatenate(tails + sums + [fill], axis=1)
     none = jnp.zeros((chans, 128), BF)
@@ -368,15 +415,15 @@
 
 
 def output_kernel(
-    with_phi, src_ref, phi_ref, mask_ref, mid_ref, fix_ref, weights_ref, cond_ref,
-    out_ref, a3, rowbuf, fixbuf,
+    with_phi, src_hbm, phi_ref, mask_ref, mid_ref, fix_ref, weights_ref, cond_ref,
+    out_ref, a3, rowbuf, fixbuf, src_ref, sem,
 ):
     chans, rows, width = src_ref.shape
     step = 3 * chans
     half = chans // 2
-    cells = tile_rows(mask_ref)
+    fetch = pltpu.make_async_copy(src_hbm, src_ref, sem)
+    fetch.start()
     if with_phi:
-        phi = phi_ref[...].astype(F32)
         gain = cond_ref[:, 2:3]
     lane8 = lane_iota(8)
     row8 = lax.rem(lax.broadcasted_iota(jnp.int32, (8, 128), 0), 4)
@@ -399,7 +446,9 @@
         y0 = R2 * it
         got = lax.dot_general(
             weights_ref[...],
-            two_windows(a3, y0 * step, (y0 + rows // 2) * step, (R2 + 2) * step),
+            jnp.concatenate(
+                [a3[(y0 + h) * step : (y0 + h + R2 + 2) * step] for h in (0, rows // 2)], axis=1
+            ),
             NN, preferred_element_type=F32,
         )
         for h in range(2):
@@ -407,15 +456,13 @@
                 y = y0 + h * (rows // 2) + r
                 part = got[r * chans : (r + 1) * chans, h * 128 : h * 128 + 128]
                 if with_phi:
-                    part = part + gain * phi[y : y + 1]
+                    part = part + gain * phi_ref[y : y + 1]
                 rowbuf[y] = part
 
+    fetch.wait()
     for j in range(rows // 16):
         here = slice(16 * j, 16 * j + 16)
-        keep = jnp.concatenate(
-            [jnp.broadcast_to(cells[2 * j + t : 2 * j + t + 1], (TILE, 128)) for t in range(2)],
-            axis=0,
-        )
+        keep = mask_ref[here]
         total = jnp.transpose(rowbuf[here], (1, 0, 2)) + fixbuf[:, here, :]
         out_ref[:, here, :] = ((total + src_ref[:, here, :].astype(F32)) * keep[None]).astype(BF)
 
@@ -449,11 +496,60 @@
     return pltpu.CompilerParams(vmem_limit_bytes=mib << 20)
 
 
-def stacked(block, count, chans):
-    step = 3 * chans
-    return jnp.concatenate(
-        [jnp.pad(block, ((0, 0), (r * step, (count - 1 - r) * step))) for r in range(count)], axis=0
-    )
+def keep_near(value):
+    return pltpu.with_memory_space_constraint(value, pltpu.VMEM)
+
+
+def stacked(block, count):
+    chans, taps = block.shape
+    step = taps // 3
+    rows = []
+    for r in range(count):
+        parts = [block]
+        if r:
+            parts.insert(0, jnp.zeros((chans, r * step), BF))
+        if r < count - 1:
+            parts.append(jnp.zeros((chans, (count - 1 - r) * step), BF))
+        rows.append(jnp.concatenate(parts, axis=1))
+    return jnp.concatenate(rows, axis=0)
+
+
+def weight_kernel(
+    one_hbm, two_hbm, c1_hbm, b1_hbm, c2_hbm,
+    w1f_ref, w2b_ref, w2f_ref, w1b_ref, w1s_ref, w2bs_ref, w2s_ref, w1bs_ref, cond_ref,
+    one, two, vec0, vec1, vec2, sems,
+):
+    copies = [
+        pltpu.make_async_copy(src, dst, sems.at[n])
+        for n, (src, dst) in enumerate(
+            ((one_hbm, one), (two_hbm, two), (c1_hbm, vec0), (b1_hbm, vec1), (c2_hbm, vec2))
+        )
+    ]
+    for copy in copies:
+        copy.start()
+    for copy in copies:
+        copy.wait()
+    chans = one.shape[2]
+    for src, fwd, fwd_s, count, bwd, bwd_s, back in (
+        (one, w1f_ref, w1s_ref, R1, w1b_ref, w1bs_ref, R2),
+        (two, w2f_ref, w2s_ref, R2, w2b_ref, w2bs_ref, R1),
+    ):
+        taps = [src[k // 3, k % 3] for k in range(9)]
+        plain = jnp.concatenate(taps, axis=1)
+        turned = jnp.concatenate(
+            [jnp.transpose(t.astype(F32)).astype(BF) for t in taps[::-1]], axis=1
+        )
+        fwd[...] = plain
+        bwd[...] = turned
+        fwd_s[...] = stacked(plain, count)
+        bwd_s[...] = stacked(turned, back)
+    row = lax.broadcasted_iota(jnp.int32, (8, chans), 0)
+    table = jnp.zeros((8, chans), F32)
+    for k, ref in enumerate((vec0, vec1, vec2)):
+        table = jnp.where(row == k, jnp.broadcast_to(ref[...].reshape(1, chans), (8, chans)), table)
+    table = jnp.concatenate([table, jnp.zeros((8, 128 - chans), F32)], axis=1)
+    table = jnp.concatenate([table, jnp.zeros((120, 128), F32)], axis=0)
+    cond_ref[...] = jnp.transpose(table)[:chans]
 
 
 def build(mesh):
@@ -479,6 +575,14 @@
             return move
 
         return send(first, partner(0)), send(second, partner(1))
+
+    def exchange(value, moves):
+        got = [send(value, lambda a, b: (a ^ m[0], b ^ m[1])) for m in moves]
+        if len(moves) == 1:
+            return value + got[0]
+        both = (moves[0][0] ^ moves[1][0], moves[0][1] ^ moves[1][1])
+        far = send(value, lambda a, b: (a ^ both[0], b ^ both[1]))
+        return (value + got[0]) + (got[1] + far)
 
     def local(
         sky, lens_phi, cotangent, tile_mask, weight_one, weight_two, cond_one, bias_one, cond_two
@@ -489,49 +593,91 @@
         assert 2 * rows == 128 and width == 128
         edge = jax.ShapeDtypeStruct((size, 128), BF)
         edges = jax.ShapeDtypeStruct((2, size, 128), BF)
-        vmem = pl.BlockSpec(memory_space=pltpu.VMEM)
-        first = pl.BlockSpec((chans, 16, width), lambda i: (0, 0, 0))
-        last = pl.BlockSpec((chans, 16, width), lambda i: (0, rows // 16 - 1, 0))
+        hbm = pl.BlockSpec(memory_space=pltpu.HBM)
+        near = pl.BlockSpec(memory_space=pltpu.VMEM)
+        far = [
+            pltpu.with_memory_space_constraint(v, pltpu.HBM)
+            for v in (sky, cotangent, lens_phi, tile_mask)
+        ]
         ra, rb = pl.pallas_call(
             row_kernel,
-            grid=(1,),
             out_shape=(edge, edge),
-            in_specs=[first, last, first, last, vmem, vmem],
-            out_specs=(vmem, vmem),
+            in_specs=[hbm] * 4,
+            scratch_shapes=[
+                pltpu.VMEM((4, chans, 16, width), BF),
+                pltpu.VMEM((2, 16, width), BF),
+                pltpu.VMEM(tile_mask.shape, jnp.int32),
+                pltpu.SemaphoreType.DMA((7,)),
+            ],
             compiler_params=limit(8),
             name="edge_rows",
-        )(sky, sky, cotangent, cotangent, lens_phi, tile_mask)
+        )(*far)
+        ra, rb, weight_one, weight_two = lax.optimization_barrier((ra, rb, weight_one, weight_two))
         ra, rb = swap(ra, rb, 0)
 
-        def taps(weight, back):
-            if back:
-                return weight[::-1, ::-1].transpose(3, 0, 1, 2).reshape(chans, 3 * step)
-            return weight.transpose(2, 0, 1, 3).reshape(chans, 3 * step)
-
-        w1f, w1b = taps(weight_one, False), taps(weight_one, True)
-        w2f, w2b = taps(weight_two, False), taps(weight_two, True)
-        conds = jnp.stack([cond_one, bias_one, cond_two], axis=1)
-        conds = jnp.pad(conds, ((0, 0), (0, 125)))
-
+        flat_w = jax.ShapeDtypeStruct((chans, 3 * step), BF)
+        first_w = jax.ShapeDtypeStruct((R1 * chans, (R1 + 2) * step), BF)
+        second_w = jax.ShapeDtypeStruct((R2 * chans, (R2 + 2) * step), BF)
+        w1f, w2b, w2f, w1b, w1s, w2bs, w2s, w1bs, conds = pl.pallas_call(
+            weight_kernel,
+            out_shape=(
+                flat_w, flat_w, flat_w, flat_w, first_w, first_w, second_w, second_w,
+                jax.ShapeDtypeStruct((chans, 128), F32),
+            ),
+            in_specs=[hbm] * 5,
+            scratch_shapes=[
+                pltpu.VMEM(weight_one.shape, BF),
+                pltpu.VMEM(weight_two.shape, BF),
+                pltpu.VMEM((chans,), F32),
+                pltpu.VMEM((chans,), F32),
+                pltpu.VMEM((chans,), F32),
+                pltpu.SemaphoreType.DMA((5,)),
+            ],
+            compiler_params=limit(8),
+            name="weights",
+        )(*[
+            pltpu.with_memory_space_constraint(v, pltpu.HBM)
+            for v in (weight_one, weight_two, cond_one, bias_one, cond_two)
+        ])
+
+        flops = 2 * 9 * chans * chans * rows * width
+        field = jax.ShapeDtypeStruct((2, rows * step, 128), BF)
+        flat = jax.ShapeDtypeStruct(lens_phi.shape, F32)
+        a3, mine, gphi, phi_own, mask_own = pl.pallas_call(
+            prep_kernel,
+            out_shape=(field, edges, jax.ShapeDtypeStruct((chans, 128), F32), flat, flat),
+            in_specs=[hbm] * 4,
+            scratch_shapes=[
+                pltpu.VMEM((2, 8 * chans // 2, 128), F32),
+                pltpu.VMEM(sky.shape, BF),
+                pltpu.VMEM(sky.shape, BF),
+                pltpu.VMEM(lens_phi.shape, BF),
+                pltpu.VMEM(tile_mask.shape, jnp.int32),
+                pltpu.SemaphoreType.DMA((4,)),
+            ],
+            compiler_params=limit(8),
+            cost_estimate=pl.CostEstimate(
+                flops=4 * flops, bytes_accessed=8 << 20, transcendentals=0
+            ),
+            name="prep",
+        )(*far)
         ca, cb, own, halo = pl.pallas_call(
-            col_kernel,
+            lambda *refs: col_kernel(rows, width, *refs),
             out_shape=(edge, edge, edges, edges),
-            scratch_shapes=[pltpu.VMEM((8 * chans // 2, 128), F32)],
             compiler_params=limit(8),
             name="edge_cols",
-        )(sky, cotangent, lens_phi, tile_mask, ra, rb)
+        )(mine, ra, rb)
         ca, cb = swap(ca, cb, 1)
 
-        flops = 2 * 9 * chans * chans * rows * width
-        field = pltpu.VMEM(((rows + 4) * step, 128), BF)
+        ring = pltpu.VMEM((4 * step, 128), BF)
         rowwise = pltpu.VMEM((rows + 8, 128), F32)
         inner = jax.ShapeDtypeStruct(((rows + 2) * chans, 128), BF)
         acc = jax.ShapeDtypeStruct((step, step), F32)
         hid, dpre, acc1, acc2, cacc = pl.pallas_call(
             hidden_kernel,
-            out_shape=(inner, inner, acc, acc, jax.ShapeDtypeStruct((3, chans, 128), F32)),
+            out_shape=(inner, inner, acc, acc, jax.ShapeDtypeStruct((2, chans, 128), F32)),
             scratch_shapes=[
-                field, field, pltpu.VMEM(((rows + 4) * chans, 128), BF), rowwise, rowwise,
+                pltpu.VMEM(((rows + 4) * chans, 128), BF), rowwise, rowwise, ring, ring,
             ],
             compiler_params=limit(16),
             cost_estimate=pl.CostEstimate(
@@ -539,8 +685,8 @@
             ),
             name="hidden",
         )(
-            sky, cotangent, lens_phi, tile_mask, halo,
-            stacked(w1f, R1, chans), stacked(w2b, R1, chans), conds,
+            keep_near(a3), phi_own, mask_own, halo,
+            w1s, w2bs, conds,
         )
 
         fix = jax.ShapeDtypeStruct((4 * chans, 128), F32)
@@ -552,7 +698,7 @@
             scratch_shapes=[pltpu.VMEM((2 * count, 128), F32)],
             compiler_params=limit(8),
             name="edge_parts",
-        )(ca, cb, own, w1f, w2b, w2f, w1b, conds, acc1, acc2, cacc)
+        )(ca, cb, own, w1f, w2b, w2f, w1b, conds, acc1, acc2, cacc, gphi)
 
         def output(with_phi, src, mid, fix, weights, name):
             return pl.pallas_call(
@@ -562,27 +708,30 @@
                     pltpu.VMEM(((rows + 2) * step, 128), BF),
                     pltpu.VMEM((rows, chans, 128), F32),
                     pltpu.VMEM((chans, rows, 128), F32),
+                    pltpu.VMEM(src.shape, BF),
+                    pltpu.SemaphoreType.DMA(()),
                 ],
+                in_specs=[hbm] + [near] * 6,
                 compiler_params=limit(16),
                 cost_estimate=pl.CostEstimate(
                     flops=2 * flops, bytes_accessed=4 << 20, transcendentals=0
                 ),
                 name=name,
-            )(src, lens_phi, tile_mask, mid, fix, weights, conds)
-
-        w2s, w1s = stacked(w2f, R2, chans), stacked(w1b, R2, chans)
-        moves = [lambda a, b, bit=1 << k: (a ^ bit, b) for k in range(1, ny.bit_length() - 1)]
-        moves += [lambda a, b, bit=1 << k: (a, b ^ bit) for k in range(nx.bit_length() - 1)]
+            )(src, phi_own, mask_own, mid, fix, weights, conds)
+
+        moves = [(1 << k, 0) for k in range(1, ny.bit_length() - 1)]
+        moves += [(0, 1 << k) for k in range(nx.bit_length() - 1)]
+        rounds = [moves[:2]] + [[move] for move in moves[2:]]
         keep = keep + send(give, lambda a, b: (a ^ 1, b))
         outs = []
-        for n, move in enumerate(moves):
+        for n, move in enumerate(rounds):
             if n == 0:
                 keep, hfix = lax.optimization_barrier((keep, hfix))
-                outs.append(output(True, sky, hid, hfix, w2s, "delensed"))
+                outs.append(output(True, far[0], hid, hfix, w2s, "delensed"))
             if n == 1:
                 keep, dfix = lax.optimization_barrier((keep, dfix))
-                outs.append(output(False, cotangent, dpre, dfix, w1s, "grad_input"))
-            keep = keep + send(keep, move)
+                outs.append(output(False, far[1], dpre, dfix, w1bs, "grad_input"))
+            keep = exchange(keep, move)
             if n < 2:
                 keep, outs[n] = lax.optimization_barrier((keep, outs[n]))
         delensed, grad_input = outs

time: 45.6 us -> 41.6 us (0.912)
  local copies, waits for them, and re-layouts: 6.28 us -> 0 us
  Pallas kernels: 12.1 us -> 16.2 us
  waiting for transfers between devices: 8.83 us -> 6.87 us
    unnamed x26 -> x0, local copies, waits for them, and re-layouts: 5.61 us -> none
    pallas_call x2 -> x4, Pallas kernels: 0.95 us -> 5.82 us  [the longest x1 2.59 us: local(): pl.pallas_call(prep_kernel, out_shape=(field, edges, jax.ShapeDtypeStruct...]
    ppermute x10 -> x11, waiting for transfers between devices: 8.83 us -> 6.87 us  [send(): return lax.ppermute(value, axes, pairs)]
    pallas_call x1, Pallas kernels: 4.04 us -> 3.09 us  [local(): pl.pallas_call(hidden_kernel, out_shape=(inner, inner, acc, acc, jax.Shap...]
    ppermute x10 -> x11, starting transfers between devices: 16.8 us -> 17.2 us  [send(): return lax.ppermute(value, axes, pairs)]
  transfers between devices with their start and end apart: 10 -> 11, of which waited for: 5 -> 6; matrix products, arithmetic and copies ran while one was open for 2% -> 0% of each run, Pallas kernels for 20% -> 31%
where the time goes in v4:
time: 41.6 us; the launch traced here: 41.1 us
  starting transfers between devices  17.2 us (41%)
  Pallas kernels  16.2 us (39%)
  waiting for transfers between devices  6.87 us (17%)
  between operations  0.77 us (2%)
    ppermute x11, starting transfers between devices, send(): return lax.ppermute(value, axes, pairs)  17.2 us
    ppermute x11, waiting for transfers between devices, send(): return lax.ppermute(value, axes, pairs)  6.87 us
    pallas_call x2, Pallas kernels, output(): pl.pallas_call(lambda *refs: output_kernel(with_phi, *refs), out_shape=ja...  5.44 us
    pallas_call x1, Pallas kernels, local(): pl.pallas_call(hidden_kernel, out_shape=(inner, inner, acc, acc, jax.Shap...  3.09 us
    pallas_call x1, Pallas kernels, local(): pl.pallas_call(prep_kernel, out_shape=(field, edges, jax.ShapeDtypeStruct...  2.59 us
    pallas_call x1, Pallas kernels, local(): pl.pallas_call(weight_kernel, out_shape=(flat_w, flat_w, flat_w, flat_w,...  1.48 us
    pallas_call x1, Pallas kernels, local(): pl.pallas_call(row_kernel, out_shape=(edge, edge), in_specs=[hbm] * 4, sc...  1.45 us
    pallas_call x1, Pallas kernels, local(): pl.pallas_call(lambda *refs: unpack_kernel(factor, *refs), out_shape=(gra...  1.04 us
  transfers between devices with their start and end apart: 11, of which 6 were waited for; matrix products, arithmetic and copies ran while one was open for 0% of the time, Pallas kernels for 31%

profile of v4, /device:TPU:0, one launch (start us, length us, event | category | flops | bytes accessed | tf_op | source)
XLA Modules:
  0.0 41.1 jit_solution(2903795862715664659)
XLA Ops:
  0.6 1.4 %edge_rows.1 = (bf16[208,128]{1,0:T(8,128)(2,1)S(1)}, bf16[208,128]{1,0:T(8,128)(2,1)S(1)}) custom-call(bf16[48,64,128]{2,1,0:T(8,128)(2,1)} %refs_0_.2, bf16[48,64,128]{2,1,0:T(8,128)(2,1)} %refs_0_.3, bf16[64,128]{1,0:T(8,128)(2,1)} %phi_ref.1, s32[8,16]{1,0:T(8,128)} %mask_ref.1), custom_call_target="tpu_custom_call" | custom-call | tf_op jit(solution)/shard_map/edge_rows/pallas_call | solution.py:602
  2.1 0.5 %collective-permute-start = (bf16[208,128]{1,0:T(8,128)(2,1)S(1)}, bf16[208,128]{1,0:T(8,128)(2,1)S(1)}, u32[]{:S(2)}, u32[]{:S(2)}) collective-permute-start(bf16[208,128]{1,0:T(8,128)(2,1)S(1)} %get-tuple-element.52), channel_id=1, source_target_pairs={{0,8},{1,9},{2,10},{3,11},{4,12},{5,13},{6,14},{7,15},{8,0},{9,1},... | collective-permute-start | bytes 159752 | tf_op jit(solution)/shard_map/ppermute | solution.py:566
  2.6 0.7 %collective-permute-start.1 = (bf16[208,128]{1,0:T(8,128)(2,1)S(1)}, bf16[208,128]{1,0:T(8,128)(2,1)S(1)}, u32[]{:S(2)}, u32[]{:S(2)}) collective-permute-start(bf16[208,128]{1,0:T(8,128)(2,1)S(1)} %get-tuple-element.53), channel_id=1, source_target_pairs={{8,16},{9,17},{10,18},{11,19},{12,20},{13,21},{14,22},{15,23},{16,... | collective-permute-start | bytes 159752 | tf_op jit(solution)/shard_map/ppermute | solution.py:566
  3.3 2.6 %prep.1 = (bf16[2,9216,128]{2,1,0:T(8,128)(2,1)S(1)}, bf16[2,208,128]{2,1,0:T(8,128)(2,1)S(1)}, f32[48,128]{1,0:T(8,128)S(1)}, f32[64,128]{1,0:T(8,128)S(1)}, f32[64,128]{1,0:T(8,128)S(1)}) custom-call(bf16[48,64,128]{2,1,0:T(8,128)(2,1)} %refs_0_.2, bf16[48,64,128]{2,1,0:T(8,128)(2,1)} %refs_0_.3, bf16[64,128]{1,0:T(8,128)(2,1)} %phi_ref.1, s32[8,16]{1,0:T(8,128)} %mask_ref.1), custom_call_target="tpu_custom_call" | custom-call | flops 1358954496 | bytes 8388608 | tf_op jit(solution)/shard_map/prep/pallas_call | solution.py:646
  5.9 1.5 %weights.1 = (bf16[48,432]{1,0:T(8,128)(2,1)S(1)}, bf16[48,432]{1,0:T(8,128)(2,1)S(1)}, bf16[48,432]{1,0:T(8,128)(2,1)S(1)}, bf16[48,432]{1,0:T(8,128)(2,1)S(1)}...) custom-call(bf16[3,3,48,48]{3,2,1,0:T(8,128)(2,1)} %one_hbm, ...), custom_call_target="tpu_custom_call" | custom-call | tf_op jit(solution)/shard_map/weights/pallas_call | solution.py:621
  7.3 0.0 collective-permute-done.refs_1_
  7.4 0.0 collective-permute-done.1.refs_2_
  7.4 0.3 edge_cols.1
  7.7 2.6 %collective-permute-start.2 = (bf16[208,128]{1,0:T(8,128)(2,1)S(1)}, bf16[208,128]{1,0:T(8,128)(2,1)S(1)}, u32[]{:S(2)}, u32[]{:S(2)}) collective-permute-start(bf16[208,128]{1,0:T(8,128)(2,1)S(1)} %get-tuple-element.54), channel_id=1, source_target_pairs={{0,1},{1,0},{2,3},{3,2},{4,5},{5,4},{6,7},{7,6},{8,9},{9,8},{10,11... | collective-permute-start | bytes 159752 | tf_op jit(solution)/shard_map/ppermute | solution.py:566
  10.3 0.7 %collective-permute-start.3 = (bf16[208,128]{1,0:T(8,128)(2,1)S(1)}, bf16[208,128]{1,0:T(8,128)(2,1)S(1)}, u32[]{:S(2)}, u32[]{:S(2)}) collective-permute-start(bf16[208,128]{1,0:T(8,128)(2,1)S(1)} %get-tuple-element.55), channel_id=1, source_target_pairs={{1,2},{2,1},{3,4},{4,3},{5,6},{6,5},{9,10},{10,9},{11,12},{12,11},... | collective-permute-start | bytes 159752 | tf_op jit(solution)/shard_map/ppermute | solution.py:566
  10.9 3.1 %hidden.1 = (bf16[3168,128]{1,0:T(8,128)(2,1)S(1)}, bf16[3168,128]{1,0:T(8,128)(2,1)S(1)}, f32[144,144]{1,0:T(8,128)S(1)}, f32[144,144]{1,0:T(8,128)S(1)}, f32[2,48,128]{2,1,0:T(8,128)S(1)}) custom-call(bf16[2,9216,128]{2,1,0:T(8,128)(2,1)S(1)} %get-tuple-element.64.a3, f32[64,128]{1,0:T(8,128)S(1)} %get-tuple-element.65.phi_own.refs_1_, ...), custom_call_target="tpu_custom_call" | custom-call | flops 2717908992 | bytes 8388608 | tf_op jit(solution)/shard_map/hidden/pallas_call | solution.py:676
  14.0 0.0 collective-permute-done.2.refs_0_
  14.1 0.0 collective-permute-done.3.refs_1_
  14.1 0.9 %edge_parts.1 = (f32[192,128]{1,0:T(8,128)S(1)}, f32[192,128]{1,0:T(8,128)S(1)}, f32[168,128]{1,0:T(8,128)S(1)}, f32[168,128]{1,0:T(8,128)S(1)}) custom-call(bf16[208,128]{1,0:T(8,128)(2,1)S(1)} %collective-permute-done.2.refs_0_, bf16[208,128]{1,0:T(8,128)(2,1)S(1)} %collective-permute-done.3.refs_1_, bf16[2,208,128]{2,1,0:T(8,128)(2,1)S(1)} %get-tuple-element.56.refs_2_, ...), custom_call_target="tpu_custom_call" | custom-call | tf_op jit(solution)/shard_map/edge_parts/pallas_call | solution.py:695
  14.9 2.6 %collective-permute-start.4 = (f32[168,128]{1,0:T(8,128)S(1)}, f32[168,128]{1,0:T(8,128)S(1)}, u32[]{:S(2)}, u32[]{:S(2)}) collective-permute-start(f32[168,128]{1,0:T(8,128)S(1)} %get-tuple-element.75), channel_id=1, source_target_pairs={{0,8},{1,9},{2,10},{3,11},{4,12},{5,13},{6,14},{7,15},{8,0},{9,1},... | collective-permute-start | bytes 258056 | tf_op jit(solution)/shard_map/ppermute | solution.py:566
  17.6 0.9 %collective-permute-done.4 = f32[168,128]{1,0:T(8,128)S(1)} collective-permute-done((f32[168,128]{1,0:T(8,128)S(1)}, f32[168,128]{1,0:T(8,128)S(1)}, u32[]{:S(2)}, u32[]{:S(2)}) %collective-permute-start.4) | collective-permute-done | bytes 86048 | tf_op jit(solution)/shard_map/ppermute | solution.py:566
  18.5 4.9 %collective-permute-start.7 = (f32[168,128]{1,0:T(8,128)S(1)}, f32[168,128]{1,0:T(8,128)S(1)}, u32[]{:S(2)}, u32[]{:S(2)}) collective-permute-start(f32[168,128]{1,0:T(8,128)S(1)} %add.18), channel_id=1, source_target_pairs={{0,17},{1,16},{2,19},{3,18},{4,21},{5,20},{6,23},{7,22},{8,25},{9,... | collective-permute-start | bytes 258056 | tf_op jit(solution)/shard_map/ppermute | solution.py:566
  23.4 0.0 collective-permute-start.6
  23.4 0.6 %collective-permute-start.5 = (f32[168,128]{1,0:T(8,128)S(1)}, f32[168,128]{1,0:T(8,128)S(1)}, u32[]{:S(2)}, u32[]{:S(2)}) collective-permute-start(f32[168,128]{1,0:T(8,128)S(1)} %add.18), channel_id=1, source_target_pairs={{0,16},{1,17},{2,18},{3,19},{4,20},{5,21},{6,22},{7,23},{8,24},{9,... | collective-permute-start | bytes 258056 | tf_op jit(solution)/shard_map/ppermute | solution.py:566
  24.1 2.7 %delensed.1 = bf16[48,64,128]{2,1,0:T(8,128)(2,1)} custom-call(bf16[48,64,128]{2,1,0:T(8,128)(2,1)} %refs_0_.2, f32[64,128]{1,0:T(8,128)S(1)} %get-tuple-element.65.phi_own.refs_1_, f32[64,128]{1,0:T(8,128)S(1)} %get-tuple-element.66.mask_own.refs_2_, bf16[3168,128]{1,0:T(8,128)(2,1)S(1)} %get-tuple-element.78.refs_3_, ...), custom_call_target="tpu_custom_call" | custom-call | flops 679477248 | bytes 4194304 | tf_op jit(solution)/shard_map/delensed/pallas_call | solution.py:704
  26.8 0.0 collective-permute-done.7
  26.8 1.3 %collective-permute-done.6 = f32[168,128]{1,0:T(8,128)S(1)} collective-permute-done((f32[168,128]{1,0:T(8,128)S(1)}, f32[168,128]{1,0:T(8,128)S(1)}, u32[]{:S(2)}, u32[]{:S(2)}) %collective-permute-start.6) | collective-permute-done | bytes 86048 | tf_op jit(solution)/shard_map/ppermute | solution.py:566
  28.1 0.6 %collective-permute-done.5 = f32[168,128]{1,0:T(8,128)S(1)} collective-permute-done((f32[168,128]{1,0:T(8,128)S(1)}, f32[168,128]{1,0:T(8,128)S(1)}, u32[]{:S(2)}, u32[]{:S(2)}) %collective-permute-start.5) | collective-permute-done | bytes 86048 | tf_op jit(solution)/shard_map/ppermute | solution.py:566
  28.7 1.7 %collective-permute-start.8 = (f32[168,128]{1,0:T(8,128)S(1)}, f32[168,128]{1,0:T(8,128)S(1)}, u32[]{:S(2)}, u32[]{:S(2)}) collective-permute-start(f32[168,128]{1,0:T(8,128)S(1)} %add_add_fusion), channel_id=1, source_target_pairs={{0,2},{1,3},{2,0},{3,1},{4,6},{5,7},{6,4},{7,5},{8,10},{9,11},{10,... | collective-permute-start | bytes 258056 | tf_op jit(solution)/shard_map/ppermute | solution.py:566
  30.5 2.7 %grad_input.1 = bf16[48,64,128]{2,1,0:T(8,128)(2,1)} custom-call(bf16[48,64,128]{2,1,0:T(8,128)(2,1)} %refs_0_.3, f32[64,128]{1,0:T(8,128)S(1)} %get-tuple-element.65.phi_own.refs_1_, f32[64,128]{1,0:T(8,128)S(1)} %get-tuple-element.66.mask_own.refs_2_, bf16[3168,128]{1,0:T(8,128)(2,1)S(1)} %get-tuple-element.85.refs_3_, ...), custom_call_target="tpu_custom_call" | custom-call | flops 679477248 | bytes 4194304 | tf_op jit(solution)/shard_map/grad_input/pallas_call | solution.py:704
  33.2 0.1 collective-permute-done.8
  33.3 2.8 %collective-permute-start.9 = (f32[168,128]{1,0:T(8,128)S(1)}, f32[168,128]{1,0:T(8,128)S(1)}, u32[]{:S(2)}, u32[]{:S(2)}) collective-permute-start(f32[168,128]{1,0:T(8,128)S(1)} %add.22), channel_id=1, source_target_pairs={{0,4},{1,5},{2,6},{3,7},{4,0},{5,1},{6,2},{7,3},{8,12},{9,13},{10,... | collective-permute-start | bytes 258056 | tf_op jit(solution)/shard_map/ppermute | solution.py:566
  36.0 2.7 %collective-permute-done.9 = f32[168,128]{1,0:T(8,128)S(1)} collective-permute-done((f32[168,128]{1,0:T(8,128)S(1)}, f32[168,128]{1,0:T(8,128)S(1)}, u32[]{:S(2)}, u32[]{:S(2)}) %collective-permute-start.9) | collective-permute-done | bytes 86048 | tf_op jit(solution)/shard_map/ppermute | solution.py:566
  38.8 0.1 collective-permute-start.10
  38.8 1.3 %collective-permute-done.10.refs_1_ = f32[168,128]{1,0:T(8,128)S(1)} collective-permute-done((f32[168,128]{1,0:T(8,128)S(1)}, f32[168,128]{1,0:T(8,128)S(1)}, u32[]{:S(2)}, u32[]{:S(2)}) %collective-permute-start.10) | collective-permute-done | bytes 86048 | tf_op jit(solution)/shard_map/ppermute | solution.py:566
  40.1 1.0 %unpack.1 = (f32[3,3,48,48]{3,2,1,0:T(8,128)}, f32[3,3,48,48]{3,2,1,0:T(8,128)}, f32[3,48]{1,0:T(4,128)}) custom-call(f32[168,128]{1,0:T(8,128)S(1)} %add.23.refs_0_, f32[168,128]{1,0:T(8,128)S(1)} %collective-permute-done.10.refs_1_), custom_call_target="tpu_custom_call" | custom-call | tf_op jit(solution)/shard_map/unpack/pallas_call | solution.py:742
  (4 shorter events, 0.1 us)
Async XLA Ops:
  2.1 5.3 %collective-permute-start = (bf16[208,128]{1,0:T(8,128)(2,1)S(1)}, bf16[208,128]{1,0:T(8,128)(2,1)S(1)}, u32[]{:S(2)}, u32[]{:S(2)}) collective-permute-start(bf16[208,128]{1,0:T(8,128)(2,1)S(1)} %get-tuple-element.52), channel_id=1, source_target_pairs={{0,8},{1,9},{2,10},{3,11},{4,12},{5,13},{6,14},{7,15},{8,0},{9,1},... | collective-permute-start | bytes 159752 | tf_op jit(solution)/shard_map/ppermute | solution.py:566
  2.6 4.8 %collective-permute-start.1 = (bf16[208,128]{1,0:T(8,128)(2,1)S(1)}, bf16[208,128]{1,0:T(8,128)(2,1)S(1)}, u32[]{:S(2)}, u32[]{:S(2)}) collective-permute-start(bf16[208,128]{1,0:T(8,128)(2,1)S(1)} %get-tuple-element.53), channel_id=1, source_target_pairs={{8,16},{9,17},{10,18},{11,19},{12,20},{13,21},{14,22},{15,23},{16,... | collective-permute-start | bytes 159752 | tf_op jit(solution)/shard_map/ppermute | solution.py:566
  7.7 6.4 %collective-permute-start.2 = (bf16[208,128]{1,0:T(8,128)(2,1)S(1)}, bf16[208,128]{1,0:T(8,128)(2,1)S(1)}, u32[]{:S(2)}, u32[]{:S(2)}) collective-permute-start(bf16[208,128]{1,0:T(8,128)(2,1)S(1)} %get-tuple-element.54), channel_id=1, source_target_pairs={{0,1},{1,0},{2,3},{3,2},{4,5},{5,4},{6,7},{7,6},{8,9},{9,8},{10,11... | collective-permute-start | bytes 159752 | tf_op jit(solution)/shard_map/ppermute | solution.py:566
  10.3 3.8 %collective-permute-start.3 = (bf16[208,128]{1,0:T(8,128)(2,1)S(1)}, bf16[208,128]{1,0:T(8,128)(2,1)S(1)}, u32[]{:S(2)}, u32[]{:S(2)}) collective-permute-start(bf16[208,128]{1,0:T(8,128)(2,1)S(1)} %get-tuple-element.55), channel_id=1, source_target_pairs={{1,2},{2,1},{3,4},{4,3},{5,6},{6,5},{9,10},{10,9},{11,12},{12,11},... | collective-permute-start | bytes 159752 | tf_op jit(solution)/shard_map/ppermute | solution.py:566
  14.9 3.6 %collective-permute-start.4 = (f32[168,128]{1,0:T(8,128)S(1)}, f32[168,128]{1,0:T(8,128)S(1)}, u32[]{:S(2)}, u32[]{:S(2)}) collective-permute-start(f32[168,128]{1,0:T(8,128)S(1)} %get-tuple-element.75), channel_id=1, source_target_pairs={{0,8},{1,9},{2,10},{3,11},{4,12},{5,13},{6,14},{7,15},{8,0},{9,1},... | collective-permute-start | bytes 258056 | tf_op jit(solution)/shard_map/ppermute | solution.py:566
  18.5 8.3 %collective-permute-start.7 = (f32[168,128]{1,0:T(8,128)S(1)}, f32[168,128]{1,0:T(8,128)S(1)}, u32[]{:S(2)}, u32[]{:S(2)}) collective-permute-start(f32[168,128]{1,0:T(8,128)S(1)} %add.18), channel_id=1, source_target_pairs={{0,17},{1,16},{2,19},{3,18},{4,21},{5,20},{6,23},{7,22},{8,25},{9,... | collective-permute-start | bytes 258056 | tf_op jit(solution)/shard_map/ppermute | solution.py:566
  23.4 4.7 %collective-permute-start.6 = (f32[168,128]{1,0:T(8,128)S(1)}, f32[168,128]{1,0:T(8,128)S(1)}, u32[]{:S(2)}, u32[]{:S(2)}) collective-permute-start(f32[168,128]{1,0:T(8,128)S(1)} %add.18), channel_id=1, source_target_pairs={{0,1},{1,0},{2,3},{3,2},{4,5},{5,4},{6,7},{7,6},{8,9},{9,8},{10,11... | collective-permute-start | bytes 258056 | tf_op jit(solution)/shard_map/ppermute | solution.py:566
  23.4 5.3 %collective-permute-start.5 = (f32[168,128]{1,0:T(8,128)S(1)}, f32[168,128]{1,0:T(8,128)S(1)}, u32[]{:S(2)}, u32[]{:S(2)}) collective-permute-start(f32[168,128]{1,0:T(8,128)S(1)} %add.18), channel_id=1, source_target_pairs={{0,16},{1,17},{2,18},{3,19},{4,20},{5,21},{6,22},{7,23},{8,24},{9,... | collective-permute-start | bytes 258056 | tf_op jit(solution)/shard_map/ppermute | solution.py:566
  28.7 4.6 %collective-permute-start.8 = (f32[168,128]{1,0:T(8,128)S(1)}, f32[168,128]{1,0:T(8,128)S(1)}, u32[]{:S(2)}, u32[]{:S(2)}) collective-permute-start(f32[168,128]{1,0:T(8,128)S(1)} %add_add_fusion), channel_id=1, source_target_pairs={{0,2},{1,3},{2,0},{3,1},{4,6},{5,7},{6,4},{7,5},{8,10},{9,11},{10,... | collective-permute-start | bytes 258056 | tf_op jit(solution)/shard_map/ppermute | solution.py:566
  33.3 5.4 %collective-permute-start.9 = (f32[168,128]{1,0:T(8,128)S(1)}, f32[168,128]{1,0:T(8,128)S(1)}, u32[]{:S(2)}, u32[]{:S(2)}) collective-permute-start(f32[168,128]{1,0:T(8,128)S(1)} %add.22), channel_id=1, source_target_pairs={{0,4},{1,5},{2,6},{3,7},{4,0},{5,1},{6,2},{7,3},{8,12},{9,13},{10,... | collective-permute-start | bytes 258056 | tf_op jit(solution)/shard_map/ppermute | solution.py:566
  38.8 1.3 %collective-permute-start.10 = (f32[168,128]{1,0:T(8,128)S(1)}, f32[168,128]{1,0:T(8,128)S(1)}, u32[]{:S(2)}, u32[]{:S(2)}) collective-permute-start(f32[168,128]{1,0:T(8,128)S(1)} %add.23.refs_0_), channel_id=1, source_target_pairs={{0,8},{1,9},{2,10},{3,11},{4,12},{5,13},{6,14},{7,15},{8,0},{9,1},... | collective-permute-start | bytes 258056 | tf_op jit(solution)/shard_map/ppermute | solution.py:566

commit v5 on v4

--- a/solution.py
+++ b/solution.py
@@ -33,6 +33,14 @@
 
 def is_odd(axis):
     return lax.rem(lax.axis_index(axis), 2) == 1
+
+
+def received(axis, count, a_ref, b_ref):
+    ends = (lax.axis_index(axis) == 0) | (lax.axis_index(axis) == count - 1)
+    ra = a_ref[...]
+    rb = jnp.where(ends, jnp.zeros_like(ra), b_ref[...])
+    odd = is_odd(axis)
+    return jnp.where(odd, ra, rb), jnp.where(odd, rb, ra)
 
 
 def row_kernel(sky_ref, cot_ref, phi_ref, mask_ref, a_ref, b_ref, blocks, phis, tiles, sems):
@@ -72,24 +80,30 @@
     b_ref[...] = jnp.where(odd, down, up)
 
 
-def prep_kernel(
-    sky_hbm, cot_hbm, phi_hbm, mask_hbm, a3, own_ref, gphi_ref, phix, maskx,
-    strip, sky_ref, cot_ref, phi_ref, mask_ref, sems,
+def prep_kernel(*refs):
+    far, (a3, own_ref, gphi_ref, phix, maskx), mats = refs[:9], refs[9:14], refs[14:23]
+    strip, near, sems = refs[23], refs[24:33], refs[33]
+    copies = {
+        n: pltpu.make_async_copy(far[n], near[n], sems.at[n])
+        for n in (3, 2, 4, 5, 6, 7, 8, 0, 1)
+    }
+    for copy in copies.values():
+        copy.start()
+    for n in (3, 2, 4, 5, 6, 7, 8):
+        copies[n].wait()
+    weight_matrices(*near[4:], *mats)
+    copies[0].wait()
+    copies[1].wait()
+    own_fields(*near[:4], a3, own_ref, gphi_ref, phix, maskx, strip)
+
+
+def own_fields(
+    sky_ref, cot_ref, phi_ref, mask_ref, a3, own_ref, gphi_ref, phix, maskx, strip
 ):
     chans, rows, width = sky_ref.shape
     size = own_ref.shape[1]
     step = 3 * chans
     half = chans // 2
-    copies = [
-        pltpu.make_async_copy(src, dst, sems.at[n])
-        for n, (src, dst) in enumerate(
-            ((mask_hbm, mask_ref), (phi_hbm, phi_ref), (sky_hbm, sky_ref), (cot_hbm, cot_ref))
-        )
-    ]
-    for copy in copies:
-        copy.start()
-    copies[0].wait()
-    copies[1].wait()
     cells = tile_rows(mask_ref)
     phi = phi_ref[...].astype(F32)
     phix[...] = phi
@@ -119,7 +133,6 @@
     phis = jnp.concatenate([phis, jnp.zeros((8, 128 - rows), F32)], axis=1)
     gphi = jnp.zeros((chans, 128), F32)
     for which, src in ((0, sky_ref), (1, cot_ref)):
-        copies[2 + which].wait()
         both = jnp.concatenate([src[:half], src[half:]], axis=1).reshape(half * 128, width)
         flat = lax.dot_general(pick, both, NT, preferred_element_type=F32)
         for j in range(half):
@@ -154,12 +167,9 @@
     return jnp.concatenate([pltpu.roll(value, 1, 1), value, pltpu.roll(value, 127, 1)], axis=0)
 
 
-def col_kernel(rows, width, mine_ref, a_ref, b_ref, sa_ref, sb_ref, own_ref, halo_ref):
+def col_kernel(rows, width, count, mine_ref, a_ref, b_ref, sa_ref, sb_ref, own_ref, halo_ref):
     size = a_ref.shape[0]
-    odd = is_odd("gy")
-    ra, rb = a_ref[...], b_ref[...]
-    tops = jnp.where(odd, ra, rb)
-    bots = jnp.where(odd, rb, ra)
+    tops, bots = received("gy", count, a_ref, b_ref)
     halo_ref[0] = tops
     halo_ref[1] = bots
     chans = (size - 16) // 4
@@ -303,17 +313,14 @@
 
 
 def edge_kernel(
-    rows, a_ref, b_ref, own_ref, w1c_ref, w2tc_ref, w2c_ref, w1tc_ref, cond_ref,
+    rows, count, a_ref, b_ref, own_ref, w1c_ref, w2tc_ref, cond_ref,
     acc1, acc2, cacc, gphi_ref,
-    hfix_ref, dfix_ref, keep_ref, give_ref, wire,
+    hcol_ref, dcol_ref, keep_ref, give_ref, wire,
 ):
     size = a_ref.shape[0]
     chans = (size - 16) // 4
     step = 3 * chans
-    odd = is_odd("gx")
-    ra, rb = a_ref[...], b_ref[...]
-    lft = jnp.where(odd, ra, rb)
-    rgt = jnp.where(odd, rb, ra)
+    lft, rgt = received("gx", count, a_ref, b_ref)
     own_l, own_r = own_ref[0], own_ref[1]
 
     def at(value, which, n):
@@ -343,6 +350,8 @@
     act, slope = silu_parts(pre + cond_ref[:, 0:1] * phi_c + cond_ref[:, 1:2])
     hcol = (act * mask_c).astype(BF)
     dcol = (back * mask_c * slope).astype(BF)
+    hcol_ref[...] = hcol
+    dcol_ref[...] = dcol
 
     mine = jnp.broadcast_to((lane_iota(1) < rows).astype(F32), (chans, 128)).astype(BF)
     d_own = [dcol[:, 128:256] * mine, dcol[:, 256:384] * mine]
@@ -387,10 +396,18 @@
     sums = [jnp.sum(v, axis=1, keepdims=True) for v in (dphi, dsum, gphi_ref[...])]
     fill = jnp.zeros((chans, 128 - 3 * tails[0].shape[1] - 3), F32)
     wire[2 * step : 2 * step + chans] = jnp.concatenate(tails + sums + [fill], axis=1)
+    half = wire.shape[0] // 2
+    core = lax.rem(lax.axis_index("gy"), 2)
+    keep_ref[...] = wire[pl.ds(pl.multiple_of(core * half, 8), half), :]
+    give_ref[...] = wire[pl.ds(pl.multiple_of((1 - core) * half, 8), half), :]
+
+
+def fix_kernel(rows, w2c_ref, w1tc_ref, hcol_ref, dcol_ref, hfix_ref, dfix_ref):
+    chans = hcol_ref.shape[0]
     none = jnp.zeros((chans, 128), BF)
     half = chans // 2
     lane = lane_iota(half)
-    for weights, field, fix in ((w2c_ref, hcol, hfix_ref), (w1tc_ref, dcol, dfix_ref)):
+    for weights, field, fix in ((w2c_ref, hcol_ref, hfix_ref), (w1tc_ref, dcol_ref, dfix_ref)):
         f = [field[:, 128 * k : 128 * k + 128] for k in range(4)]
         pieces = []
         for ky in range(3):
@@ -407,11 +424,6 @@
             high = part.astype(BF).astype(F32)
             fix[pl.ds(k, half, stride=8), :] = high
             fix[pl.ds(4 + k, half, stride=8), :] = part - high
-
-    count = wire.shape[0] // 2
-    core = lax.rem(lax.axis_index("gy"), 2)
-    keep_ref[...] = wire[pl.ds(pl.multiple_of(core * count, 8), count), :]
-    give_ref[...] = wire[pl.ds(pl.multiple_of((1 - core) * count, 8), count), :]
 
 
 def output_kernel(
@@ -514,21 +526,10 @@
     return jnp.concatenate(rows, axis=0)
 
 
-def weight_kernel(
-    one_hbm, two_hbm, c1_hbm, b1_hbm, c2_hbm,
+def weight_matrices(
+    one, two, vec0, vec1, vec2,
     w1f_ref, w2b_ref, w2f_ref, w1b_ref, w1s_ref, w2bs_ref, w2s_ref, w1bs_ref, cond_ref,
-    one, two, vec0, vec1, vec2, sems,
 ):
-    copies = [
-        pltpu.make_async_copy(src, dst, sems.at[n])
-        for n, (src, dst) in enumerate(
-            ((one_hbm, one), (two_hbm, two), (c1_hbm, vec0), (b1_hbm, vec1), (c2_hbm, vec2))
-        )
-    ]
-    for copy in copies:
-        copy.start()
-    for copy in copies:
-        copy.wait()
     chans = one.shape[2]
     for src, fwd, fwd_s, count, bwd, bwd_s, back in (
         (one, w1f_ref, w1s_ref, R1, w1b_ref, w1bs_ref, R2),
@@ -561,8 +562,7 @@
         for a in range(ny):
             for b in range(nx):
                 to = move(a, b)
-                if 0 <= to[0] < ny and 0 <= to[1] < nx:
-                    pairs.append((a * nx + b, to[0] * nx + to[1]))
+                pairs.append((a * nx + b, to[0] * nx + to[1]))
         return lax.ppermute(value, axes, pairs)
 
     def swap(first, second, axis):
@@ -570,7 +570,9 @@
             def move(a, b):
                 v = [a, b]
                 v[axis] += 1 if (v[axis] + offset) % 2 == 0 else -1
-                return v
+                if 0 <= v[axis] < (ny, nx)[axis]:
+                    return v
+                return (a, b ^ 1) if axis == 0 else (a ^ 1, b)
 
             return move
 
@@ -594,11 +596,14 @@
         edge = jax.ShapeDtypeStruct((size, 128), BF)
         edges = jax.ShapeDtypeStruct((2, size, 128), BF)
         hbm = pl.BlockSpec(memory_space=pltpu.HBM)
-        near = pl.BlockSpec(memory_space=pltpu.VMEM)
         far = [
             pltpu.with_memory_space_constraint(v, pltpu.HBM)
-            for v in (sky, cotangent, lens_phi, tile_mask)
+            for v in (
+                sky, cotangent, lens_phi, tile_mask,
+                weight_one, weight_two, cond_one, bias_one, cond_two,
+            )
         ]
+        vmem = pl.BlockSpec(memory_space=pltpu.VMEM)
         ra, rb = pl.pallas_call(
             row_kernel,
             out_shape=(edge, edge),
@@ -611,58 +616,36 @@
             ],
             compiler_params=limit(8),
             name="edge_rows",
-        )(*far)
-        ra, rb, weight_one, weight_two = lax.optimization_barrier((ra, rb, weight_one, weight_two))
+        )(*far[:4])
         ra, rb = swap(ra, rb, 0)
 
         flat_w = jax.ShapeDtypeStruct((chans, 3 * step), BF)
         first_w = jax.ShapeDtypeStruct((R1 * chans, (R1 + 2) * step), BF)
         second_w = jax.ShapeDtypeStruct((R2 * chans, (R2 + 2) * step), BF)
-        w1f, w2b, w2f, w1b, w1s, w2bs, w2s, w1bs, conds = pl.pallas_call(
-            weight_kernel,
-            out_shape=(
-                flat_w, flat_w, flat_w, flat_w, first_w, first_w, second_w, second_w,
-                jax.ShapeDtypeStruct((chans, 128), F32),
-            ),
-            in_specs=[hbm] * 5,
-            scratch_shapes=[
-                pltpu.VMEM(weight_one.shape, BF),
-                pltpu.VMEM(weight_two.shape, BF),
-                pltpu.VMEM((chans,), F32),
-                pltpu.VMEM((chans,), F32),
-                pltpu.VMEM((chans,), F32),
-                pltpu.SemaphoreType.DMA((5,)),
-            ],
-            compiler_params=limit(8),
-            name="weights",
-        )(*[
-            pltpu.with_memory_space_constraint(v, pltpu.HBM)
-            for v in (weight_one, weight_two, cond_one, bias_one, cond_two)
-        ])
-
+        matrices = (
+            flat_w, flat_w, flat_w, flat_w, first_w, first_w, second_w, second_w,
+            jax.ShapeDtypeStruct((chans, 128), F32),
+        )
         flops = 2 * 9 * chans * chans * rows * width
         field = jax.ShapeDtypeStruct((2, rows * step, 128), BF)
         flat = jax.ShapeDtypeStruct(lens_phi.shape, F32)
-        a3, mine, gphi, phi_own, mask_own = pl.pallas_call(
+        a3, mine, gphi, phi_own, mask_own, *matrices = pl.pallas_call(
             prep_kernel,
-            out_shape=(field, edges, jax.ShapeDtypeStruct((chans, 128), F32), flat, flat),
-            in_specs=[hbm] * 4,
-            scratch_shapes=[
-                pltpu.VMEM((2, 8 * chans // 2, 128), F32),
-                pltpu.VMEM(sky.shape, BF),
-                pltpu.VMEM(sky.shape, BF),
-                pltpu.VMEM(lens_phi.shape, BF),
-                pltpu.VMEM(tile_mask.shape, jnp.int32),
-                pltpu.SemaphoreType.DMA((4,)),
-            ],
+            out_shape=(field, edges, jax.ShapeDtypeStruct((chans, 128), F32), flat, flat)
+            + matrices,
+            in_specs=[hbm] * 9,
+            scratch_shapes=[pltpu.VMEM((2, 8 * chans // 2, 128), F32)]
+            + [pltpu.VMEM(v.shape, v.dtype) for v in far]
+            + [pltpu.SemaphoreType.DMA((9,))],
             compiler_params=limit(8),
             cost_estimate=pl.CostEstimate(
                 flops=4 * flops, bytes_accessed=8 << 20, transcendentals=0
             ),
             name="prep",
         )(*far)
+        w1f, w2b, w2f, w1b, w1s, w2bs, w2s, w1bs, conds = matrices
         ca, cb, own, halo = pl.pallas_call(
-            lambda *refs: col_kernel(rows, width, *refs),
+            lambda *refs: col_kernel(rows, width, ny, *refs),
             out_shape=(edge, edge, edges, edges),
             compiler_params=limit(8),
             name="edge_cols",
@@ -692,13 +675,23 @@
         fix = jax.ShapeDtypeStruct((4 * chans, 128), F32)
         count = (2 * step + chans) // 2
         wires = jax.ShapeDtypeStruct((count, 128), F32)
-        hfix, dfix, keep, give = pl.pallas_call(
-            lambda *refs: edge_kernel(rows, *refs),
-            out_shape=(fix, fix, wires, wires),
+        cols = jax.ShapeDtypeStruct((chans, 512), BF)
+        hcol, dcol, keep, give = pl.pallas_call(
+            lambda *refs: edge_kernel(rows, nx, *refs),
+            out_shape=(cols, cols, wires, wires),
             scratch_shapes=[pltpu.VMEM((2 * count, 128), F32)],
             compiler_params=limit(8),
             name="edge_parts",
-        )(ca, cb, own, w1f, w2b, w2f, w1b, conds, acc1, acc2, cacc, gphi)
+        )(ca, cb, own, w1f, w2b, conds, acc1, acc2, cacc, gphi)
+        hfix, dfix = pl.pallas_call(
+            lambda *refs: fix_kernel(rows, *refs),
+            out_shape=(fix, fix),
+            compiler_params=limit(8),
+            cost_estimate=pl.CostEstimate(
+                flops=flops // 2, bytes_accessed=1 << 20, transcendentals=0
+            ),
+            name="edge_fixes",
+        )(w2f, w1b, hcol, dcol)
 
         def output(with_phi, src, mid, fix, weights, name):
             return pl.pallas_call(
@@ -711,7 +704,7 @@
                     pltpu.VMEM(src.shape, BF),
                     pltpu.SemaphoreType.DMA(()),
                 ],
-                in_specs=[hbm] + [near] * 6,
+                in_specs=[hbm] + [vmem] * 6,
                 compiler_params=limit(16),
                 cost_estimate=pl.CostEstimate(
                     flops=2 * flops, bytes_accessed=4 << 20, transcendentals=0

time: 41.6 us -> 38.3 us (0.921)
  starting transfers between devices: 17.2 us -> 14.1 us
  waiting for transfers between devices: 6.87 us -> 7.75 us
  Pallas kernels: 16.2 us -> 15.5 us
    ppermute x11, starting transfers between devices: 17.2 us -> 14.1 us  [send(): return lax.ppermute(value, axes, pairs)]
    pallas_call x3, Pallas kernels: 2.64 us -> 1.5 us  [the longest x1 0.8 us: local(): pl.pallas_call(lambda *refs: edge_kernel(rows, nx, *refs), out_shape=(col...]
    ppermute x11, waiting for transfers between devices: 6.87 us -> 7.75 us  [send(): return lax.ppermute(value, axes, pairs)]
    pallas_call x1, Pallas kernels: 2.59 us -> 3 us  [local(): pl.pallas_call(prep_kernel, out_shape=(field, edges, jax.ShapeDtypeStruct...]
  transfers between devices with their start and end apart: 11 -> 11, of which waited for: 6 -> 5; matrix products, arithmetic and copies ran while one was open for 0% -> 0% of each run, Pallas kernels for 31% -> 31%
where the time goes in v5:
time: 38.3 us; the launch traced here: 38.1 us
  Pallas kernels  15.5 us (40%)
  starting transfers between devices  14.1 us (37%)
  waiting for transfers between devices  7.75 us (20%)
  between operations  0.76 us (2%)
    ppermute x11, starting transfers between devices, send(): return lax.ppermute(value, axes, pairs)  14.1 us
    ppermute x11, waiting for transfers between devices, send(): return lax.ppermute(value, axes, pairs)  7.75 us
    pallas_call x2, Pallas kernels, output(): pl.pallas_call(lambda *refs: output_kernel(with_phi, *refs), out_shape=ja...  5.44 us
    pallas_call x1, Pallas kernels, local(): pl.pallas_call(hidden_kernel, out_shape=(inner, inner, acc, acc, jax.Shap...  3.06 us
    pallas_call x1, Pallas kernels, local(): pl.pallas_call(prep_kernel, out_shape=(field, edges, jax.ShapeDtypeStruct...  3 us
    pallas_call x1, Pallas kernels, local(): pl.pallas_call(row_kernel, out_shape=(edge, edge), in_specs=[hbm] * 4, sc...  1.45 us
    pallas_call x1, Pallas kernels, local(): pl.pallas_call(lambda *refs: unpack_kernel(factor, *refs), out_shape=(gra...  1.04 us
    pallas_call x1, Pallas kernels, local(): pl.pallas_call(lambda *refs: edge_kernel(rows, nx, *refs), out_shape=(col...  0.8 us
  transfers between devices with their start and end apart: 11, of which 5 were waited for; matrix products, arithmetic and copies ran while one was open for 0% of the time, Pallas kernels for 31%

profile of v5, /device:TPU:0, one launch (start us, length us, event | category | flops | bytes accessed | tf_op | source)
XLA Modules:
  0.0 38.1 jit_solution(6448969576579154052)
XLA Ops:
  0.6 1.4 %edge_rows.1 = (bf16[208,128]{1,0:T(8,128)(2,1)S(1)}, bf16[208,128]{1,0:T(8,128)(2,1)S(1)}) custom-call(bf16[48,64,128]{2,1,0:T(8,128)(2,1)} %refs_0_.4, bf16[48,64,128]{2,1,0:T(8,128)(2,1)} %refs_0_.5, bf16[64,128]{1,0:T(8,128)(2,1)} %phi_ref.1, s32[8,16]{1,0:T(8,128)} %mask_ref.1), custom_call_target="tpu_custom_call" | custom-call | tf_op jit(solution)/shard_map/edge_rows/pallas_call | solution.py:607
  2.1 0.5 %collective-permute-start = (bf16[208,128]{1,0:T(8,128)(2,1)S(1)}, bf16[208,128]{1,0:T(8,128)(2,1)S(1)}, u32[]{:S(2)}, u32[]{:S(2)}) collective-permute-start(bf16[208,128]{1,0:T(8,128)(2,1)S(1)} %get-tuple-element.48), channel_id=1, source_target_pairs={{0,8},{1,9},{2,10},{3,11},{4,12},{5,13},{6,14},{7,15},{8,0},{9,1},... | collective-permute-start | bytes 159752 | tf_op jit(solution)/shard_map/ppermute | solution.py:566
  2.6 2.6 %collective-permute-start.1 = (bf16[208,128]{1,0:T(8,128)(2,1)S(1)}, bf16[208,128]{1,0:T(8,128)(2,1)S(1)}, u32[]{:S(2)}, u32[]{:S(2)}) collective-permute-start(bf16[208,128]{1,0:T(8,128)(2,1)S(1)} %get-tuple-element.49), channel_id=1, source_target_pairs={{0,1},{1,0},{2,3},{3,2},{4,5},{5,4},{6,7},{7,6},{8,16},{9,17},{10,... | collective-permute-start | bytes 159752 | tf_op jit(solution)/shard_map/ppermute | solution.py:566
  5.2 3.0 %prep.1 = (bf16[2,9216,128]{2,1,0:T(8,128)(2,1)S(1)}, bf16[2,208,128]{2,1,0:T(8,128)(2,1)S(1)}, f32[48,128]{1,0:T(8,128)S(1)}, f32[64,128]{1,0:T(8,128)S(1)}, f3...) custom-call(bf16[48,64,128]{2,1,0:T(8,128)(2,1)} %refs_0_.4, ...), custom_call_target="tpu_custom_call" | custom-call | flops 1358954496 | bytes 8388608 | tf_op jit(solution)/shard_map/prep/pallas_call | solution.py:632
  8.2 0.0 collective-permute-done.refs_1_
  8.2 0.0 collective-permute-done.1.refs_2_
  8.2 0.3 edge_cols.1
  8.5 1.2 %collective-permute-start.2 = (bf16[208,128]{1,0:T(8,128)(2,1)S(1)}, bf16[208,128]{1,0:T(8,128)(2,1)S(1)}, u32[]{:S(2)}, u32[]{:S(2)}) collective-permute-start(bf16[208,128]{1,0:T(8,128)(2,1)S(1)} %get-tuple-element.50), channel_id=1, source_target_pairs={{0,1},{1,0},{2,3},{3,2},{4,5},{5,4},{6,7},{7,6},{8,9},{9,8},{10,11... | collective-permute-start | bytes 159752 | tf_op jit(solution)/shard_map/ppermute | solution.py:566
  9.7 0.2 collective-permute-start.3
  9.9 3.1 %hidden.1 = (bf16[3168,128]{1,0:T(8,128)(2,1)S(1)}, bf16[3168,128]{1,0:T(8,128)(2,1)S(1)}, f32[144,144]{1,0:T(8,128)S(1)}, f32[144,144]{1,0:T(8,128)S(1)}, f32[2,48,128]{2,1,0:T(8,128)S(1)}) custom-call(bf16[2,9216,128]{2,1,0:T(8,128)(2,1)S(1)} %get-tuple-element.56.a3, f32[64,128]{1,0:T(8,128)S(1)} %get-tuple-element.57.phi_own.refs_1_, ...), custom_call_target="tpu_custom_call" | custom-call | flops 2717908992 | bytes 8388608 | tf_op jit(solution)/shard_map/hidden/pallas_call | solution.py:659
  13.0 0.0 collective-permute-done.2.refs_0_
  13.0 0.0 collective-permute-done.3.refs_1_
  13.0 0.8 %edge_parts.1 = (bf16[48,512]{1,0:T(8,128)(2,1)S(1)}, bf16[48,512]{1,0:T(8,128)(2,1)S(1)}, f32[168,128]{1,0:T(8,128)S(1)}, f32[168,128]{1,0:T(8,128)S(1)}) custom-call(bf16[208,128]{1,0:T(8,128)(2,1)S(1)} %collective-permute-done.2.refs_0_, bf16[208,128]{1,0:T(8,128)(2,1)S(1)} %collective-permute-done.3.refs_1_, ...), custom_call_target="tpu_custom_call" | custom-call | tf_op jit(solution)/shard_map/edge_parts/pallas_call | solution.py:679
  13.8 0.3 collective-permute-start.4
  14.2 0.4 %edge_fixes.1 = (f32[192,128]{1,0:T(8,128)S(1)}, f32[192,128]{1,0:T(8,128)S(1)}) custom-call(bf16[48,432]{1,0:T(8,128)(2,1)S(1)} %get-tuple-element.68.refs_0_, bf16[48,432]{1,0:T(8,128)(2,1)S(1)} %get-tuple-element.69.refs_1_, bf16[48,512]{1,0:T(8,128)(2,1)S(1)} %get-tuple-element.70.refs_2_, bf16[48,512]{1,0:T(8,128)(2,1)S(1)} %get-tuple-element.71.refs_3_), custom_call_target="tpu_custom_call" | custom-call | flops 169869312 | bytes 1048576 | tf_op jit(solution)/shard_map/edge_fixes/pallas_call | solution.py:686
  14.6 0.6 %collective-permute-done.4 = f32[168,128]{1,0:T(8,128)S(1)} collective-permute-done((f32[168,128]{1,0:T(8,128)S(1)}, f32[168,128]{1,0:T(8,128)S(1)}, u32[]{:S(2)}, u32[]{:S(2)}) %collective-permute-start.4) | collective-permute-done | bytes 86048 | tf_op jit(solution)/shard_map/ppermute | solution.py:566
  15.2 3.3 %collective-permute-start.7 = (f32[168,128]{1,0:T(8,128)S(1)}, f32[168,128]{1,0:T(8,128)S(1)}, u32[]{:S(2)}, u32[]{:S(2)}) collective-permute-start(f32[168,128]{1,0:T(8,128)S(1)} %add.18), channel_id=1, source_target_pairs={{0,17},{1,16},{2,19},{3,18},{4,21},{5,20},{6,23},{7,22},{8,25},{9,... | collective-permute-start | bytes 258056 | tf_op jit(solution)/shard_map/ppermute | solution.py:566
  18.5 0.0 collective-permute-start.6
  18.5 1.1 %collective-permute-start.5 = (f32[168,128]{1,0:T(8,128)S(1)}, f32[168,128]{1,0:T(8,128)S(1)}, u32[]{:S(2)}, u32[]{:S(2)}) collective-permute-start(f32[168,128]{1,0:T(8,128)S(1)} %add.18), channel_id=1, source_target_pairs={{0,16},{1,17},{2,18},{3,19},{4,20},{5,21},{6,22},{7,23},{8,24},{9,... | collective-permute-start | bytes 258056 | tf_op jit(solution)/shard_map/ppermute | solution.py:566
  19.5 2.7 %delensed.1 = bf16[48,64,128]{2,1,0:T(8,128)(2,1)} custom-call(bf16[48,64,128]{2,1,0:T(8,128)(2,1)} %refs_0_.4, f32[64,128]{1,0:T(8,128)S(1)} %get-tuple-element.57.phi_own.refs_1_, f32[64,128]{1,0:T(8,128)S(1)} %get-tuple-element.58.mask_own.refs_2_, bf16[3168,128]{1,0:T(8,128)(2,1)S(1)} %get-tuple-element.74.refs_3_, ...), custom_call_target="tpu_custom_call" | custom-call | flops 679477248 | bytes 4194304 | tf_op jit(solution)/shard_map/delensed/pallas_call | solution.py:697
  22.3 0.0 collective-permute-done.7
  22.3 0.9 %collective-permute-done.6 = f32[168,128]{1,0:T(8,128)S(1)} collective-permute-done((f32[168,128]{1,0:T(8,128)S(1)}, f32[168,128]{1,0:T(8,128)S(1)}, u32[]{:S(2)}, u32[]{:S(2)}) %collective-permute-start.6) | collective-permute-done | bytes 86048 | tf_op jit(solution)/shard_map/ppermute | solution.py:566
  23.2 0.8 %collective-permute-done.5 = f32[168,128]{1,0:T(8,128)S(1)} collective-permute-done((f32[168,128]{1,0:T(8,128)S(1)}, f32[168,128]{1,0:T(8,128)S(1)}, u32[]{:S(2)}, u32[]{:S(2)}) %collective-permute-start.5) | collective-permute-done | bytes 86048 | tf_op jit(solution)/shard_map/ppermute | solution.py:566
  24.0 2.0 %collective-permute-start.8 = (f32[168,128]{1,0:T(8,128)S(1)}, f32[168,128]{1,0:T(8,128)S(1)}, u32[]{:S(2)}, u32[]{:S(2)}) collective-permute-start(f32[168,128]{1,0:T(8,128)S(1)} %add_add_fusion), channel_id=1, source_target_pairs={{0,2},{1,3},{2,0},{3,1},{4,6},{5,7},{6,4},{7,5},{8,10},{9,11},{10,... | collective-permute-start | bytes 258056 | tf_op jit(solution)/shard_map/ppermute | solution.py:566
  26.0 2.7 %grad_input.1 = bf16[48,64,128]{2,1,0:T(8,128)(2,1)} custom-call(bf16[48,64,128]{2,1,0:T(8,128)(2,1)} %refs_0_.5, f32[64,128]{1,0:T(8,128)S(1)} %get-tuple-element.57.phi_own.refs_1_, f32[64,128]{1,0:T(8,128)S(1)} %get-tuple-element.58.mask_own.refs_2_, bf16[3168,128]{1,0:T(8,128)(2,1)S(1)} %get-tuple-element.81.refs_3_, ...), custom_call_target="tpu_custom_call" | custom-call | flops 679477248 | bytes 4194304 | tf_op jit(solution)/shard_map/grad_input/pallas_call | solution.py:697
  28.7 0.0 collective-permute-done.8
  28.7 2.8 %collective-permute-start.9 = (f32[168,128]{1,0:T(8,128)S(1)}, f32[168,128]{1,0:T(8,128)S(1)}, u32[]{:S(2)}, u32[]{:S(2)}) collective-permute-start(f32[168,128]{1,0:T(8,128)S(1)} %add.22), channel_id=1, source_target_pairs={{0,4},{1,5},{2,6},{3,7},{4,0},{5,1},{6,2},{7,3},{8,12},{9,13},{10,... | collective-permute-start | bytes 258056 | tf_op jit(solution)/shard_map/ppermute | solution.py:566
  31.6 4.2 %collective-permute-done.9 = f32[168,128]{1,0:T(8,128)S(1)} collective-permute-done((f32[168,128]{1,0:T(8,128)S(1)}, f32[168,128]{1,0:T(8,128)S(1)}, u32[]{:S(2)}, u32[]{:S(2)}) %collective-permute-start.9) | collective-permute-done | bytes 86048 | tf_op jit(solution)/shard_map/ppermute | solution.py:566
  35.7 0.1 collective-permute-start.10
  35.8 1.3 %collective-permute-done.10.refs_1_ = f32[168,128]{1,0:T(8,128)S(1)} collective-permute-done((f32[168,128]{1,0:T(8,128)S(1)}, f32[168,128]{1,0:T(8,128)S(1)}, u32[]{:S(2)}, u32[]{:S(2)}) %collective-permute-start.10) | collective-permute-done | bytes 86048 | tf_op jit(solution)/shard_map/ppermute | solution.py:566
  37.1 1.0 %unpack.1 = (f32[3,3,48,48]{3,2,1,0:T(8,128)}, f32[3,3,48,48]{3,2,1,0:T(8,128)}, f32[3,48]{1,0:T(4,128)}) custom-call(f32[168,128]{1,0:T(8,128)S(1)} %add.23.refs_0_, f32[168,128]{1,0:T(8,128)S(1)} %collective-permute-done.10.refs_1_), custom_call_target="tpu_custom_call" | custom-call | tf_op jit(solution)/shard_map/unpack/pallas_call | solution.py:735
  (4 shorter events, 0.1 us)
Async XLA Ops:
  2.1 6.1 %collective-permute-start = (bf16[208,128]{1,0:T(8,128)(2,1)S(1)}, bf16[208,128]{1,0:T(8,128)(2,1)S(1)}, u32[]{:S(2)}, u32[]{:S(2)}) collective-permute-start(bf16[208,128]{1,0:T(8,128)(2,1)S(1)} %get-tuple-element.48), channel_id=1, source_target_pairs={{0,8},{1,9},{2,10},{3,11},{4,12},{5,13},{6,14},{7,15},{8,0},{9,1},... | collective-permute-start | bytes 159752 | tf_op jit(solution)/shard_map/ppermute | solution.py:566
  2.6 5.6 %collective-permute-start.1 = (bf16[208,128]{1,0:T(8,128)(2,1)S(1)}, bf16[208,128]{1,0:T(8,128)(2,1)S(1)}, u32[]{:S(2)}, u32[]{:S(2)}) collective-permute-start(bf16[208,128]{1,0:T(8,128)(2,1)S(1)} %get-tuple-element.49), channel_id=1, source_target_pairs={{0,1},{1,0},{2,3},{3,2},{4,5},{5,4},{6,7},{7,6},{8,16},{9,17},{10,... | collective-permute-start | bytes 159752 | tf_op jit(solution)/shard_map/ppermute | solution.py:566
  8.5 4.5 %collective-permute-start.2 = (bf16[208,128]{1,0:T(8,128)(2,1)S(1)}, bf16[208,128]{1,0:T(8,128)(2,1)S(1)}, u32[]{:S(2)}, u32[]{:S(2)}) collective-permute-start(bf16[208,128]{1,0:T(8,128)(2,1)S(1)} %get-tuple-element.50), channel_id=1, source_target_pairs={{0,1},{1,0},{2,3},{3,2},{4,5},{5,4},{6,7},{7,6},{8,9},{9,8},{10,11... | collective-permute-start | bytes 159752 | tf_op jit(solution)/shard_map/ppermute | solution.py:566
  9.7 3.3 %collective-permute-start.3 = (bf16[208,128]{1,0:T(8,128)(2,1)S(1)}, bf16[208,128]{1,0:T(8,128)(2,1)S(1)}, u32[]{:S(2)}, u32[]{:S(2)}) collective-permute-start(bf16[208,128]{1,0:T(8,128)(2,1)S(1)} %get-tuple-element.51), channel_id=1, source_target_pairs={{0,8},{1,2},{2,1},{3,4},{4,3},{5,6},{6,5},{7,15},{8,0},{9,10},{10,... | collective-permute-start | bytes 159752 | tf_op jit(solution)/shard_map/ppermute | solution.py:566
  13.8 1.3 %collective-permute-start.4 = (f32[168,128]{1,0:T(8,128)S(1)}, f32[168,128]{1,0:T(8,128)S(1)}, u32[]{:S(2)}, u32[]{:S(2)}) collective-permute-start(f32[168,128]{1,0:T(8,128)S(1)} %get-tuple-element.67), channel_id=1, source_target_pairs={{0,8},{1,9},{2,10},{3,11},{4,12},{5,13},{6,14},{7,15},{8,0},{9,1},... | collective-permute-start | bytes 258056 | tf_op jit(solution)/shard_map/ppermute | solution.py:566
  15.2 7.1 %collective-permute-start.7 = (f32[168,128]{1,0:T(8,128)S(1)}, f32[168,128]{1,0:T(8,128)S(1)}, u32[]{:S(2)}, u32[]{:S(2)}) collective-permute-start(f32[168,128]{1,0:T(8,128)S(1)} %add.18), channel_id=1, source_target_pairs={{0,17},{1,16},{2,19},{3,18},{4,21},{5,20},{6,23},{7,22},{8,25},{9,... | collective-permute-start | bytes 258056 | tf_op jit(solution)/shard_map/ppermute | solution.py:566
  18.5 4.7 %collective-permute-start.6 = (f32[168,128]{1,0:T(8,128)S(1)}, f32[168,128]{1,0:T(8,128)S(1)}, u32[]{:S(2)}, u32[]{:S(2)}) collective-permute-start(f32[168,128]{1,0:T(8,128)S(1)} %add.18), channel_id=1, source_target_pairs={{0,1},{1,0},{2,3},{3,2},{4,5},{5,4},{6,7},{7,6},{8,9},{9,8},{10,11... | collective-permute-start | bytes 258056 | tf_op jit(solution)/shard_map/ppermute | solution.py:566
  18.5 5.5 %collective-permute-start.5 = (f32[168,128]{1,0:T(8,128)S(1)}, f32[168,128]{1,0:T(8,128)S(1)}, u32[]{:S(2)}, u32[]{:S(2)}) collective-permute-start(f32[168,128]{1,0:T(8,128)S(1)} %add.18), channel_id=1, source_target_pairs={{0,16},{1,17},{2,18},{3,19},{4,20},{5,21},{6,22},{7,23},{8,24},{9,... | collective-permute-start | bytes 258056 | tf_op jit(solution)/shard_map/ppermute | solution.py:566
  24.0 4.7 %collective-permute-start.8 = (f32[168,128]{1,0:T(8,128)S(1)}, f32[168,128]{1,0:T(8,128)S(1)}, u32[]{:S(2)}, u32[]{:S(2)}) collective-permute-start(f32[168,128]{1,0:T(8,128)S(1)} %add_add_fusion), channel_id=1, source_target_pairs={{0,2},{1,3},{2,0},{3,1},{4,6},{5,7},{6,4},{7,5},{8,10},{9,11},{10,... | collective-permute-start | bytes 258056 | tf_op jit(solution)/shard_map/ppermute | solution.py:566
  28.7 7.0 %collective-permute-start.9 = (f32[168,128]{1,0:T(8,128)S(1)}, f32[168,128]{1,0:T(8,128)S(1)}, u32[]{:S(2)}, u32[]{:S(2)}) collective-permute-start(f32[168,128]{1,0:T(8,128)S(1)} %add.22), channel_id=1, source_target_pairs={{0,4},{1,5},{2,6},{3,7},{4,0},{5,1},{6,2},{7,3},{8,12},{9,13},{10,... | collective-permute-start | bytes 258056 | tf_op jit(solution)/shard_map/ppermute | solution.py:566
  35.7 1.3 %collective-permute-start.10 = (f32[168,128]{1,0:T(8,128)S(1)}, f32[168,128]{1,0:T(8,128)S(1)}, u32[]{:S(2)}, u32[]{:S(2)}) collective-permute-start(f32[168,128]{1,0:T(8,128)S(1)} %add.23.refs_0_), channel_id=1, source_target_pairs={{0,8},{1,9},{2,10},{3,11},{4,12},{5,13},{6,14},{7,15},{8,0},{9,1},... | collective-permute-start | bytes 258056 | tf_op jit(solution)/shard_map/ppermute | solution.py:566

commit v6 on v5

--- a/solution.py
+++ b/solution.py
@@ -721,12 +721,12 @@
             if n == 0:
                 keep, hfix = lax.optimization_barrier((keep, hfix))
                 outs.append(output(True, far[0], hid, hfix, w2s, "delensed"))
-            if n == 1:
+            if n == len(rounds) - 1:
                 keep, dfix = lax.optimization_barrier((keep, dfix))
                 outs.append(output(False, far[1], dpre, dfix, w1bs, "grad_input"))
             keep = exchange(keep, move)
-            if n < 2:
-                keep, outs[n] = lax.optimization_barrier((keep, outs[n]))
+            if n in (0, len(rounds) - 1):
+                keep, outs[-1] = lax.optimization_barrier((keep, outs[-1]))
         delensed, grad_input = outs
         other = send(keep, lambda a, b: (a ^ 1, b))
 

time: 38.3 us -> 37 us (0.966)
  waiting for transfers between devices: 7.75 us -> 6.41 us
    ppermute x11, waiting for transfers between devices: 7.75 us -> 6.41 us  [send(): return lax.ppermute(value, axes, pairs)]
  transfers between devices with their start and end apart: 11 -> 11, of which waited for: 5 -> 6; matrix products, arithmetic and copies ran while one was open for 0% -> 0% of each run, Pallas kernels for 31% -> 32%
where the time goes in v6:
time: 37 us; the launch traced here: 36.8 us
  Pallas kernels  15.5 us (42%)
  starting transfers between devices  14.1 us (38%)
  waiting for transfers between devices  6.41 us (17%)
  between operations  0.75 us (2%)
    ppermute x11, starting transfers between devices, send(): return lax.ppermute(value, axes, pairs)  14.1 us
    ppermute x11, waiting for transfers between devices, send(): return lax.ppermute(value, axes, pairs)  6.41 us
    pallas_call x2, Pallas kernels, output(): pl.pallas_call(lambda *refs: output_kernel(with_phi, *refs), out_shape=ja...  5.44 us
    pallas_call x1, Pallas kernels, local(): pl.pallas_call(hidden_kernel, out_shape=(inner, inner, acc, acc, jax.Shap...  3.06 us
    pallas_call x1, Pallas kernels, local(): pl.pallas_call(prep_kernel, out_shape=(field, edges, jax.ShapeDtypeStruct...  3 us
    pallas_call x1, Pallas kernels, local(): pl.pallas_call(row_kernel, out_shape=(edge, edge), in_specs=[hbm] * 4, sc...  1.45 us
    pallas_call x1, Pallas kernels, local(): pl.pallas_call(lambda *refs: unpack_kernel(factor, *refs), out_shape=(gra...  1.04 us
    pallas_call x1, Pallas kernels, local(): pl.pallas_call(lambda *refs: edge_kernel(rows, nx, *refs), out_shape=(col...  0.8 us
  transfers between devices with their start and end apart: 11, of which 6 were waited for; matrix products, arithmetic and copies ran while one was open for 0% of the time, Pallas kernels for 32%

profile of v6, /device:TPU:0, one launch (start us, length us, event | category | flops | bytes accessed | tf_op | source)
XLA Modules:
  0.0 36.8 jit_solution(6145612079133540500)
XLA Ops:
  0.6 1.4 %edge_rows.1 = (bf16[208,128]{1,0:T(8,128)(2,1)S(1)}, bf16[208,128]{1,0:T(8,128)(2,1)S(1)}) custom-call(bf16[48,64,128]{2,1,0:T(8,128)(2,1)} %refs_0_.4, bf16[48,64,128]{2,1,0:T(8,128)(2,1)} %refs_0_.5, bf16[64,128]{1,0:T(8,128)(2,1)} %phi_ref.1, s32[8,16]{1,0:T(8,128)} %mask_ref.1), custom_call_target="tpu_custom_call" | custom-call | tf_op jit(solution)/shard_map/edge_rows/pallas_call | solution.py:607
  2.1 0.5 %collective-permute-start = (bf16[208,128]{1,0:T(8,128)(2,1)S(1)}, bf16[208,128]{1,0:T(8,128)(2,1)S(1)}, u32[]{:S(2)}, u32[]{:S(2)}) collective-permute-start(bf16[208,128]{1,0:T(8,128)(2,1)S(1)} %get-tuple-element.48), channel_id=1, source_target_pairs={{0,8},{1,9},{2,10},{3,11},{4,12},{5,13},{6,14},{7,15},{8,0},{9,1},... | collective-permute-start | bytes 159752 | tf_op jit(solution)/shard_map/ppermute | solution.py:566
  2.6 2.6 %collective-permute-start.1 = (bf16[208,128]{1,0:T(8,128)(2,1)S(1)}, bf16[208,128]{1,0:T(8,128)(2,1)S(1)}, u32[]{:S(2)}, u32[]{:S(2)}) collective-permute-start(bf16[208,128]{1,0:T(8,128)(2,1)S(1)} %get-tuple-element.49), channel_id=1, source_target_pairs={{0,1},{1,0},{2,3},{3,2},{4,5},{5,4},{6,7},{7,6},{8,16},{9,17},{10,... | collective-permute-start | bytes 159752 | tf_op jit(solution)/shard_map/ppermute | solution.py:566
  5.2 3.0 %prep.1 = (bf16[2,9216,128]{2,1,0:T(8,128)(2,1)S(1)}, bf16[2,208,128]{2,1,0:T(8,128)(2,1)S(1)}, f32[48,128]{1,0:T(8,128)S(1)}, f32[64,128]{1,0:T(8,128)S(1)}, f3...) custom-call(bf16[48,64,128]{2,1,0:T(8,128)(2,1)} %refs_0_.4, ...), custom_call_target="tpu_custom_call" | custom-call | flops 1358954496 | bytes 8388608 | tf_op jit(solution)/shard_map/prep/pallas_call | solution.py:632
  8.2 0.0 collective-permute-done.refs_1_
  8.2 0.0 collective-permute-done.1.refs_2_
  8.2 0.3 edge_cols.1
  8.5 1.2 %collective-permute-start.2 = (bf16[208,128]{1,0:T(8,128)(2,1)S(1)}, bf16[208,128]{1,0:T(8,128)(2,1)S(1)}, u32[]{:S(2)}, u32[]{:S(2)}) collective-permute-start(bf16[208,128]{1,0:T(8,128)(2,1)S(1)} %get-tuple-element.50), channel_id=1, source_target_pairs={{0,1},{1,0},{2,3},{3,2},{4,5},{5,4},{6,7},{7,6},{8,9},{9,8},{10,11... | collective-permute-start | bytes 159752 | tf_op jit(solution)/shard_map/ppermute | solution.py:566
  9.7 0.2 collective-permute-start.3
  9.9 3.1 %hidden.1 = (bf16[3168,128]{1,0:T(8,128)(2,1)S(1)}, bf16[3168,128]{1,0:T(8,128)(2,1)S(1)}, f32[144,144]{1,0:T(8,128)S(1)}, f32[144,144]{1,0:T(8,128)S(1)}, f32[2,48,128]{2,1,0:T(8,128)S(1)}) custom-call(bf16[2,9216,128]{2,1,0:T(8,128)(2,1)S(1)} %get-tuple-element.56.a3, f32[64,128]{1,0:T(8,128)S(1)} %get-tuple-element.57.phi_own.refs_1_, ...), custom_call_target="tpu_custom_call" | custom-call | flops 2717908992 | bytes 8388608 | tf_op jit(solution)/shard_map/hidden/pallas_call | solution.py:659
  13.0 0.0 collective-permute-done.2.refs_0_
  13.0 0.0 collective-permute-done.3.refs_1_
  13.0 0.8 %edge_parts.1 = (bf16[48,512]{1,0:T(8,128)(2,1)S(1)}, bf16[48,512]{1,0:T(8,128)(2,1)S(1)}, f32[168,128]{1,0:T(8,128)S(1)}, f32[168,128]{1,0:T(8,128)S(1)}) custom-call(bf16[208,128]{1,0:T(8,128)(2,1)S(1)} %collective-permute-done.2.refs_0_, bf16[208,128]{1,0:T(8,128)(2,1)S(1)} %collective-permute-done.3.refs_1_, ...), custom_call_target="tpu_custom_call" | custom-call | tf_op jit(solution)/shard_map/edge_parts/pallas_call | solution.py:679
  13.8 0.3 collective-permute-start.4
  14.2 0.4 %edge_fixes.1 = (f32[192,128]{1,0:T(8,128)S(1)}, f32[192,128]{1,0:T(8,128)S(1)}) custom-call(bf16[48,432]{1,0:T(8,128)(2,1)S(1)} %get-tuple-element.68.refs_0_, bf16[48,432]{1,0:T(8,128)(2,1)S(1)} %get-tuple-element.69.refs_1_, bf16[48,512]{1,0:T(8,128)(2,1)S(1)} %get-tuple-element.70.refs_2_, bf16[48,512]{1,0:T(8,128)(2,1)S(1)} %get-tuple-element.71.refs_3_), custom_call_target="tpu_custom_call" | custom-call | flops 169869312 | bytes 1048576 | tf_op jit(solution)/shard_map/edge_fixes/pallas_call | solution.py:686
  14.6 0.6 %collective-permute-done.4 = f32[168,128]{1,0:T(8,128)S(1)} collective-permute-done((f32[168,128]{1,0:T(8,128)S(1)}, f32[168,128]{1,0:T(8,128)S(1)}, u32[]{:S(2)}, u32[]{:S(2)}) %collective-permute-start.4) | collective-permute-done | bytes 86048 | tf_op jit(solution)/shard_map/ppermute | solution.py:566
  15.2 3.3 %collective-permute-start.7 = (f32[168,128]{1,0:T(8,128)S(1)}, f32[168,128]{1,0:T(8,128)S(1)}, u32[]{:S(2)}, u32[]{:S(2)}) collective-permute-start(f32[168,128]{1,0:T(8,128)S(1)} %add.18), channel_id=1, source_target_pairs={{0,17},{1,16},{2,19},{3,18},{4,21},{5,20},{6,23},{7,22},{8,25},{9,... | collective-permute-start | bytes 258056 | tf_op jit(solution)/shard_map/ppermute | solution.py:566
  18.5 0.0 collective-permute-start.6
  18.5 1.1 %collective-permute-start.5 = (f32[168,128]{1,0:T(8,128)S(1)}, f32[168,128]{1,0:T(8,128)S(1)}, u32[]{:S(2)}, u32[]{:S(2)}) collective-permute-start(f32[168,128]{1,0:T(8,128)S(1)} %add.18), channel_id=1, source_target_pairs={{0,16},{1,17},{2,18},{3,19},{4,20},{5,21},{6,22},{7,23},{8,24},{9,... | collective-permute-start | bytes 258056 | tf_op jit(solution)/shard_map/ppermute | solution.py:566
  19.5 2.7 %delensed.1 = bf16[48,64,128]{2,1,0:T(8,128)(2,1)} custom-call(bf16[48,64,128]{2,1,0:T(8,128)(2,1)} %refs_0_.4, f32[64,128]{1,0:T(8,128)S(1)} %get-tuple-element.57.phi_own.refs_1_, f32[64,128]{1,0:T(8,128)S(1)} %get-tuple-element.58.mask_own.refs_2_, bf16[3168,128]{1,0:T(8,128)(2,1)S(1)} %get-tuple-element.74.refs_3_, ...), custom_call_target="tpu_custom_call" | custom-call | flops 679477248 | bytes 4194304 | tf_op jit(solution)/shard_map/delensed/pallas_call | solution.py:697
  22.3 0.0 collective-permute-done.7
  22.3 0.9 %collective-permute-done.6 = f32[168,128]{1,0:T(8,128)S(1)} collective-permute-done((f32[168,128]{1,0:T(8,128)S(1)}, f32[168,128]{1,0:T(8,128)S(1)}, u32[]{:S(2)}, u32[]{:S(2)}) %collective-permute-start.6) | collective-permute-done | bytes 86048 | tf_op jit(solution)/shard_map/ppermute | solution.py:566
  23.2 0.8 %collective-permute-done.5 = f32[168,128]{1,0:T(8,128)S(1)} collective-permute-done((f32[168,128]{1,0:T(8,128)S(1)}, f32[168,128]{1,0:T(8,128)S(1)}, u32[]{:S(2)}, u32[]{:S(2)}) %collective-permute-start.5) | collective-permute-done | bytes 86048 | tf_op jit(solution)/shard_map/ppermute | solution.py:566
  24.0 2.0 %collective-permute-start.8 = (f32[168,128]{1,0:T(8,128)S(1)}, f32[168,128]{1,0:T(8,128)S(1)}, u32[]{:S(2)}, u32[]{:S(2)}) collective-permute-start(f32[168,128]{1,0:T(8,128)S(1)} %add_add_fusion), channel_id=1, source_target_pairs={{0,2},{1,3},{2,0},{3,1},{4,6},{5,7},{6,4},{7,5},{8,10},{9,11},{10,... | collective-permute-start | bytes 258056 | tf_op jit(solution)/shard_map/ppermute | solution.py:566
  26.0 2.7 %collective-permute-done.8 = f32[168,128]{1,0:T(8,128)S(1)} collective-permute-done((f32[168,128]{1,0:T(8,128)S(1)}, f32[168,128]{1,0:T(8,128)S(1)}, u32[]{:S(2)}, u32[]{:S(2)}) %collective-permute-start.8) | collective-permute-done | bytes 86048 | tf_op jit(solution)/shard_map/ppermute | solution.py:566
  28.7 2.9 %collective-permute-start.9 = (f32[168,128]{1,0:T(8,128)S(1)}, f32[168,128]{1,0:T(8,128)S(1)}, u32[]{:S(2)}, u32[]{:S(2)}) collective-permute-start(f32[168,128]{1,0:T(8,128)S(1)} %add.22), channel_id=1, source_target_pairs={{0,4},{1,5},{2,6},{3,7},{4,0},{5,1},{6,2},{7,3},{8,12},{9,13},{10,... | collective-permute-start | bytes 258056 | tf_op jit(solution)/shard_map/ppermute | solution.py:566
  31.6 2.7 %grad_input.1 = bf16[48,64,128]{2,1,0:T(8,128)(2,1)} custom-call(bf16[48,64,128]{2,1,0:T(8,128)(2,1)} %refs_0_.5, f32[64,128]{1,0:T(8,128)S(1)} %get-tuple-element.57.phi_own.refs_1_, f32[64,128]{1,0:T(8,128)S(1)} %get-tuple-element.58.mask_own.refs_2_, bf16[3168,128]{1,0:T(8,128)(2,1)S(1)} %get-tuple-element.81.refs_3_, ...), custom_call_target="tpu_custom_call" | custom-call | flops 679477248 | bytes 4194304 | tf_op jit(solution)/shard_map/grad_input/pallas_call | solution.py:697
  34.3 0.1 collective-permute-done.9
  34.4 0.1 collective-permute-start.10
  34.5 1.3 %collective-permute-done.10.refs_1_ = f32[168,128]{1,0:T(8,128)S(1)} collective-permute-done((f32[168,128]{1,0:T(8,128)S(1)}, f32[168,128]{1,0:T(8,128)S(1)}, u32[]{:S(2)}, u32[]{:S(2)}) %collective-permute-start.10) | collective-permute-done | bytes 86048 | tf_op jit(solution)/shard_map/ppermute | solution.py:566
  35.7 1.0 %unpack.1 = (f32[3,3,48,48]{3,2,1,0:T(8,128)}, f32[3,3,48,48]{3,2,1,0:T(8,128)}, f32[3,48]{1,0:T(4,128)}) custom-call(f32[168,128]{1,0:T(8,128)S(1)} %add.23.refs_0_, f32[168,128]{1,0:T(8,128)S(1)} %collective-permute-done.10.refs_1_), custom_call_target="tpu_custom_call" | custom-call | tf_op jit(solution)/shard_map/unpack/pallas_call | solution.py:735
  (4 shorter events, 0.1 us)
Async XLA Ops:
  2.1 6.1 %collective-permute-start = (bf16[208,128]{1,0:T(8,128)(2,1)S(1)}, bf16[208,128]{1,0:T(8,128)(2,1)S(1)}, u32[]{:S(2)}, u32[]{:S(2)}) collective-permute-start(bf16[208,128]{1,0:T(8,128)(2,1)S(1)} %get-tuple-element.48), channel_id=1, source_target_pairs={{0,8},{1,9},{2,10},{3,11},{4,12},{5,13},{6,14},{7,15},{8,0},{9,1},... | collective-permute-start | bytes 159752 | tf_op jit(solution)/shard_map/ppermute | solution.py:566
  2.6 5.6 %collective-permute-start.1 = (bf16[208,128]{1,0:T(8,128)(2,1)S(1)}, bf16[208,128]{1,0:T(8,128)(2,1)S(1)}, u32[]{:S(2)}, u32[]{:S(2)}) collective-permute-start(bf16[208,128]{1,0:T(8,128)(2,1)S(1)} %get-tuple-element.49), channel_id=1, source_target_pairs={{0,1},{1,0},{2,3},{3,2},{4,5},{5,4},{6,7},{7,6},{8,16},{9,17},{10,... | collective-permute-start | bytes 159752 | tf_op jit(solution)/shard_map/ppermute | solution.py:566
  8.5 4.5 %collective-permute-start.2 = (bf16[208,128]{1,0:T(8,128)(2,1)S(1)}, bf16[208,128]{1,0:T(8,128)(2,1)S(1)}, u32[]{:S(2)}, u32[]{:S(2)}) collective-permute-start(bf16[208,128]{1,0:T(8,128)(2,1)S(1)} %get-tuple-element.50), channel_id=1, source_target_pairs={{0,1},{1,0},{2,3},{3,2},{4,5},{5,4},{6,7},{7,6},{8,9},{9,8},{10,11... | collective-permute-start | bytes 159752 | tf_op jit(solution)/shard_map/ppermute | solution.py:566
  9.7 3.3 %collective-permute-start.3 = (bf16[208,128]{1,0:T(8,128)(2,1)S(1)}, bf16[208,128]{1,0:T(8,128)(2,1)S(1)}, u32[]{:S(2)}, u32[]{:S(2)}) collective-permute-start(bf16[208,128]{1,0:T(8,128)(2,1)S(1)} %get-tuple-element.51), channel_id=1, source_target_pairs={{0,8},{1,2},{2,1},{3,4},{4,3},{5,6},{6,5},{7,15},{8,0},{9,10},{10,... | collective-permute-start | bytes 159752 | tf_op jit(solution)/shard_map/ppermute | solution.py:566
  13.8 1.3 %collective-permute-start.4 = (f32[168,128]{1,0:T(8,128)S(1)}, f32[168,128]{1,0:T(8,128)S(1)}, u32[]{:S(2)}, u32[]{:S(2)}) collective-permute-start(f32[168,128]{1,0:T(8,128)S(1)} %get-tuple-element.67), channel_id=1, source_target_pairs={{0,8},{1,9},{2,10},{3,11},{4,12},{5,13},{6,14},{7,15},{8,0},{9,1},... | collective-permute-start | bytes 258056 | tf_op jit(solution)/shard_map/ppermute | solution.py:566
  15.2 7.1 %collective-permute-start.7 = (f32[168,128]{1,0:T(8,128)S(1)}, f32[168,128]{1,0:T(8,128)S(1)}, u32[]{:S(2)}, u32[]{:S(2)}) collective-permute-start(f32[168,128]{1,0:T(8,128)S(1)} %add.18), channel_id=1, source_target_pairs={{0,17},{1,16},{2,19},{3,18},{4,21},{5,20},{6,23},{7,22},{8,25},{9,... | collective-permute-start | bytes 258056 | tf_op jit(solution)/shard_map/ppermute | solution.py:566
  18.5 4.7 %collective-permute-start.6 = (f32[168,128]{1,0:T(8,128)S(1)}, f32[168,128]{1,0:T(8,128)S(1)}, u32[]{:S(2)}, u32[]{:S(2)}) collective-permute-start(f32[168,128]{1,0:T(8,128)S(1)} %add.18), channel_id=1, source_target_pairs={{0,1},{1,0},{2,3},{3,2},{4,5},{5,4},{6,7},{7,6},{8,9},{9,8},{10,11... | collective-permute-start | bytes 258056 | tf_op jit(solution)/shard_map/ppermute | solution.py:566
  18.5 5.5 %collective-permute-start.5 = (f32[168,128]{1,0:T(8,128)S(1)}, f32[168,128]{1,0:T(8,128)S(1)}, u32[]{:S(2)}, u32[]{:S(2)}) collective-permute-start(f32[168,128]{1,0:T(8,128)S(1)} %add.18), channel_id=1, source_target_pairs={{0,16},{1,17},{2,18},{3,19},{4,20},{5,21},{6,22},{7,23},{8,24},{9,... | collective-permute-start | bytes 258056 | tf_op jit(solution)/shard_map/ppermute | solution.py:566
  24.0 4.7 %collective-permute-start.8 = (f32[168,128]{1,0:T(8,128)S(1)}, f32[168,128]{1,0:T(8,128)S(1)}, u32[]{:S(2)}, u32[]{:S(2)}) collective-permute-start(f32[168,128]{1,0:T(8,128)S(1)} %add_add_fusion), channel_id=1, source_target_pairs={{0,2},{1,3},{2,0},{3,1},{4,6},{5,7},{6,4},{7,5},{8,10},{9,11},{10,... | collective-permute-start | bytes 258056 | tf_op jit(solution)/shard_map/ppermute | solution.py:566
  28.7 5.7 %collective-permute-start.9 = (f32[168,128]{1,0:T(8,128)S(1)}, f32[168,128]{1,0:T(8,128)S(1)}, u32[]{:S(2)}, u32[]{:S(2)}) collective-permute-start(f32[168,128]{1,0:T(8,128)S(1)} %add.22), channel_id=1, source_target_pairs={{0,4},{1,5},{2,6},{3,7},{4,0},{5,1},{6,2},{7,3},{8,12},{9,13},{10,... | collective-permute-start | bytes 258056 | tf_op jit(solution)/shard_map/ppermute | solution.py:566
  34.4 1.3 %collective-permute-start.10 = (f32[168,128]{1,0:T(8,128)S(1)}, f32[168,128]{1,0:T(8,128)S(1)}, u32[]{:S(2)}, u32[]{:S(2)}) collective-permute-start(f32[168,128]{1,0:T(8,128)S(1)} %add.23.refs_0_), channel_id=1, source_target_pairs={{0,8},{1,9},{2,10},{3,11},{4,12},{5,13},{6,14},{7,15},{8,0},{9,1},... | collective-permute-start | bytes 258056 | tf_op jit(solution)/shard_map/ppermute | solution.py:566

commit v7 on v6

--- a/solution.py
+++ b/solution.py
@@ -48,9 +48,9 @@
     copies = []
     for n, (src, dst) in enumerate(
         [
-            (ref.at[:, pl.ds(first, 16), :], blocks.at[k])
+            (ref.at[:, pl.ds(first, 8), :], blocks.at[k])
             for k, (ref, first) in enumerate(
-                ((sky_ref, 0), (cot_ref, 0), (sky_ref, rows - 16), (cot_ref, rows - 16))
+                ((sky_ref, 0), (cot_ref, 0), (sky_ref, rows - 8), (cot_ref, rows - 8))
             )
         ]
         + [(phi_ref.at[pl.ds(0, 16), :], phis.at[0]), (phi_ref.at[pl.ds(rows - 16, 16), :], phis.at[1])]
@@ -63,7 +63,7 @@
     cells = tile_rows(tiles)
     odd = is_odd("gy")
     parts = []
-    for side, (first, mrow) in enumerate(((0, 0), (14, tiles.shape[0] - 1))):
+    for side, (first, mrow) in enumerate(((0, 0), (6, tiles.shape[0] - 1))):
         keep = cells[mrow : mrow + 1]
         low = jnp.broadcast_to(keep, (chans, 128)).astype(BF)
         part = []
@@ -579,12 +579,13 @@
         return send(first, partner(0)), send(second, partner(1))
 
     def exchange(value, moves):
-        got = [send(value, lambda a, b: (a ^ m[0], b ^ m[1])) for m in moves]
+        sent = value.astype(BF)
+        got = [send(sent, lambda a, b: (a ^ m[0], b ^ m[1])).astype(F32) for m in moves]
         if len(moves) == 1:
-            return value + got[0]
+            return sent.astype(F32) + got[0]
         both = (moves[0][0] ^ moves[1][0], moves[0][1] ^ moves[1][1])
-        far = send(value, lambda a, b: (a ^ both[0], b ^ both[1]))
-        return (value + got[0]) + (got[1] + far)
+        far = send(sent, lambda a, b: (a ^ both[0], b ^ both[1])).astype(F32)
+        return (sent.astype(F32) + got[0]) + (got[1] + far)
 
     def local(
         sky, lens_phi, cotangent, tile_mask, weight_one, weight_two, cond_one, bias_one, cond_two
@@ -609,7 +610,7 @@
             out_shape=(edge, edge),
             in_specs=[hbm] * 4,
             scratch_shapes=[
-                pltpu.VMEM((4, chans, 16, width), BF),
+                pltpu.VMEM((4, chans, 8, width), BF),
                 pltpu.VMEM((2, 16, width), BF),
                 pltpu.VMEM(tile_mask.shape, jnp.int32),
                 pltpu.SemaphoreType.DMA((7,)),
@@ -714,7 +715,7 @@
 
         moves = [(1 << k, 0) for k in range(1, ny.bit_length() - 1)]
         moves += [(0, 1 << k) for k in range(nx.bit_length() - 1)]
-        rounds = [moves[:2]] + [[move] for move in moves[2:]]
+        rounds = [moves[k : k + 2] for k in range(0, len(moves), 2)]
         keep = keep + send(give, lambda a, b: (a ^ 1, b))
         outs = []
         for n, move in enumerate(rounds):

time: 37 us -> 35.8 us (0.968)
  waiting for transfers between devices: 6.41 us -> 5.62 us
    ppermute x11 -> x12, waiting for transfers between devices: 6.41 us -> 5.62 us  [send(): return lax.ppermute(value, axes, pairs)]
    ppermute x11 -> x12, starting transfers between devices: 14.1 us -> 13.8 us  [send(): return lax.ppermute(value, axes, pairs)]
  transfers between devices with their start and end apart: 11 -> 12, of which waited for: 6 -> 4; matrix products, arithmetic and copies ran while one was open for 0% -> 0% of each run, Pallas kernels for 32% -> 33%
where the time goes in v7:
time: 35.8 us; the launch traced here: 35.5 us
  Pallas kernels  15.3 us (43%)
  starting transfers between devices  13.8 us (39%)
  waiting for transfers between devices  5.62 us (16%)
  between operations  0.77 us (2%)
    ppermute x12, starting transfers between devices, send(): return lax.ppermute(value, axes, pairs)  13.8 us
    ppermute x12, waiting for transfers between devices, send(): return lax.ppermute(value, axes, pairs)  5.62 us
    pallas_call x2, Pallas kernels, output(): pl.pallas_call(lambda *refs: output_kernel(with_phi, *refs), out_shape=ja...  5.44 us
    pallas_call x1, Pallas kernels, local(): pl.pallas_call(hidden_kernel, out_shape=(inner, inner, acc, acc, jax.Shap...  3.06 us
    pallas_call x1, Pallas kernels, local(): pl.pallas_call(prep_kernel, out_shape=(field, edges, jax.ShapeDtypeStruct...  3 us
    pallas_call x1, Pallas kernels, local(): pl.pallas_call(row_kernel, out_shape=(edge, edge), in_specs=[hbm] * 4, sc...  1.27 us
    pallas_call x1, Pallas kernels, local(): pl.pallas_call(lambda *refs: unpack_kernel(factor, *refs), out_shape=(gra...  1.04 us
    pallas_call x1, Pallas kernels, local(): pl.pallas_call(lambda *refs: edge_kernel(rows, nx, *refs), out_shape=(col...  0.8 us
  transfers between devices with their start and end apart: 12, of which 4 were waited for; matrix products, arithmetic and copies ran while one was open for 0% of the time, Pallas kernels for 33%

profile of v7, /device:TPU:0, one launch (start us, length us, event | category | flops | bytes accessed | tf_op | source)
XLA Modules:
  0.0 35.5 jit_solution(2069706920413461725)
XLA Ops:
  0.6 1.3 %edge_rows.1 = (bf16[208,128]{1,0:T(8,128)(2,1)S(1)}, bf16[208,128]{1,0:T(8,128)(2,1)S(1)}) custom-call(bf16[48,64,128]{2,1,0:T(8,128)(2,1)} %refs_0_.4, bf16[48,64,128]{2,1,0:T(8,128)(2,1)} %refs_0_.5, bf16[64,128]{1,0:T(8,128)(2,1)} %phi_ref.1, s32[8,16]{1,0:T(8,128)} %mask_ref.1), custom_call_target="tpu_custom_call" | custom-call | tf_op jit(solution)/shard_map/edge_rows/pallas_call | solution.py:608
  1.9 0.5 %collective-permute-start = (bf16[208,128]{1,0:T(8,128)(2,1)S(1)}, bf16[208,128]{1,0:T(8,128)(2,1)S(1)}, u32[]{:S(2)}, u32[]{:S(2)}) collective-permute-start(bf16[208,128]{1,0:T(8,128)(2,1)S(1)} %get-tuple-element.48), channel_id=1, source_target_pairs={{0,8},{1,9},{2,10},{3,11},{4,12},{5,13},{6,14},{7,15},{8,0},{9,1},... | collective-permute-start | bytes 159752 | tf_op jit(solution)/shard_map/ppermute | solution.py:566
  2.4 2.6 %collective-permute-start.1 = (bf16[208,128]{1,0:T(8,128)(2,1)S(1)}, bf16[208,128]{1,0:T(8,128)(2,1)S(1)}, u32[]{:S(2)}, u32[]{:S(2)}) collective-permute-start(bf16[208,128]{1,0:T(8,128)(2,1)S(1)} %get-tuple-element.49), channel_id=1, source_target_pairs={{0,1},{1,0},{2,3},{3,2},{4,5},{5,4},{6,7},{7,6},{8,16},{9,17},{10,... | collective-permute-start | bytes 159752 | tf_op jit(solution)/shard_map/ppermute | solution.py:566
  5.0 3.0 %prep.1 = (bf16[2,9216,128]{2,1,0:T(8,128)(2,1)S(1)}, bf16[2,208,128]{2,1,0:T(8,128)(2,1)S(1)}, f32[48,128]{1,0:T(8,128)S(1)}, f32[64,128]{1,0:T(8,128)S(1)}, f3...) custom-call(bf16[48,64,128]{2,1,0:T(8,128)(2,1)} %refs_0_.4, ...), custom_call_target="tpu_custom_call" | custom-call | flops 1358954496 | bytes 8388608 | tf_op jit(solution)/shard_map/prep/pallas_call | solution.py:633
  8.0 0.0 collective-permute-done.refs_1_
  8.0 0.0 collective-permute-done.1.refs_2_
  8.0 0.3 edge_cols.1
  8.4 1.2 %collective-permute-start.2 = (bf16[208,128]{1,0:T(8,128)(2,1)S(1)}, bf16[208,128]{1,0:T(8,128)(2,1)S(1)}, u32[]{:S(2)}, u32[]{:S(2)}) collective-permute-start(bf16[208,128]{1,0:T(8,128)(2,1)S(1)} %get-tuple-element.50), channel_id=1, source_target_pairs={{0,1},{1,0},{2,3},{3,2},{4,5},{5,4},{6,7},{7,6},{8,9},{9,8},{10,11... | collective-permute-start | bytes 159752 | tf_op jit(solution)/shard_map/ppermute | solution.py:566
  9.5 0.2 collective-permute-start.3
  9.8 3.1 %hidden.1 = (bf16[3168,128]{1,0:T(8,128)(2,1)S(1)}, bf16[3168,128]{1,0:T(8,128)(2,1)S(1)}, f32[144,144]{1,0:T(8,128)S(1)}, f32[144,144]{1,0:T(8,128)S(1)}, f32[2,48,128]{2,1,0:T(8,128)S(1)}) custom-call(bf16[2,9216,128]{2,1,0:T(8,128)(2,1)S(1)} %get-tuple-element.56.a3, f32[64,128]{1,0:T(8,128)S(1)} %get-tuple-element.57.phi_own.refs_1_, ...), custom_call_target="tpu_custom_call" | custom-call | flops 2717908992 | bytes 8388608 | tf_op jit(solution)/shard_map/hidden/pallas_call | solution.py:660
  12.8 0.0 collective-permute-done.2.refs_0_
  12.8 0.0 collective-permute-done.3.refs_1_
  12.8 0.8 %edge_parts.1 = (bf16[48,512]{1,0:T(8,128)(2,1)S(1)}, bf16[48,512]{1,0:T(8,128)(2,1)S(1)}, f32[168,128]{1,0:T(8,128)S(1)}, f32[168,128]{1,0:T(8,128)S(1)}) custom-call(bf16[208,128]{1,0:T(8,128)(2,1)S(1)} %collective-permute-done.2.refs_0_, bf16[208,128]{1,0:T(8,128)(2,1)S(1)} %collective-permute-done.3.refs_1_, ...), custom_call_target="tpu_custom_call" | custom-call | tf_op jit(solution)/shard_map/edge_parts/pallas_call | solution.py:680
  13.6 0.3 collective-permute-start.4
  14.0 0.4 %edge_fixes.1 = (f32[192,128]{1,0:T(8,128)S(1)}, f32[192,128]{1,0:T(8,128)S(1)}) custom-call(bf16[48,432]{1,0:T(8,128)(2,1)S(1)} %get-tuple-element.68.refs_0_, bf16[48,432]{1,0:T(8,128)(2,1)S(1)} %get-tuple-element.69.refs_1_, bf16[48,512]{1,0:T(8,128)(2,1)S(1)} %get-tuple-element.70.refs_2_, bf16[48,512]{1,0:T(8,128)(2,1)S(1)} %get-tuple-element.71.refs_3_), custom_call_target="tpu_custom_call" | custom-call | flops 169869312 | bytes 1048576 | tf_op jit(solution)/shard_map/edge_fixes/pallas_call | solution.py:687
  14.4 0.6 %collective-permute-done.4 = f32[168,128]{1,0:T(8,128)S(1)} collective-permute-done((f32[168,128]{1,0:T(8,128)S(1)}, f32[168,128]{1,0:T(8,128)S(1)}, u32[]{:S(2)}, u32[]{:S(2)}) %collective-permute-start.4) | collective-permute-done | bytes 86048 | tf_op jit(solution)/shard_map/ppermute | solution.py:566
  15.0 2.9 %collective-permute-start.6 = (bf16[168,128]{1,0:T(8,128)(2,1)S(1)}, bf16[168,128]{1,0:T(8,128)(2,1)S(1)}, u32[]{:S(2)}, u32[]{:S(2)}) collective-permute-start(bf16[168,128]{1,0:T(8,128)(2,1)S(1)} %add.21), channel_id=1, source_target_pairs={{0,1},{1,0},{2,3},{3,2},{4,5},{5,4},{6,7},{7,6},{8,9},{9,8},{10,11... | collective-permute-start | bytes 129032 | tf_op jit(solution)/shard_map/ppermute | solution.py:566
  17.9 1.0 %collective-permute-start.5 = (bf16[168,128]{1,0:T(8,128)(2,1)S(1)}, bf16[168,128]{1,0:T(8,128)(2,1)S(1)}, u32[]{:S(2)}, u32[]{:S(2)}) collective-permute-start(bf16[168,128]{1,0:T(8,128)(2,1)S(1)} %add.21), channel_id=1, source_target_pairs={{0,16},{1,17},{2,18},{3,19},{4,20},{5,21},{6,22},{7,23},{8,24},{9,... | collective-permute-start | bytes 129032 | tf_op jit(solution)/shard_map/ppermute | solution.py:566
  18.8 0.6 %collective-permute-start.7 = (bf16[168,128]{1,0:T(8,128)(2,1)S(1)}, bf16[168,128]{1,0:T(8,128)(2,1)S(1)}, u32[]{:S(2)}, u32[]{:S(2)}) collective-permute-start(bf16[168,128]{1,0:T(8,128)(2,1)S(1)} %add.21), channel_id=1, source_target_pairs={{0,17},{1,16},{2,19},{3,18},{4,21},{5,20},{6,23},{7,22},{8,25},{9,... | collective-permute-start | bytes 129032 | tf_op jit(solution)/shard_map/ppermute | solution.py:566
  19.4 2.7 %delensed.1 = bf16[48,64,128]{2,1,0:T(8,128)(2,1)} custom-call(bf16[48,64,128]{2,1,0:T(8,128)(2,1)} %refs_0_.4, f32[64,128]{1,0:T(8,128)S(1)} %get-tuple-element.57.phi_own.refs_1_, f32[64,128]{1,0:T(8,128)S(1)} %get-tuple-element.58.mask_own.refs_2_, bf16[3168,128]{1,0:T(8,128)(2,1)S(1)} %get-tuple-element.74.refs_3_, ...), custom_call_target="tpu_custom_call" | custom-call | flops 679477248 | bytes 4194304 | tf_op jit(solution)/shard_map/delensed/pallas_call | solution.py:698
  22.2 0.0 collective-permute-done.6
  22.2 0.0 collective-permute-done.5
  22.2 1.6 %collective-permute-done.7 = bf16[168,128]{1,0:T(8,128)(2,1)S(1)} collective-permute-done((bf16[168,128]{1,0:T(8,128)(2,1)S(1)}, bf16[168,128]{1,0:T(8,128)(2,1)S(1)}, u32[]{:S(2)}, u32[]{:S(2)}) %collective-permute-start.7) | collective-permute-done | bytes 43040 | tf_op jit(solution)/shard_map/ppermute | solution.py:566
  23.8 2.7 %collective-permute-start.9 = (bf16[168,128]{1,0:T(8,128)(2,1)S(1)}, bf16[168,128]{1,0:T(8,128)(2,1)S(1)}, u32[]{:S(2)}, u32[]{:S(2)}) collective-permute-start(bf16[168,128]{1,0:T(8,128)(2,1)S(1)} %add_add_fusion.1), channel_id=1, source_target_pairs={{0,4},{1,5},{2,6},{3,7},{4,0},{5,1},{6,2},{7,3},{8,12},{9,13},{10,... | collective-permute-start | bytes 129032 | tf_op jit(solution)/shard_map/ppermute | solution.py:566
  26.5 0.9 %collective-permute-start.8 = (bf16[168,128]{1,0:T(8,128)(2,1)S(1)}, bf16[168,128]{1,0:T(8,128)(2,1)S(1)}, u32[]{:S(2)}, u32[]{:S(2)}) collective-permute-start(bf16[168,128]{1,0:T(8,128)(2,1)S(1)} %add_add_fusion.1), channel_id=1, source_target_pairs={{0,2},{1,3},{2,0},{3,1},{4,6},{5,7},{6,4},{7,5},{8,10},{9,11},{10,... | collective-permute-start | bytes 129032 | tf_op jit(solution)/shard_map/ppermute | solution.py:566
  27.3 0.9 %collective-permute-start.10 = (bf16[168,128]{1,0:T(8,128)(2,1)S(1)}, bf16[168,128]{1,0:T(8,128)(2,1)S(1)}, u32[]{:S(2)}, u32[]{:S(2)}) collective-permute-start(bf16[168,128]{1,0:T(8,128)(2,1)S(1)} %add_add_fusion.1), channel_id=1, source_target_pairs={{0,6},{1,7},{2,4},{3,5},{4,2},{5,3},{6,0},{7,1},{8,14},{9,15},{10,... | collective-permute-start | bytes 129032 | tf_op jit(solution)/shard_map/ppermute | solution.py:566
  28.3 2.7 %grad_input.1 = bf16[48,64,128]{2,1,0:T(8,128)(2,1)} custom-call(bf16[48,64,128]{2,1,0:T(8,128)(2,1)} %refs_0_.5, f32[64,128]{1,0:T(8,128)S(1)} %get-tuple-element.57.phi_own.refs_1_, f32[64,128]{1,0:T(8,128)S(1)} %get-tuple-element.58.mask_own.refs_2_, bf16[3168,128]{1,0:T(8,128)(2,1)S(1)} %get-tuple-element.81.refs_3_, ...), custom_call_target="tpu_custom_call" | custom-call | flops 679477248 | bytes 4194304 | tf_op jit(solution)/shard_map/grad_input/pallas_call | solution.py:698
  31.0 0.0 collective-permute-done.9
  31.0 2.1 %collective-permute-done.10 = bf16[168,128]{1,0:T(8,128)(2,1)S(1)} collective-permute-done((bf16[168,128]{1,0:T(8,128)(2,1)S(1)}, bf16[168,128]{1,0:T(8,128)(2,1)S(1)}, u32[]{:S(2)}, u32[]{:S(2)}) %collective-permute-start.10) | collective-permute-done | bytes 43040 | tf_op jit(solution)/shard_map/ppermute | solution.py:566
  33.2 0.1 collective-permute-start.11
  33.2 1.3 %collective-permute-done.11.refs_1_ = f32[168,128]{1,0:T(8,128)S(1)} collective-permute-done((f32[168,128]{1,0:T(8,128)S(1)}, f32[168,128]{1,0:T(8,128)S(1)}, u32[]{:S(2)}, u32[]{:S(2)}) %collective-permute-start.11) | collective-permute-done | bytes 86048 | tf_op jit(solution)/shard_map/ppermute | solution.py:566
  34.5 1.0 %unpack.1 = (f32[3,3,48,48]{3,2,1,0:T(8,128)}, f32[3,3,48,48]{3,2,1,0:T(8,128)}, f32[3,48]{1,0:T(4,128)}) custom-call(f32[168,128]{1,0:T(8,128)S(1)} %add_add_fusion.refs_0_, f32[168,128]{1,0:T(8,128)S(1)} %collective-permute-done.11.refs_1_), custom_call_target="tpu_custom_call" | custom-call | tf_op jit(solution)/shard_map/unpack/pallas_call | solution.py:736
  (4 shorter events, 0.1 us)
Async XLA Ops:
  1.9 6.1 %collective-permute-start = (bf16[208,128]{1,0:T(8,128)(2,1)S(1)}, bf16[208,128]{1,0:T(8,128)(2,1)S(1)}, u32[]{:S(2)}, u32[]{:S(2)}) collective-permute-start(bf16[208,128]{1,0:T(8,128)(2,1)S(1)} %get-tuple-element.48), channel_id=1, source_target_pairs={{0,8},{1,9},{2,10},{3,11},{4,12},{5,13},{6,14},{7,15},{8,0},{9,1},... | collective-permute-start | bytes 159752 | tf_op jit(solution)/shard_map/ppermute | solution.py:566
  2.4 5.6 %collective-permute-start.1 = (bf16[208,128]{1,0:T(8,128)(2,1)S(1)}, bf16[208,128]{1,0:T(8,128)(2,1)S(1)}, u32[]{:S(2)}, u32[]{:S(2)}) collective-permute-start(bf16[208,128]{1,0:T(8,128)(2,1)S(1)} %get-tuple-element.49), channel_id=1, source_target_pairs={{0,1},{1,0},{2,3},{3,2},{4,5},{5,4},{6,7},{7,6},{8,16},{9,17},{10,... | collective-permute-start | bytes 159752 | tf_op jit(solution)/shard_map/ppermute | solution.py:566
  8.4 4.5 %collective-permute-start.2 = (bf16[208,128]{1,0:T(8,128)(2,1)S(1)}, bf16[208,128]{1,0:T(8,128)(2,1)S(1)}, u32[]{:S(2)}, u32[]{:S(2)}) collective-permute-start(bf16[208,128]{1,0:T(8,128)(2,1)S(1)} %get-tuple-element.50), channel_id=1, source_target_pairs={{0,1},{1,0},{2,3},{3,2},{4,5},{5,4},{6,7},{7,6},{8,9},{9,8},{10,11... | collective-permute-start | bytes 159752 | tf_op jit(solution)/shard_map/ppermute | solution.py:566
  9.5 3.3 %collective-permute-start.3 = (bf16[208,128]{1,0:T(8,128)(2,1)S(1)}, bf16[208,128]{1,0:T(8,128)(2,1)S(1)}, u32[]{:S(2)}, u32[]{:S(2)}) collective-permute-start(bf16[208,128]{1,0:T(8,128)(2,1)S(1)} %get-tuple-element.51), channel_id=1, source_target_pairs={{0,8},{1,2},{2,1},{3,4},{4,3},{5,6},{6,5},{7,15},{8,0},{9,10},{10,... | collective-permute-start | bytes 159752 | tf_op jit(solution)/shard_map/ppermute | solution.py:566
  13.6 1.3 %collective-permute-start.4 = (f32[168,128]{1,0:T(8,128)S(1)}, f32[168,128]{1,0:T(8,128)S(1)}, u32[]{:S(2)}, u32[]{:S(2)}) collective-permute-start(f32[168,128]{1,0:T(8,128)S(1)} %get-tuple-element.67), channel_id=1, source_target_pairs={{0,8},{1,9},{2,10},{3,11},{4,12},{5,13},{6,14},{7,15},{8,0},{9,1},... | collective-permute-start | bytes 258056 | tf_op jit(solution)/shard_map/ppermute | solution.py:566
  15.0 7.2 %collective-permute-start.6 = (bf16[168,128]{1,0:T(8,128)(2,1)S(1)}, bf16[168,128]{1,0:T(8,128)(2,1)S(1)}, u32[]{:S(2)}, u32[]{:S(2)}) collective-permute-start(bf16[168,128]{1,0:T(8,128)(2,1)S(1)} %add.21), channel_id=1, source_target_pairs={{0,1},{1,0},{2,3},{3,2},{4,5},{5,4},{6,7},{7,6},{8,9},{9,8},{10,11... | collective-permute-start | bytes 129032 | tf_op jit(solution)/shard_map/ppermute | solution.py:566
  17.9 4.3 %collective-permute-start.5 = (bf16[168,128]{1,0:T(8,128)(2,1)S(1)}, bf16[168,128]{1,0:T(8,128)(2,1)S(1)}, u32[]{:S(2)}, u32[]{:S(2)}) collective-permute-start(bf16[168,128]{1,0:T(8,128)(2,1)S(1)} %add.21), channel_id=1, source_target_pairs={{0,16},{1,17},{2,18},{3,19},{4,20},{5,21},{6,22},{7,23},{8,24},{9,... | collective-permute-start | bytes 129032 | tf_op jit(solution)/shard_map/ppermute | solution.py:566
  18.8 4.9 %collective-permute-start.7 = (bf16[168,128]{1,0:T(8,128)(2,1)S(1)}, bf16[168,128]{1,0:T(8,128)(2,1)S(1)}, u32[]{:S(2)}, u32[]{:S(2)}) collective-permute-start(bf16[168,128]{1,0:T(8,128)(2,1)S(1)} %add.21), channel_id=1, source_target_pairs={{0,17},{1,16},{2,19},{3,18},{4,21},{5,20},{6,23},{7,22},{8,25},{9,... | collective-permute-start | bytes 129032 | tf_op jit(solution)/shard_map/ppermute | solution.py:566
  23.8 7.2 %collective-permute-start.9 = (bf16[168,128]{1,0:T(8,128)(2,1)S(1)}, bf16[168,128]{1,0:T(8,128)(2,1)S(1)}, u32[]{:S(2)}, u32[]{:S(2)}) collective-permute-start(bf16[168,128]{1,0:T(8,128)(2,1)S(1)} %add_add_fusion.1), channel_id=1, source_target_pairs={{0,4},{1,5},{2,6},{3,7},{4,0},{5,1},{6,2},{7,3},{8,12},{9,13},{10,... | collective-permute-start | bytes 129032 | tf_op jit(solution)/shard_map/ppermute | solution.py:566
  26.5 4.5 %collective-permute-start.8 = (bf16[168,128]{1,0:T(8,128)(2,1)S(1)}, bf16[168,128]{1,0:T(8,128)(2,1)S(1)}, u32[]{:S(2)}, u32[]{:S(2)}) collective-permute-start(bf16[168,128]{1,0:T(8,128)(2,1)S(1)} %add_add_fusion.1), channel_id=1, source_target_pairs={{0,2},{1,3},{2,0},{3,1},{4,6},{5,7},{6,4},{7,5},{8,10},{9,11},{10,... | collective-permute-start | bytes 129032 | tf_op jit(solution)/shard_map/ppermute | solution.py:566
  27.3 5.8 %collective-permute-start.10 = (bf16[168,128]{1,0:T(8,128)(2,1)S(1)}, bf16[168,128]{1,0:T(8,128)(2,1)S(1)}, u32[]{:S(2)}, u32[]{:S(2)}) collective-permute-start(bf16[168,128]{1,0:T(8,128)(2,1)S(1)} %add_add_fusion.1), channel_id=1, source_target_pairs={{0,6},{1,7},{2,4},{3,5},{4,2},{5,3},{6,0},{7,1},{8,14},{9,15},{10,... | collective-permute-start | bytes 129032 | tf_op jit(solution)/shard_map/ppermute | solution.py:566
  33.2 1.3 %collective-permute-start.11 = (f32[168,128]{1,0:T(8,128)S(1)}, f32[168,128]{1,0:T(8,128)S(1)}, u32[]{:S(2)}, u32[]{:S(2)}) collective-permute-start(f32[168,128]{1,0:T(8,128)S(1)} %add_add_fusion.refs_0_), channel_id=1, source_target_pairs={{0,8},{1,9},{2,10},{3,11},{4,12},{5,13},{6,14},{7,15},{8,0},{9,1},... | collective-permute-start | bytes 258056 | tf_op jit(solution)/shard_map/ppermute | solution.py:566

commit v8 on v7

--- a/solution.py
+++ b/solution.py
@@ -15,6 +15,7 @@
 R2 = 4
 GROUP1 = 6
 GROUP2 = 8
+COPY_STEP = 0.1
 
 
 def lane_iota(rows):
@@ -394,8 +395,13 @@
         dphi = dphi + d.astype(F32) * extra[k][0:1]
         dsum = dsum + d.astype(F32)
     sums = [jnp.sum(v, axis=1, keepdims=True) for v in (dphi, dsum, gphi_ref[...])]
-    fill = jnp.zeros((chans, 128 - 3 * tails[0].shape[1] - 3), F32)
-    wire[2 * step : 2 * step + chans] = jnp.concatenate(tails + sums + [fill], axis=1)
+    base = 3 * tails[0].shape[1]
+    place = jnp.maximum(lane_iota(chans) - base, 0)
+    which = lax.rem(place, 3)
+    wide_sums = [jnp.broadcast_to(v, (chans, 128)) for v in sums]
+    coded = jnp.where(which == 0, wide_sums[0], jnp.where(which == 1, *wide_sums[1:]))
+    coded = coded * (1.0 + COPY_STEP * (place // 3).astype(F32))
+    wire[2 * step : 2 * step + chans] = jnp.concatenate(tails + [coded[:, base:]], axis=1)
     half = wire.shape[0] // 2
     core = lax.rem(lax.axis_index("gy"), 2)
     keep_ref[...] = wire[pl.ds(pl.multiple_of(core * half, 8), half), :]
@@ -501,7 +507,13 @@
         for k in range(3):
             w1_ref[2 - n, k] = wide[:, k * chans : (k + 1) * chans]
             w2_ref[k, 2 - n] = wide[:, step + k * chans : step + (k + 1) * chans]
-    cond_ref[...] = jnp.transpose(tail)[3 * rest_w : 3 * rest_w + 3, :chans]
+    turned = jnp.transpose(tail)[:, :chans]
+    copies = (128 - 3 * rest_w) // 3
+    total = jnp.zeros((3, chans), F32)
+    for j in range(copies):
+        at = 3 * (rest_w + j)
+        total = total + turned[at : at + 3] * (1.0 / (copies * (1.0 + COPY_STEP * j)))
+    cond_ref[...] = total
 
 
 def limit(mib):

time: 35.8 us -> 35.8 us (level)
  no operation moved by 1% of the time
where the time goes in v8:
time: 35.8 us; the launch traced here: 35.6 us
  Pallas kernels  15.3 us (43%)
  starting transfers between devices  13.8 us (39%)
  waiting for transfers between devices  5.63 us (16%)
  between operations  0.77 us (2%)
    ppermute x12, starting transfers between devices, send(): return lax.ppermute(value, axes, pairs)  13.8 us
    ppermute x12, waiting for transfers between devices, send(): return lax.ppermute(value, axes, pairs)  5.63 us
    pallas_call x2, Pallas kernels, output(): pl.pallas_call(lambda *refs: output_kernel(with_phi, *refs), out_shape=ja...  5.44 us
    pallas_call x1, Pallas kernels, local(): pl.pallas_call(hidden_kernel, out_shape=(inner, inner, acc, acc, jax.Shap...  3.06 us
    pallas_call x1, Pallas kernels, local(): pl.pallas_call(prep_kernel, out_shape=(field, edges, jax.ShapeDtypeStruct...  3 us
    pallas_call x1, Pallas kernels, local(): pl.pallas_call(row_kernel, out_shape=(edge, edge), in_specs=[hbm] * 4, sc...  1.27 us
    pallas_call x1, Pallas kernels, local(): pl.pallas_call(lambda *refs: unpack_kernel(factor, *refs), out_shape=(gra...  1.06 us
    pallas_call x1, Pallas kernels, local(): pl.pallas_call(lambda *refs: edge_kernel(rows, nx, *refs), out_shape=(col...  0.8 us
  transfers between devices with their start and end apart: 12, of which 4 were waited for; matrix products, arithmetic and copies ran while one was open for 0% of the time, Pallas kernels for 33%

profile of v8, /device:TPU:0, one launch (start us, length us, event | category | flops | bytes accessed | tf_op | source)
XLA Modules:
  0.0 35.6 jit_solution(7297464894358052466)
XLA Ops:
  0.6 1.3 %edge_rows.1 = (bf16[208,128]{1,0:T(8,128)(2,1)S(1)}, bf16[208,128]{1,0:T(8,128)(2,1)S(1)}) custom-call(bf16[48,64,128]{2,1,0:T(8,128)(2,1)} %refs_0_.4, bf16[48,64,128]{2,1,0:T(8,128)(2,1)} %refs_0_.5, bf16[64,128]{1,0:T(8,128)(2,1)} %phi_ref.1, s32[8,16]{1,0:T(8,128)} %mask_ref.1), custom_call_target="tpu_custom_call" | custom-call | tf_op jit(solution)/shard_map/edge_rows/pallas_call | solution.py:620
  1.9 0.5 %collective-permute-start = (bf16[208,128]{1,0:T(8,128)(2,1)S(1)}, bf16[208,128]{1,0:T(8,128)(2,1)S(1)}, u32[]{:S(2)}, u32[]{:S(2)}) collective-permute-start(bf16[208,128]{1,0:T(8,128)(2,1)S(1)} %get-tuple-element.48), channel_id=1, source_target_pairs={{0,8},{1,9},{2,10},{3,11},{4,12},{5,13},{6,14},{7,15},{8,0},{9,1},... | collective-permute-start | bytes 159752 | tf_op jit(solution)/shard_map/ppermute | solution.py:578
  2.4 2.6 %collective-permute-start.1 = (bf16[208,128]{1,0:T(8,128)(2,1)S(1)}, bf16[208,128]{1,0:T(8,128)(2,1)S(1)}, u32[]{:S(2)}, u32[]{:S(2)}) collective-permute-start(bf16[208,128]{1,0:T(8,128)(2,1)S(1)} %get-tuple-element.49), channel_id=1, source_target_pairs={{0,1},{1,0},{2,3},{3,2},{4,5},{5,4},{6,7},{7,6},{8,16},{9,17},{10,... | collective-permute-start | bytes 159752 | tf_op jit(solution)/shard_map/ppermute | solution.py:578
  5.0 3.0 %prep.1 = (bf16[2,9216,128]{2,1,0:T(8,128)(2,1)S(1)}, bf16[2,208,128]{2,1,0:T(8,128)(2,1)S(1)}, f32[48,128]{1,0:T(8,128)S(1)}, f32[64,128]{1,0:T(8,128)S(1)}, f3...) custom-call(bf16[48,64,128]{2,1,0:T(8,128)(2,1)} %refs_0_.4, ...), custom_call_target="tpu_custom_call" | custom-call | flops 1358954496 | bytes 8388608 | tf_op jit(solution)/shard_map/prep/pallas_call | solution.py:645
  8.0 0.0 collective-permute-done.refs_1_
  8.0 0.0 collective-permute-done.1.refs_2_
  8.0 0.3 edge_cols.1
  8.4 1.2 %collective-permute-start.2 = (bf16[208,128]{1,0:T(8,128)(2,1)S(1)}, bf16[208,128]{1,0:T(8,128)(2,1)S(1)}, u32[]{:S(2)}, u32[]{:S(2)}) collective-permute-start(bf16[208,128]{1,0:T(8,128)(2,1)S(1)} %get-tuple-element.50), channel_id=1, source_target_pairs={{0,1},{1,0},{2,3},{3,2},{4,5},{5,4},{6,7},{7,6},{8,9},{9,8},{10,11... | collective-permute-start | bytes 159752 | tf_op jit(solution)/shard_map/ppermute | solution.py:578
  9.5 0.2 collective-permute-start.3
  9.8 3.1 %hidden.1 = (bf16[3168,128]{1,0:T(8,128)(2,1)S(1)}, bf16[3168,128]{1,0:T(8,128)(2,1)S(1)}, f32[144,144]{1,0:T(8,128)S(1)}, f32[144,144]{1,0:T(8,128)S(1)}, f32[2,48,128]{2,1,0:T(8,128)S(1)}) custom-call(bf16[2,9216,128]{2,1,0:T(8,128)(2,1)S(1)} %get-tuple-element.56.a3, f32[64,128]{1,0:T(8,128)S(1)} %get-tuple-element.57.phi_own.refs_1_, ...), custom_call_target="tpu_custom_call" | custom-call | flops 2717908992 | bytes 8388608 | tf_op jit(solution)/shard_map/hidden/pallas_call | solution.py:672
  12.8 0.0 collective-permute-done.2.refs_0_
  12.8 0.0 collective-permute-done.3.refs_1_
  12.8 0.8 %edge_parts.1 = (bf16[48,512]{1,0:T(8,128)(2,1)S(1)}, bf16[48,512]{1,0:T(8,128)(2,1)S(1)}, f32[168,128]{1,0:T(8,128)S(1)}, f32[168,128]{1,0:T(8,128)S(1)}) custom-call(bf16[208,128]{1,0:T(8,128)(2,1)S(1)} %collective-permute-done.2.refs_0_, bf16[208,128]{1,0:T(8,128)(2,1)S(1)} %collective-permute-done.3.refs_1_, ...), custom_call_target="tpu_custom_call" | custom-call | tf_op jit(solution)/shard_map/edge_parts/pallas_call | solution.py:692
  13.6 0.3 collective-permute-start.4
  14.0 0.4 %edge_fixes.1 = (f32[192,128]{1,0:T(8,128)S(1)}, f32[192,128]{1,0:T(8,128)S(1)}) custom-call(bf16[48,432]{1,0:T(8,128)(2,1)S(1)} %get-tuple-element.68.refs_0_, bf16[48,432]{1,0:T(8,128)(2,1)S(1)} %get-tuple-element.69.refs_1_, bf16[48,512]{1,0:T(8,128)(2,1)S(1)} %get-tuple-element.70.refs_2_, bf16[48,512]{1,0:T(8,128)(2,1)S(1)} %get-tuple-element.71.refs_3_), custom_call_target="tpu_custom_call" | custom-call | flops 169869312 | bytes 1048576 | tf_op jit(solution)/shard_map/edge_fixes/pallas_call | solution.py:699
  14.4 0.6 %collective-permute-done.4 = f32[168,128]{1,0:T(8,128)S(1)} collective-permute-done((f32[168,128]{1,0:T(8,128)S(1)}, f32[168,128]{1,0:T(8,128)S(1)}, u32[]{:S(2)}, u32[]{:S(2)}) %collective-permute-start.4) | collective-permute-done | bytes 86048 | tf_op jit(solution)/shard_map/ppermute | solution.py:578
  15.0 2.9 %collective-permute-start.6 = (bf16[168,128]{1,0:T(8,128)(2,1)S(1)}, bf16[168,128]{1,0:T(8,128)(2,1)S(1)}, u32[]{:S(2)}, u32[]{:S(2)}) collective-permute-start(bf16[168,128]{1,0:T(8,128)(2,1)S(1)} %add.21), channel_id=1, source_target_pairs={{0,1},{1,0},{2,3},{3,2},{4,5},{5,4},{6,7},{7,6},{8,9},{9,8},{10,11... | collective-permute-start | bytes 129032 | tf_op jit(solution)/shard_map/ppermute | solution.py:578
  17.9 1.0 %collective-permute-start.5 = (bf16[168,128]{1,0:T(8,128)(2,1)S(1)}, bf16[168,128]{1,0:T(8,128)(2,1)S(1)}, u32[]{:S(2)}, u32[]{:S(2)}) collective-permute-start(bf16[168,128]{1,0:T(8,128)(2,1)S(1)} %add.21), channel_id=1, source_target_pairs={{0,16},{1,17},{2,18},{3,19},{4,20},{5,21},{6,22},{7,23},{8,24},{9,... | collective-permute-start | bytes 129032 | tf_op jit(solution)/shard_map/ppermute | solution.py:578
  18.8 0.6 %collective-permute-start.7 = (bf16[168,128]{1,0:T(8,128)(2,1)S(1)}, bf16[168,128]{1,0:T(8,128)(2,1)S(1)}, u32[]{:S(2)}, u32[]{:S(2)}) collective-permute-start(bf16[168,128]{1,0:T(8,128)(2,1)S(1)} %add.21), channel_id=1, source_target_pairs={{0,17},{1,16},{2,19},{3,18},{4,21},{5,20},{6,23},{7,22},{8,25},{9,... | collective-permute-start | bytes 129032 | tf_op jit(solution)/shard_map/ppermute | solution.py:578
  19.4 2.7 %delensed.1 = bf16[48,64,128]{2,1,0:T(8,128)(2,1)} custom-call(bf16[48,64,128]{2,1,0:T(8,128)(2,1)} %refs_0_.4, f32[64,128]{1,0:T(8,128)S(1)} %get-tuple-element.57.phi_own.refs_1_, f32[64,128]{1,0:T(8,128)S(1)} %get-tuple-element.58.mask_own.refs_2_, bf16[3168,128]{1,0:T(8,128)(2,1)S(1)} %get-tuple-element.74.refs_3_, ...), custom_call_target="tpu_custom_call" | custom-call | flops 679477248 | bytes 4194304 | tf_op jit(solution)/shard_map/delensed/pallas_call | solution.py:710
  22.2 0.0 collective-permute-done.6
  22.2 0.0 collective-permute-done.5
  22.2 1.6 %collective-permute-done.7 = bf16[168,128]{1,0:T(8,128)(2,1)S(1)} collective-permute-done((bf16[168,128]{1,0:T(8,128)(2,1)S(1)}, bf16[168,128]{1,0:T(8,128)(2,1)S(1)}, u32[]{:S(2)}, u32[]{:S(2)}) %collective-permute-start.7) | collective-permute-done | bytes 43040 | tf_op jit(solution)/shard_map/ppermute | solution.py:578
  23.8 2.7 %collective-permute-start.9 = (bf16[168,128]{1,0:T(8,128)(2,1)S(1)}, bf16[168,128]{1,0:T(8,128)(2,1)S(1)}, u32[]{:S(2)}, u32[]{:S(2)}) collective-permute-start(bf16[168,128]{1,0:T(8,128)(2,1)S(1)} %add_add_fusion.1), channel_id=1, source_target_pairs={{0,4},{1,5},{2,6},{3,7},{4,0},{5,1},{6,2},{7,3},{8,12},{9,13},{10,... | collective-permute-start | bytes 129032 | tf_op jit(solution)/shard_map/ppermute | solution.py:578
  26.5 0.9 %collective-permute-start.8 = (bf16[168,128]{1,0:T(8,128)(2,1)S(1)}, bf16[168,128]{1,0:T(8,128)(2,1)S(1)}, u32[]{:S(2)}, u32[]{:S(2)}) collective-permute-start(bf16[168,128]{1,0:T(8,128)(2,1)S(1)} %add_add_fusion.1), channel_id=1, source_target_pairs={{0,2},{1,3},{2,0},{3,1},{4,6},{5,7},{6,4},{7,5},{8,10},{9,11},{10,... | collective-permute-start | bytes 129032 | tf_op jit(solution)/shard_map/ppermute | solution.py:578
  27.3 0.9 %collective-permute-start.10 = (bf16[168,128]{1,0:T(8,128)(2,1)S(1)}, bf16[168,128]{1,0:T(8,128)(2,1)S(1)}, u32[]{:S(2)}, u32[]{:S(2)}) collective-permute-start(bf16[168,128]{1,0:T(8,128)(2,1)S(1)} %add_add_fusion.1), channel_id=1, source_target_pairs={{0,6},{1,7},{2,4},{3,5},{4,2},{5,3},{6,0},{7,1},{8,14},{9,15},{10,... | collective-permute-start | bytes 129032 | tf_op jit(solution)/shard_map/ppermute | solution.py:578
  28.3 2.7 %grad_input.1 = bf16[48,64,128]{2,1,0:T(8,128)(2,1)} custom-call(bf16[48,64,128]{2,1,0:T(8,128)(2,1)} %refs_0_.5, f32[64,128]{1,0:T(8,128)S(1)} %get-tuple-element.57.phi_own.refs_1_, f32[64,128]{1,0:T(8,128)S(1)} %get-tuple-element.58.mask_own.refs_2_, bf16[3168,128]{1,0:T(8,128)(2,1)S(1)} %get-tuple-element.81.refs_3_, ...), custom_call_target="tpu_custom_call" | custom-call | flops 679477248 | bytes 4194304 | tf_op jit(solution)/shard_map/grad_input/pallas_call | solution.py:710
  31.0 0.0 collective-permute-done.8
  31.0 2.1 %collective-permute-done.10 = bf16[168,128]{1,0:T(8,128)(2,1)S(1)} collective-permute-done((bf16[168,128]{1,0:T(8,128)(2,1)S(1)}, bf16[168,128]{1,0:T(8,128)(2,1)S(1)}, u32[]{:S(2)}, u32[]{:S(2)}) %collective-permute-start.10) | collective-permute-done | bytes 43040 | tf_op jit(solution)/shard_map/ppermute | solution.py:578
  33.2 0.1 collective-permute-start.11
  33.2 1.3 %collective-permute-done.11.refs_1_ = f32[168,128]{1,0:T(8,128)S(1)} collective-permute-done((f32[168,128]{1,0:T(8,128)S(1)}, f32[168,128]{1,0:T(8,128)S(1)}, u32[]{:S(2)}, u32[]{:S(2)}) %collective-permute-start.11) | collective-permute-done | bytes 86048 | tf_op jit(solution)/shard_map/ppermute | solution.py:578
  34.5 1.1 %unpack.1 = (f32[3,3,48,48]{3,2,1,0:T(8,128)}, f32[3,3,48,48]{3,2,1,0:T(8,128)}, f32[3,48]{1,0:T(4,128)}) custom-call(f32[168,128]{1,0:T(8,128)S(1)} %add_add_fusion.refs_0_, f32[168,128]{1,0:T(8,128)S(1)} %collective-permute-done.11.refs_1_), custom_call_target="tpu_custom_call" | custom-call | tf_op jit(solution)/shard_map/unpack/pallas_call | solution.py:748
  (4 shorter events, 0.1 us)
Async XLA Ops:
  1.9 6.1 %collective-permute-start = (bf16[208,128]{1,0:T(8,128)(2,1)S(1)}, bf16[208,128]{1,0:T(8,128)(2,1)S(1)}, u32[]{:S(2)}, u32[]{:S(2)}) collective-permute-start(bf16[208,128]{1,0:T(8,128)(2,1)S(1)} %get-tuple-element.48), channel_id=1, source_target_pairs={{0,8},{1,9},{2,10},{3,11},{4,12},{5,13},{6,14},{7,15},{8,0},{9,1},... | collective-permute-start | bytes 159752 | tf_op jit(solution)/shard_map/ppermute | solution.py:578
  2.4 5.6 %collective-permute-start.1 = (bf16[208,128]{1,0:T(8,128)(2,1)S(1)}, bf16[208,128]{1,0:T(8,128)(2,1)S(1)}, u32[]{:S(2)}, u32[]{:S(2)}) collective-permute-start(bf16[208,128]{1,0:T(8,128)(2,1)S(1)} %get-tuple-element.49), channel_id=1, source_target_pairs={{0,1},{1,0},{2,3},{3,2},{4,5},{5,4},{6,7},{7,6},{8,16},{9,17},{10,... | collective-permute-start | bytes 159752 | tf_op jit(solution)/shard_map/ppermute | solution.py:578
  8.4 4.5 %collective-permute-start.2 = (bf16[208,128]{1,0:T(8,128)(2,1)S(1)}, bf16[208,128]{1,0:T(8,128)(2,1)S(1)}, u32[]{:S(2)}, u32[]{:S(2)}) collective-permute-start(bf16[208,128]{1,0:T(8,128)(2,1)S(1)} %get-tuple-element.50), channel_id=1, source_target_pairs={{0,1},{1,0},{2,3},{3,2},{4,5},{5,4},{6,7},{7,6},{8,9},{9,8},{10,11... | collective-permute-start | bytes 159752 | tf_op jit(solution)/shard_map/ppermute | solution.py:578
  9.5 3.3 %collective-permute-start.3 = (bf16[208,128]{1,0:T(8,128)(2,1)S(1)}, bf16[208,128]{1,0:T(8,128)(2,1)S(1)}, u32[]{:S(2)}, u32[]{:S(2)}) collective-permute-start(bf16[208,128]{1,0:T(8,128)(2,1)S(1)} %get-tuple-element.51), channel_id=1, source_target_pairs={{0,8},{1,2},{2,1},{3,4},{4,3},{5,6},{6,5},{7,15},{8,0},{9,10},{10,... | collective-permute-start | bytes 159752 | tf_op jit(solution)/shard_map/ppermute | solution.py:578
  13.6 1.3 %collective-permute-start.4 = (f32[168,128]{1,0:T(8,128)S(1)}, f32[168,128]{1,0:T(8,128)S(1)}, u32[]{:S(2)}, u32[]{:S(2)}) collective-permute-start(f32[168,128]{1,0:T(8,128)S(1)} %get-tuple-element.67), channel_id=1, source_target_pairs={{0,8},{1,9},{2,10},{3,11},{4,12},{5,13},{6,14},{7,15},{8,0},{9,1},... | collective-permute-start | bytes 258056 | tf_op jit(solution)/shard_map/ppermute | solution.py:578
  15.0 7.2 %collective-permute-start.6 = (bf16[168,128]{1,0:T(8,128)(2,1)S(1)}, bf16[168,128]{1,0:T(8,128)(2,1)S(1)}, u32[]{:S(2)}, u32[]{:S(2)}) collective-permute-start(bf16[168,128]{1,0:T(8,128)(2,1)S(1)} %add.21), channel_id=1, source_target_pairs={{0,1},{1,0},{2,3},{3,2},{4,5},{5,4},{6,7},{7,6},{8,9},{9,8},{10,11... | collective-permute-start | bytes 129032 | tf_op jit(solution)/shard_map/ppermute | solution.py:578
  17.9 4.3 %collective-permute-start.5 = (bf16[168,128]{1,0:T(8,128)(2,1)S(1)}, bf16[168,128]{1,0:T(8,128)(2,1)S(1)}, u32[]{:S(2)}, u32[]{:S(2)}) collective-permute-start(bf16[168,128]{1,0:T(8,128)(2,1)S(1)} %add.21), channel_id=1, source_target_pairs={{0,16},{1,17},{2,18},{3,19},{4,20},{5,21},{6,22},{7,23},{8,24},{9,... | collective-permute-start | bytes 129032 | tf_op jit(solution)/shard_map/ppermute | solution.py:578
  18.8 4.9 %collective-permute-start.7 = (bf16[168,128]{1,0:T(8,128)(2,1)S(1)}, bf16[168,128]{1,0:T(8,128)(2,1)S(1)}, u32[]{:S(2)}, u32[]{:S(2)}) collective-permute-start(bf16[168,128]{1,0:T(8,128)(2,1)S(1)} %add.21), channel_id=1, source_target_pairs={{0,17},{1,16},{2,19},{3,18},{4,21},{5,20},{6,23},{7,22},{8,25},{9,... | collective-permute-start | bytes 129032 | tf_op jit(solution)/shard_map/ppermute | solution.py:578
  23.8 7.2 %collective-permute-start.9 = (bf16[168,128]{1,0:T(8,128)(2,1)S(1)}, bf16[168,128]{1,0:T(8,128)(2,1)S(1)}, u32[]{:S(2)}, u32[]{:S(2)}) collective-permute-start(bf16[168,128]{1,0:T(8,128)(2,1)S(1)} %add_add_fusion.1), channel_id=1, source_target_pairs={{0,4},{1,5},{2,6},{3,7},{4,0},{5,1},{6,2},{7,3},{8,12},{9,13},{10,... | collective-permute-start | bytes 129032 | tf_op jit(solution)/shard_map/ppermute | solution.py:578
  26.5 4.5 %collective-permute-start.8 = (bf16[168,128]{1,0:T(8,128)(2,1)S(1)}, bf16[168,128]{1,0:T(8,128)(2,1)S(1)}, u32[]{:S(2)}, u32[]{:S(2)}) collective-permute-start(bf16[168,128]{1,0:T(8,128)(2,1)S(1)} %add_add_fusion.1), channel_id=1, source_target_pairs={{0,2},{1,3},{2,0},{3,1},{4,6},{5,7},{6,4},{7,5},{8,10},{9,11},{10,... | collective-permute-start | bytes 129032 | tf_op jit(solution)/shard_map/ppermute | solution.py:578
  27.3 5.8 %collective-permute-start.10 = (bf16[168,128]{1,0:T(8,128)(2,1)S(1)}, bf16[168,128]{1,0:T(8,128)(2,1)S(1)}, u32[]{:S(2)}, u32[]{:S(2)}) collective-permute-start(bf16[168,128]{1,0:T(8,128)(2,1)S(1)} %add_add_fusion.1), channel_id=1, source_target_pairs={{0,6},{1,7},{2,4},{3,5},{4,2},{5,3},{6,0},{7,1},{8,14},{9,15},{10,... | collective-permute-start | bytes 129032 | tf_op jit(solution)/shard_map/ppermute | solution.py:578
  33.2 1.3 %collective-permute-start.11 = (f32[168,128]{1,0:T(8,128)S(1)}, f32[168,128]{1,0:T(8,128)S(1)}, u32[]{:S(2)}, u32[]{:S(2)}) collective-permute-start(f32[168,128]{1,0:T(8,128)S(1)} %add_add_fusion.refs_0_), channel_id=1, source_target_pairs={{0,8},{1,9},{2,10},{3,11},{4,12},{5,13},{6,14},{7,15},{8,0},{9,1},... | collective-permute-start | bytes 258056 | tf_op jit(solution)/shard_map/ppermute | solution.py:578

commit v9 on v8

--- a/solution.py
+++ b/solution.py
@@ -597,7 +597,7 @@
             return sent.astype(F32) + got[0]
         both = (moves[0][0] ^ moves[1][0], moves[0][1] ^ moves[1][1])
         far = send(sent, lambda a, b: (a ^ both[0], b ^ both[1])).astype(F32)
-        return (sent.astype(F32) + got[0]) + (got[1] + far)
+        return (sent.astype(F32) + got[0]) + (far + got[1])
 
     def local(
         sky, lens_phi, cotangent, tile_mask, weight_one, weight_two, cond_one, bias_one, cond_two

time: 35.8 us -> 34.3 us (0.958)
  waiting for transfers between devices: 5.63 us -> 4.25 us
    ppermute x12, waiting for transfers between devices: 5.63 us -> 4.25 us  [send(): return lax.ppermute(value, axes, pairs)]
  transfers between devices with their start and end apart: 12 -> 12, of which waited for: 4 -> 6; matrix products, arithmetic and copies ran while one was open for 0% -> 0% of each run, Pallas kernels for 33% -> 35%
where the time goes in v9:
time: 34.3 us; the launch traced here: 34.1 us
  Pallas kernels  15.3 us (45%)
  starting transfers between devices  13.7 us (40%)
  waiting for transfers between devices  4.25 us (12%)
  between operations  0.76 us (2%)
    ppermute x12, starting transfers between devices, send(): return lax.ppermute(value, axes, pairs)  13.7 us
    pallas_call x2, Pallas kernels, output(): pl.pallas_call(lambda *refs: output_kernel(with_phi, *refs), out_shape=ja...  5.44 us
    ppermute x12, waiting for transfers between devices, send(): return lax.ppermute(value, axes, pairs)  4.25 us
    pallas_call x1, Pallas kernels, local(): pl.pallas_call(hidden_kernel, out_shape=(inner, inner, acc, acc, jax.Shap...  3.06 us
    pallas_call x1, Pallas kernels, local(): pl.pallas_call(prep_kernel, out_shape=(field, edges, jax.ShapeDtypeStruct...  3 us
    pallas_call x1, Pallas kernels, local(): pl.pallas_call(row_kernel, out_shape=(edge, edge), in_specs=[hbm] * 4, sc...  1.27 us
    pallas_call x1, Pallas kernels, local(): pl.pallas_call(lambda *refs: unpack_kernel(factor, *refs), out_shape=(gra...  1.06 us
    pallas_call x1, Pallas kernels, local(): pl.pallas_call(lambda *refs: edge_kernel(rows, nx, *refs), out_shape=(col...  0.8 us
  transfers between devices with their start and end apart: 12, of which 6 were waited for; matrix products, arithmetic and copies ran while one was open for 0% of the time, Pallas kernels for 35%

profile of v9, /device:TPU:0, one launch (start us, length us, event | category | flops | bytes accessed | tf_op | source)
XLA Modules:
  0.0 34.1 jit_solution(15519620889982742175)
XLA Ops:
  0.6 1.3 %edge_rows.1 = (bf16[208,128]{1,0:T(8,128)(2,1)S(1)}, bf16[208,128]{1,0:T(8,128)(2,1)S(1)}) custom-call(bf16[48,64,128]{2,1,0:T(8,128)(2,1)} %refs_0_.4, bf16[48,64,128]{2,1,0:T(8,128)(2,1)} %refs_0_.5, bf16[64,128]{1,0:T(8,128)(2,1)} %phi_ref.1, s32[8,16]{1,0:T(8,128)} %mask_ref.1), custom_call_target="tpu_custom_call" | custom-call | tf_op jit(solution)/shard_map/edge_rows/pallas_call | solution.py:620
  1.9 0.5 %collective-permute-start = (bf16[208,128]{1,0:T(8,128)(2,1)S(1)}, bf16[208,128]{1,0:T(8,128)(2,1)S(1)}, u32[]{:S(2)}, u32[]{:S(2)}) collective-permute-start(bf16[208,128]{1,0:T(8,128)(2,1)S(1)} %get-tuple-element.48), channel_id=1, source_target_pairs={{0,8},{1,9},{2,10},{3,11},{4,12},{5,13},{6,14},{7,15},{8,0},{9,1},... | collective-permute-start | bytes 159752 | tf_op jit(solution)/shard_map/ppermute | solution.py:578
  2.4 2.6 %collective-permute-start.1 = (bf16[208,128]{1,0:T(8,128)(2,1)S(1)}, bf16[208,128]{1,0:T(8,128)(2,1)S(1)}, u32[]{:S(2)}, u32[]{:S(2)}) collective-permute-start(bf16[208,128]{1,0:T(8,128)(2,1)S(1)} %get-tuple-element.49), channel_id=1, source_target_pairs={{0,1},{1,0},{2,3},{3,2},{4,5},{5,4},{6,7},{7,6},{8,16},{9,17},{10,... | collective-permute-start | bytes 159752 | tf_op jit(solution)/shard_map/ppermute | solution.py:578
  5.0 3.0 %prep.1 = (bf16[2,9216,128]{2,1,0:T(8,128)(2,1)S(1)}, bf16[2,208,128]{2,1,0:T(8,128)(2,1)S(1)}, f32[48,128]{1,0:T(8,128)S(1)}, f32[64,128]{1,0:T(8,128)S(1)}, f3...) custom-call(bf16[48,64,128]{2,1,0:T(8,128)(2,1)} %refs_0_.4, ...), custom_call_target="tpu_custom_call" | custom-call | flops 1358954496 | bytes 8388608 | tf_op jit(solution)/shard_map/prep/pallas_call | solution.py:645
  8.0 0.0 collective-permute-done.refs_1_
  8.0 0.0 collective-permute-done.1.refs_2_
  8.0 0.3 edge_cols.1
  8.4 1.2 %collective-permute-start.2 = (bf16[208,128]{1,0:T(8,128)(2,1)S(1)}, bf16[208,128]{1,0:T(8,128)(2,1)S(1)}, u32[]{:S(2)}, u32[]{:S(2)}) collective-permute-start(bf16[208,128]{1,0:T(8,128)(2,1)S(1)} %get-tuple-element.50), channel_id=1, source_target_pairs={{0,1},{1,0},{2,3},{3,2},{4,5},{5,4},{6,7},{7,6},{8,9},{9,8},{10,11... | collective-permute-start | bytes 159752 | tf_op jit(solution)/shard_map/ppermute | solution.py:578
  9.5 0.2 collective-permute-start.3
  9.8 3.1 %hidden.1 = (bf16[3168,128]{1,0:T(8,128)(2,1)S(1)}, bf16[3168,128]{1,0:T(8,128)(2,1)S(1)}, f32[144,144]{1,0:T(8,128)S(1)}, f32[144,144]{1,0:T(8,128)S(1)}, f32[2,48,128]{2,1,0:T(8,128)S(1)}) custom-call(bf16[2,9216,128]{2,1,0:T(8,128)(2,1)S(1)} %get-tuple-element.56.a3, f32[64,128]{1,0:T(8,128)S(1)} %get-tuple-element.57.phi_own.refs_1_, ...), custom_call_target="tpu_custom_call" | custom-call | flops 2717908992 | bytes 8388608 | tf_op jit(solution)/shard_map/hidden/pallas_call | solution.py:672
  12.8 0.0 collective-permute-done.2.refs_0_
  12.8 0.0 collective-permute-done.3.refs_1_
  12.8 0.8 %edge_parts.1 = (bf16[48,512]{1,0:T(8,128)(2,1)S(1)}, bf16[48,512]{1,0:T(8,128)(2,1)S(1)}, f32[168,128]{1,0:T(8,128)S(1)}, f32[168,128]{1,0:T(8,128)S(1)}) custom-call(bf16[208,128]{1,0:T(8,128)(2,1)S(1)} %collective-permute-done.2.refs_0_, bf16[208,128]{1,0:T(8,128)(2,1)S(1)} %collective-permute-done.3.refs_1_, ...), custom_call_target="tpu_custom_call" | custom-call | tf_op jit(solution)/shard_map/edge_parts/pallas_call | solution.py:692
  13.6 0.3 %collective-permute-start.4 = (f32[168,128]{1,0:T(8,128)S(1)}, f32[168,128]{1,0:T(8,128)S(1)}, u32[]{:S(2)}, u32[]{:S(2)}) collective-permute-start(f32[168,128]{1,0:T(8,128)S(1)} %get-tuple-element.67), channel_id=1, source_target_pairs={{0,8},{1,9},{2,10},{3,11},{4,12},{5,13},{6,14},{7,15},{8,0},{9,1},... | collective-permute-start | bytes 258056 | tf_op jit(solution)/shard_map/ppermute | solution.py:578
  14.0 0.4 %edge_fixes.1 = (f32[192,128]{1,0:T(8,128)S(1)}, f32[192,128]{1,0:T(8,128)S(1)}) custom-call(bf16[48,432]{1,0:T(8,128)(2,1)S(1)} %get-tuple-element.68.refs_0_, bf16[48,432]{1,0:T(8,128)(2,1)S(1)} %get-tuple-element.69.refs_1_, bf16[48,512]{1,0:T(8,128)(2,1)S(1)} %get-tuple-element.70.refs_2_, bf16[48,512]{1,0:T(8,128)(2,1)S(1)} %get-tuple-element.71.refs_3_), custom_call_target="tpu_custom_call" | custom-call | flops 169869312 | bytes 1048576 | tf_op jit(solution)/shard_map/edge_fixes/pallas_call | solution.py:699
  14.4 0.6 %collective-permute-done.4 = f32[168,128]{1,0:T(8,128)S(1)} collective-permute-done((f32[168,128]{1,0:T(8,128)S(1)}, f32[168,128]{1,0:T(8,128)S(1)}, u32[]{:S(2)}, u32[]{:S(2)}) %collective-permute-start.4) | collective-permute-done | bytes 86048 | tf_op jit(solution)/shard_map/ppermute | solution.py:578
  15.0 3.3 %collective-permute-start.6 = (bf16[168,128]{1,0:T(8,128)(2,1)S(1)}, bf16[168,128]{1,0:T(8,128)(2,1)S(1)}, u32[]{:S(2)}, u32[]{:S(2)}) collective-permute-start(bf16[168,128]{1,0:T(8,128)(2,1)S(1)} %add.21), channel_id=1, source_target_pairs={{0,17},{1,16},{2,19},{3,18},{4,21},{5,20},{6,23},{7,22},{8,25},{9,... | collective-permute-start | bytes 129032 | tf_op jit(solution)/shard_map/ppermute | solution.py:578
  18.3 1.1 %collective-permute-start.5 = (bf16[168,128]{1,0:T(8,128)(2,1)S(1)}, bf16[168,128]{1,0:T(8,128)(2,1)S(1)}, u32[]{:S(2)}, u32[]{:S(2)}) collective-permute-start(bf16[168,128]{1,0:T(8,128)(2,1)S(1)} %add.21), channel_id=1, source_target_pairs={{0,16},{1,17},{2,18},{3,19},{4,20},{5,21},{6,22},{7,23},{8,24},{9,... | collective-permute-start | bytes 129032 | tf_op jit(solution)/shard_map/ppermute | solution.py:578
  19.3 0.0 collective-permute-start.7
  19.3 2.7 %delensed.1 = bf16[48,64,128]{2,1,0:T(8,128)(2,1)} custom-call(bf16[48,64,128]{2,1,0:T(8,128)(2,1)} %refs_0_.4, f32[64,128]{1,0:T(8,128)S(1)} %get-tuple-element.57.phi_own.refs_1_, f32[64,128]{1,0:T(8,128)S(1)} %get-tuple-element.58.mask_own.refs_2_, bf16[3168,128]{1,0:T(8,128)(2,1)S(1)} %get-tuple-element.74.refs_3_, ...), custom_call_target="tpu_custom_call" | custom-call | flops 679477248 | bytes 4194304 | tf_op jit(solution)/shard_map/delensed/pallas_call | solution.py:710
  22.1 0.2 collective-permute-done.5
  22.3 1.1 %collective-permute-done.7 = bf16[168,128]{1,0:T(8,128)(2,1)S(1)} collective-permute-done((bf16[168,128]{1,0:T(8,128)(2,1)S(1)}, bf16[168,128]{1,0:T(8,128)(2,1)S(1)}, u32[]{:S(2)}, u32[]{:S(2)}) %collective-permute-start.7) | collective-permute-done | bytes 43040 | tf_op jit(solution)/shard_map/ppermute | solution.py:578
  23.4 3.3 %collective-permute-start.9 = (bf16[168,128]{1,0:T(8,128)(2,1)S(1)}, bf16[168,128]{1,0:T(8,128)(2,1)S(1)}, u32[]{:S(2)}, u32[]{:S(2)}) collective-permute-start(bf16[168,128]{1,0:T(8,128)(2,1)S(1)} %add_add_fusion.1), channel_id=1, source_target_pairs={{0,6},{1,7},{2,4},{3,5},{4,2},{5,3},{6,0},{7,1},{8,14},{9,15},{10,... | collective-permute-start | bytes 129032 | tf_op jit(solution)/shard_map/ppermute | solution.py:578
  26.7 0.0 collective-permute-start.8
  26.8 1.1 %collective-permute-start.10 = (bf16[168,128]{1,0:T(8,128)(2,1)S(1)}, bf16[168,128]{1,0:T(8,128)(2,1)S(1)}, u32[]{:S(2)}, u32[]{:S(2)}) collective-permute-start(bf16[168,128]{1,0:T(8,128)(2,1)S(1)} %add_add_fusion.1), channel_id=1, source_target_pairs={{0,4},{1,5},{2,6},{3,7},{4,0},{5,1},{6,2},{7,3},{8,12},{9,13},{10,... | collective-permute-start | bytes 129032 | tf_op jit(solution)/shard_map/ppermute | solution.py:578
  27.9 2.7 %grad_input.1 = bf16[48,64,128]{2,1,0:T(8,128)(2,1)} custom-call(bf16[48,64,128]{2,1,0:T(8,128)(2,1)} %refs_0_.5, f32[64,128]{1,0:T(8,128)S(1)} %get-tuple-element.57.phi_own.refs_1_, f32[64,128]{1,0:T(8,128)S(1)} %get-tuple-element.58.mask_own.refs_2_, bf16[3168,128]{1,0:T(8,128)(2,1)S(1)} %get-tuple-element.81.refs_3_, ...), custom_call_target="tpu_custom_call" | custom-call | flops 679477248 | bytes 4194304 | tf_op jit(solution)/shard_map/grad_input/pallas_call | solution.py:710
  30.6 0.0 collective-permute-done.9
  30.6 0.2 collective-permute-done.8
  30.8 0.9 %collective-permute-done.10 = bf16[168,128]{1,0:T(8,128)(2,1)S(1)} collective-permute-done((bf16[168,128]{1,0:T(8,128)(2,1)S(1)}, bf16[168,128]{1,0:T(8,128)(2,1)S(1)}, u32[]{:S(2)}, u32[]{:S(2)}) %collective-permute-start.10) | collective-permute-done | bytes 43040 | tf_op jit(solution)/shard_map/ppermute | solution.py:578
  31.7 0.1 collective-permute-start.11
  31.8 1.3 %collective-permute-done.11.refs_1_ = f32[168,128]{1,0:T(8,128)S(1)} collective-permute-done((f32[168,128]{1,0:T(8,128)S(1)}, f32[168,128]{1,0:T(8,128)S(1)}, u32[]{:S(2)}, u32[]{:S(2)}) %collective-permute-start.11) | collective-permute-done | bytes 86048 | tf_op jit(solution)/shard_map/ppermute | solution.py:578
  33.1 1.1 %unpack.1 = (f32[3,3,48,48]{3,2,1,0:T(8,128)}, f32[3,3,48,48]{3,2,1,0:T(8,128)}, f32[3,48]{1,0:T(4,128)}) custom-call(f32[168,128]{1,0:T(8,128)S(1)} %add_add_fusion.refs_0_, f32[168,128]{1,0:T(8,128)S(1)} %collective-permute-done.11.refs_1_), custom_call_target="tpu_custom_call" | custom-call | tf_op jit(solution)/shard_map/unpack/pallas_call | solution.py:748
  (4 shorter events, 0.1 us)
Async XLA Ops:
  1.9 6.1 %collective-permute-start = (bf16[208,128]{1,0:T(8,128)(2,1)S(1)}, bf16[208,128]{1,0:T(8,128)(2,1)S(1)}, u32[]{:S(2)}, u32[]{:S(2)}) collective-permute-start(bf16[208,128]{1,0:T(8,128)(2,1)S(1)} %get-tuple-element.48), channel_id=1, source_target_pairs={{0,8},{1,9},{2,10},{3,11},{4,12},{5,13},{6,14},{7,15},{8,0},{9,1},... | collective-permute-start | bytes 159752 | tf_op jit(solution)/shard_map/ppermute | solution.py:578
  2.4 5.6 %collective-permute-start.1 = (bf16[208,128]{1,0:T(8,128)(2,1)S(1)}, bf16[208,128]{1,0:T(8,128)(2,1)S(1)}, u32[]{:S(2)}, u32[]{:S(2)}) collective-permute-start(bf16[208,128]{1,0:T(8,128)(2,1)S(1)} %get-tuple-element.49), channel_id=1, source_target_pairs={{0,1},{1,0},{2,3},{3,2},{4,5},{5,4},{6,7},{7,6},{8,16},{9,17},{10,... | collective-permute-start | bytes 159752 | tf_op jit(solution)/shard_map/ppermute | solution.py:578
  8.4 4.5 %collective-permute-start.2 = (bf16[208,128]{1,0:T(8,128)(2,1)S(1)}, bf16[208,128]{1,0:T(8,128)(2,1)S(1)}, u32[]{:S(2)}, u32[]{:S(2)}) collective-permute-start(bf16[208,128]{1,0:T(8,128)(2,1)S(1)} %get-tuple-element.50), channel_id=1, source_target_pairs={{0,1},{1,0},{2,3},{3,2},{4,5},{5,4},{6,7},{7,6},{8,9},{9,8},{10,11... | collective-permute-start | bytes 159752 | tf_op jit(solution)/shard_map/ppermute | solution.py:578
  9.5 3.3 %collective-permute-start.3 = (bf16[208,128]{1,0:T(8,128)(2,1)S(1)}, bf16[208,128]{1,0:T(8,128)(2,1)S(1)}, u32[]{:S(2)}, u32[]{:S(2)}) collective-permute-start(bf16[208,128]{1,0:T(8,128)(2,1)S(1)} %get-tuple-element.51), channel_id=1, source_target_pairs={{0,8},{1,2},{2,1},{3,4},{4,3},{5,6},{6,5},{7,15},{8,0},{9,10},{10,... | collective-permute-start | bytes 159752 | tf_op jit(solution)/shard_map/ppermute | solution.py:578
  13.6 1.3 %collective-permute-start.4 = (f32[168,128]{1,0:T(8,128)S(1)}, f32[168,128]{1,0:T(8,128)S(1)}, u32[]{:S(2)}, u32[]{:S(2)}) collective-permute-start(f32[168,128]{1,0:T(8,128)S(1)} %get-tuple-element.67), channel_id=1, source_target_pairs={{0,8},{1,9},{2,10},{3,11},{4,12},{5,13},{6,14},{7,15},{8,0},{9,1},... | collective-permute-start | bytes 258056 | tf_op jit(solution)/shard_map/ppermute | solution.py:578
  15.0 7.1 %collective-permute-start.6 = (bf16[168,128]{1,0:T(8,128)(2,1)S(1)}, bf16[168,128]{1,0:T(8,128)(2,1)S(1)}, u32[]{:S(2)}, u32[]{:S(2)}) collective-permute-start(bf16[168,128]{1,0:T(8,128)(2,1)S(1)} %add.21), channel_id=1, source_target_pairs={{0,17},{1,16},{2,19},{3,18},{4,21},{5,20},{6,23},{7,22},{8,25},{9,... | collective-permute-start | bytes 129032 | tf_op jit(solution)/shard_map/ppermute | solution.py:578
  18.3 4.0 %collective-permute-start.5 = (bf16[168,128]{1,0:T(8,128)(2,1)S(1)}, bf16[168,128]{1,0:T(8,128)(2,1)S(1)}, u32[]{:S(2)}, u32[]{:S(2)}) collective-permute-start(bf16[168,128]{1,0:T(8,128)(2,1)S(1)} %add.21), channel_id=1, source_target_pairs={{0,16},{1,17},{2,18},{3,19},{4,20},{5,21},{6,22},{7,23},{8,24},{9,... | collective-permute-start | bytes 129032 | tf_op jit(solution)/shard_map/ppermute | solution.py:578
  19.3 4.0 %collective-permute-start.7 = (bf16[168,128]{1,0:T(8,128)(2,1)S(1)}, bf16[168,128]{1,0:T(8,128)(2,1)S(1)}, u32[]{:S(2)}, u32[]{:S(2)}) collective-permute-start(bf16[168,128]{1,0:T(8,128)(2,1)S(1)} %add.21), channel_id=1, source_target_pairs={{0,1},{1,0},{2,3},{3,2},{4,5},{5,4},{6,7},{7,6},{8,9},{9,8},{10,11... | collective-permute-start | bytes 129032 | tf_op jit(solution)/shard_map/ppermute | solution.py:578
  23.4 7.2 %collective-permute-start.9 = (bf16[168,128]{1,0:T(8,128)(2,1)S(1)}, bf16[168,128]{1,0:T(8,128)(2,1)S(1)}, u32[]{:S(2)}, u32[]{:S(2)}) collective-permute-start(bf16[168,128]{1,0:T(8,128)(2,1)S(1)} %add_add_fusion.1), channel_id=1, source_target_pairs={{0,6},{1,7},{2,4},{3,5},{4,2},{5,3},{6,0},{7,1},{8,14},{9,15},{10,... | collective-permute-start | bytes 129032 | tf_op jit(solution)/shard_map/ppermute | solution.py:578
  26.7 4.0 %collective-permute-start.8 = (bf16[168,128]{1,0:T(8,128)(2,1)S(1)}, bf16[168,128]{1,0:T(8,128)(2,1)S(1)}, u32[]{:S(2)}, u32[]{:S(2)}) collective-permute-start(bf16[168,128]{1,0:T(8,128)(2,1)S(1)} %add_add_fusion.1), channel_id=1, source_target_pairs={{0,2},{1,3},{2,0},{3,1},{4,6},{5,7},{6,4},{7,5},{8,10},{9,11},{10,... | collective-permute-start | bytes 129032 | tf_op jit(solution)/shard_map/ppermute | solution.py:578
  26.8 4.9 %collective-permute-start.10 = (bf16[168,128]{1,0:T(8,128)(2,1)S(1)}, bf16[168,128]{1,0:T(8,128)(2,1)S(1)}, u32[]{:S(2)}, u32[]{:S(2)}) collective-permute-start(bf16[168,128]{1,0:T(8,128)(2,1)S(1)} %add_add_fusion.1), channel_id=1, source_target_pairs={{0,4},{1,5},{2,6},{3,7},{4,0},{5,1},{6,2},{7,3},{8,12},{9,13},{10,... | collective-permute-start | bytes 129032 | tf_op jit(solution)/shard_map/ppermute | solution.py:578
  31.7 1.3 %collective-permute-start.11 = (f32[168,128]{1,0:T(8,128)S(1)}, f32[168,128]{1,0:T(8,128)S(1)}, u32[]{:S(2)}, u32[]{:S(2)}) collective-permute-start(f32[168,128]{1,0:T(8,128)S(1)} %add_add_fusion.refs_0_), channel_id=1, source_target_pairs={{0,8},{1,9},{2,10},{3,11},{4,12},{5,13},{6,14},{7,15},{8,0},{9,1},... | collective-permute-start | bytes 258056 | tf_op jit(solution)/shard_map/ppermute | solution.py:578
